TPU v7x, 256 devices: a whole 4x4x8 slice. The times are simulated.
256 devices in a mesh: rows: 64 (over x, z, core), cols: 4 (over y).
Axes of the slice: x: 4, y: 4, z: 8, core: 2. Of those that a mesh axis runs over, the one named last changes fastest.
Arguments:
- panel: float32 [32768, 1024], P('rows'), as said below
- window_block: float32 [32768, 2048], P('rows', 'cols'), may hold values from -6 to 6
- row_live: int32 [64], replicated, may hold values 0 or 1
- window_rows: int32 [4], replicated, may hold values from 2 to 63, as said below
Outputs:
- factor: float32 [32768, 1024], P('rows')
- updated: float32 [32768, 2048], P('rows', 'cols')
Inputs may be any that keep to these rules, and one draw needn't show every extreme that they name: `window_rows`: distinct tile rows, none inside the supernode. `row_live`: the value for tile rows below 2 is ignored: those rows are always present. `panel`: the first 1024 rows hold a symmetric positive definite block.
All inputs are finite; a program needn't handle non-finite values.
Results may differ from a plain program's by a relative error of at most 0.0001.
Values sent between devices are 32-bit elements; how exact they have to be, the bound alone decides.
No kernel may reach another device: no remote copies, remote signals or barrier semaphores. Data moves between devices by JAX's collectives and lax.ppermute only.
A program may use at most 128 MiB of HBM per device.

v0:
```python
import functools

import jax
import jax.numpy as jnp
from jax import lax
from jax.experimental import pallas as pl
from jax.experimental.pallas import tpu as pltpu
from jax.sharding import PartitionSpec as P

F32 = jnp.float32
B = 512
NB = 128
NX, NZ, NY = 4, 8, 4
VMEM_LIMIT = 56 << 20
CONTRACT = (((1,), (1,)), ((), ()))


def lanes(v, j):
    return jnp.broadcast_to(v[:, j : j + 1], (8, NB))


def sublanes(v, s):
    return jnp.broadcast_to(v[s : s + 1, :], (8, NB))


def factor_block(V):
    sub = lax.broadcasted_iota(jnp.int32, (8, NB), 0)
    lane = lax.broadcasted_iota(jnp.int32, (8, NB), 1)
    groups = NB // 8
    E = [jnp.where(lane == sub + 8 * k, 1.0, 0.0).astype(F32) for k in range(groups)]
    upper, inverse = [], []
    for k in range(groups):
        R = [sublanes(V[k], a) for a in range(8)]
        Q = [sublanes(E[k], a) for a in range(8)]
        s = {(a, b): lanes(R[a], 8 * k + b) for a in range(8) for b in range(a + 1)}
        C = {kk: [lanes(V[kk], 8 * k + b) for b in range(8)] for kk in range(k + 1, groups)}
        for b in range(8):
            inv = lax.rsqrt(s[b, b])
            l = {a: s[a, b] * inv for a in range(b + 1, 8)}
            for a in range(b + 1, 8):
                for c in range(b + 1, a + 1):
                    s[a, c] = s[a, c] - l[a] * l[c]
            R[b] = R[b] * inv
            Q[b] = Q[b] * inv
            for a in range(b + 1, 8):
                R[a] = R[a] - l[a] * R[b]
                Q[a] = Q[a] - l[a] * Q[b]
            for kk in C:
                C[kk][b] = C[kk][b] * inv
                for a in range(b + 1, 8):
                    C[kk][a] = C[kk][a] - C[kk][b] * l[a]
        for kk in C:
            for b in range(8):
                V[kk] = V[kk] - C[kk][b] * R[b]
                E[kk] = E[kk] - C[kk][b] * Q[b]
        u, x = R[0], Q[0]
        for a in range(1, 8):
            u = jnp.where(sub == a, R[a], u)
            x = jnp.where(sub == a, Q[a], x)
        upper.append(jnp.where(lane >= sub + 8 * k, u, 0.0))
        inverse.append(x)
    return upper, inverse


def halves(a):
    hi = a.astype(jnp.bfloat16)
    return hi, (a - hi.astype(F32)).astype(jnp.bfloat16)


def mul_t(a, b):
    ah, al = halves(a)
    bh, bl = halves(b)
    d = functools.partial(lax.dot_general, dimension_numbers=CONTRACT, preferred_element_type=F32)
    return d(ah, bh) + (d(ah, bl) + d(al, bh))


def mirrored(d):
    r = lax.broadcasted_iota(jnp.int32, (NB, NB), 0)
    c = lax.broadcasted_iota(jnp.int32, (NB, NB), 1)
    return jnp.where(r >= c, d, d.T)


def tall_factor(a_ref, f_ref, dinv_ref, d_ref):
    m, n = a_ref.shape
    nb = n // NB
    for k in range(nb):
        o = k * NB
        a_ref[o : o + NB, o : o + NB] = mirrored(a_ref[o : o + NB, o : o + NB])
    d_ref[...] = a_ref[0:NB, 0:NB]

    def body(k, carry):
        V = [d_ref[8 * i : 8 * i + 8, :] for i in range(NB // 8)]
        upper, inverse = factor_block(V)
        low = jnp.concatenate(upper, 0).T
        X = jnp.concatenate(inverse, 0)
        dinv_ref[k] = X

        def branch(kk):
            def run():
                o = NB * kk
                e = o + NB
                f_ref[o:e, o:e] = low
                Lp = mul_t(a_ref[e:, o:e], X)
                f_ref[e:, o:e] = Lp
                if e < n:
                    f_ref[o:e, e:] = jnp.zeros((NB, n - e), F32)
                    T = a_ref[e:, e:] - mul_t(Lp, Lp[: n - e])
                    a_ref[e:, e:] = T
                    d_ref[...] = T[:NB, :NB]
                return 0

            return run

        return lax.switch(k, [branch(kk) for kk in range(nb)]) + carry

    lax.fori_loop(0, nb, body, 0)


def place(meta, own_ref, other_ref, m_ref):
    y, mine = meta[3], meta[2]
    rows = own_ref.shape[1]
    for dy in range(NY):
        row = pl.multiple_of(lax.rem(y - dy + NY, NY) * rows, 8)
        m_ref[mine, pl.ds(row, rows), :] = own_ref[dy]
        m_ref[1 - mine, pl.ds(row, rows), :] = other_ref[dy]


H = B // 2


def kernel_a(meta, own_ref, other_ref, panel_ref, f_ref, dinv_ref, m_ref, a_ref, d_ref):
    place(meta, own_ref, other_ref, m_ref)
    a_ref[:H, :H] = m_ref[0, :H, :]
    a_ref[:H, H:] = jnp.zeros((H, H), F32)
    a_ref[H:B, :H] = m_ref[0, H : 2 * H, :]
    a_ref[H:B, H:] = m_ref[0, 2 * H : 3 * H, :]
    for i in range(2):
        for j in range(2):
            o = (2 * i + j) * H
            a_ref[B + i * H : B + (i + 1) * H, j * H : (j + 1) * H] = m_ref[1, o : o + H, :]
    a_ref[2 * B :, :] = panel_ref[...] * meta[5].astype(F32)
    tall_factor(a_ref, f_ref, dinv_ref, d_ref)


def kernel_b(meta, own_ref, other_ref, panel_ref, f0_ref, f1_ref, dinv_ref, factor_ref, m_ref, a_ref, d_ref):
    place(meta, own_ref, other_ref, m_ref)
    a_ref[:H, :H] = m_ref[1, 4 * H :, :]
    a_ref[:H, H:] = jnp.zeros((H, H), F32)
    a_ref[H:B, :H] = m_ref[0, 3 * H : 4 * H, :]
    a_ref[H:B, H:] = m_ref[0, 4 * H :, :]
    a_ref[B:, :] = panel_ref[...] * meta[5].astype(F32)
    low = f0_ref[B : 2 * B, :]
    a_ref[...] = a_ref[...] - mul_t(f0_ref[B:, :], low)
    tall_factor(a_ref, f1_ref, dinv_ref, d_ref)
    row = meta[4]

    @pl.when(row == 0)
    def _():
        factor_ref[:, :B] = f0_ref[:B, :]
        factor_ref[:, B:] = jnp.zeros((B, B), F32)

    @pl.when(row == 1)
    def _():
        factor_ref[:, :B] = f0_ref[B : 2 * B, :]
        factor_ref[:, B:] = f1_ref[:B, :]

    @pl.when(row > 1)
    def _():
        factor_ref[:, :B] = f0_ref[2 * B :, :]
        factor_ref[:, B:] = f1_ref[B:, :]


def kernel_c(meta, own_ref, other_ref, f0_ref, f1_ref, d0_ref, d1_ref, factor_ref, window_ref, out_ref, s_ref):
    mine = meta[2]
    live = meta[6].astype(F32)
    for j in range(NX * NZ):
        s_ref[pl.ds(pl.multiple_of((2 * j + mine) * 8, 8), 8), :] = own_ref[j] * live
        s_ref[pl.ds(pl.multiple_of((2 * j + 1 - mine) * 8, 8), 8), :] = other_ref[j] * live
    for k in range(4):
        o, e = k * NB, k * NB + NB
        X = mul_t(s_ref[:, o:e], d0_ref[k])
        s_ref[:, o:e] = X
        s_ref[:, e:] = s_ref[:, e:] - mul_t(X, f0_ref[e : 2 * B, o:e])
    for k in range(4):
        o, e = k * NB, k * NB + NB
        X = mul_t(s_ref[:, B + o : B + e], d1_ref[k])
        s_ref[:, B + o : B + e] = X
        if e < B:
            s_ref[:, B + e :] = s_ref[:, B + e :] - mul_t(X, f1_ref[e:B, o:e])
    out_ref[...] = window_ref[...] - mul_t(factor_ref[...], s_ref[...])


SMEM = pl.BlockSpec(memory_space=pltpu.SMEM)
VM = pl.BlockSpec(memory_space=pltpu.VMEM)


def call(kernel, flops, outs, scratch, *args):
    return pl.pallas_call(
        kernel,
        out_shape=[jax.ShapeDtypeStruct(s, F32) for s in outs],
        in_specs=[SMEM] + [VM] * (len(args) - 1),
        out_specs=[VM] * len(outs),
        scratch_shapes=[pltpu.VMEM(s, F32) for s in scratch],
        compiler_params=pltpu.CompilerParams(vmem_limit_bytes=VMEM_LIMIT),
        cost_estimate=pl.CostEstimate(flops=flops, transcendentals=0, bytes_accessed=8 << 20),
    )(*args)


def rid(x, z, c):
    return (x * NZ + z) * 2 + c


def move(v, keep, to):
    pairs = [
        (rid(x, z, c), rid(*to(x, z, c)))
        for x in range(NX)
        for z in range(NZ)
        for c in range(2)
        if keep(x, z, c)
    ]
    return lax.ppermute(v, "rows", pairs)


def always(x, z, c):
    return True


def by_x(v, d, keep=always):
    return move(v, keep, lambda x, z, c: ((x + d) % NX, z, c))


def by_z(v, d, keep=always):
    return move(v, keep, lambda x, z, c: (x, (z + d) % NZ, c))


def swap_core(v):
    return move(v, always, lambda x, z, c: (x, z, 1 - c))


GROUPS = [[rid(x, z, c) for x in range(NX) for z in range(NZ)] for c in range(2)]


def spread_static(v, x, z, y):
    piece = lax.dynamic_slice_in_dim(v, y * (v.shape[0] // NY), v.shape[0] // NY, 0)
    piece = jnp.where((x == 0) & (z == 0), piece, 0.0)
    piece = piece + sum(by_x(piece, d, lambda x, z, c: x == 0 and z == 0) for d in range(1, NX))
    piece = piece + sum(by_z(piece, d, lambda x, z, c: z == 0) for d in (2, 4, 6))
    piece = piece + by_z(piece, 1, lambda x, z, c: z % 2 == 0)
    own = jnp.stack([piece] + [lax.ppermute(piece, "cols", [(i, (i + d) % NY) for i in range(NY)]) for d in range(1, NY)])
    return own, swap_core(own)


def after(value, *others):
    return lax.optimization_barrier((value,) + others)[0]


def shards(panel, window_block, row_live, window_rows):
    row = lax.axis_index("rows")
    y = lax.axis_index("cols")
    x, z, core = row // (2 * NZ), (row // 2) % NZ, row % 2
    target = window_rows[y]
    live = jnp.where(row < 2, 1, row_live[row])
    meta = jnp.stack([x, z, core, y, row, live, row_live[target], 0]).astype(jnp.int32)

    width = 2 * B // NY
    mine = lax.dynamic_slice_in_dim(panel, y * width, width, 1).reshape(64, 8, width)
    parts = lax.all_to_all(mine, "rows", 0, 0)

    low = lax.ppermute(panel[H:, B:], "rows", [(1, 0)])
    first = jnp.concatenate([panel[:H, :H], panel[H:, :H], panel[H:, H:B], low[:, :H], low[:, H:]])
    second = jnp.concatenate([panel[:H, :H], panel[:H, H:B], panel[H:, :H], panel[H:, H:B], panel[:H, B : B + H]])
    own, other = spread_static(jnp.where(core == 0, first, second), x, z, y)

    chosen = jnp.stack([lax.dynamic_index_in_dim(parts, window_rows[c], 0, keepdims=False) for c in range(NY)])
    quarters = lax.all_to_all(chosen, "cols", 0, 0)
    shard = jnp.concatenate([quarters[q] for q in range(NY)], axis=1)
    t_own = lax.all_to_all(jnp.broadcast_to(shard, (32,) + shard.shape), "rows", 0, 0, axis_index_groups=GROUPS)

    meta_a = after(meta, shard)
    f0, d0 = call(
        kernel_a, 10**10, [(3 * B, B), (4, NB, NB)], [(2, 5 * H, H), (3 * B, B), (NB, NB)], meta_a, own, other, panel[:, :B]
    )
    t_other = swap_core(after(t_own, f0))
    f1, d1, factor = call(
        kernel_b,
        10**10,
        [(2 * B, B), (4, NB, NB), (B, 2 * B)],
        [(2, 5 * H, H), (2 * B, B), (NB, NB)],
        meta, own, other, panel[:, B:], f0,
    )
    (updated,) = call(
        kernel_c, 10**9, [(B, B)], [(B, 2 * B)], meta, t_own, t_other, f0, f1, d0, d1, factor, window_block
    )
    return factor, updated


def solution(mesh):
    in_specs = (P("rows", None), P("rows", "cols"), P(), P())
    out_specs = (P("rows", None), P("rows", "cols"))
    return jax.shard_map(shards, mesh=mesh, in_specs=in_specs, out_specs=out_specs, check_vma=False)
```

profile of v0, /device:TPU:1, one launch (start us, length us, event | category | flops | bytes accessed | tf_op | source)
XLA Modules:
  0.0 174.5 jit_solution(17411441949697821506)
XLA Ops:
  0.6 1.2 slice.62
  1.9 5.2 %collective-permute-start = (f32[256,512]{1,0:T(8,128)S(1)}, f32[256,512]{1,0:T(8,128)S(1)}, u32[]{:S(2)}, u32[]{:S(2)}) collective-permute-start(f32[256,512]{1,0:T(8,128)S(1)} %slice.62), channel_id=1, source_target_pairs={{4,0},{5,1},{6,2},{7,3}} | collective-permute-start | bytes 1572872 | tf_op jit(solution)/shard_map/ppermute | solution.py:269
  7.1 1.7 slice_dynamic-update-slice_fusion.3
  8.7 1.7 slice_dynamic-update-slice_fusion.2
  10.4 1.7 slice_dynamic-update-slice_fusion.1
  14.5 1.3 fusion.4
  15.8 1.3 collective-permute-start.3
  17.1 1.3 collective-permute-start.1
  18.4 1.3 collective-permute-start.2
  19.7 4.3 %collective-permute-done.3 = f32[320,256]{1,0:T(8,128)S(1)} collective-permute-done((f32[320,256]{1,0:T(8,128)S(1)}, f32[320,256]{1,0:T(8,128)S(1)}, u32[]{:S(2)}, u32[]{:S(2)}) %collective-permute-start.3) | collective-permute-done | bytes 327712 | tf_op jit(solution)/shard_map/ppermute | solution.py:221
  24.1 1.3 collective-permute-done.1
  25.4 7.0 %collective-permute-done.2 = f32[320,256]{1,0:T(8,128)S(1)} collective-permute-done((f32[320,256]{1,0:T(8,128)S(1)}, f32[320,256]{1,0:T(8,128)S(1)}, u32[]{:S(2)}, u32[]{:S(2)}) %collective-permute-start.2) | collective-permute-done | bytes 327712 | tf_op jit(solution)/shard_map/ppermute | solution.py:221
  32.5 1.3 collective-permute-start.6
  33.8 2.0 %collective-permute-start.4 = (f32[320,256]{1,0:T(8,128)S(1)}, f32[320,256]{1,0:T(8,128)}, u32[]{:S(2)}, u32[]{:S(2)}) collective-permute-start(f32[320,256]{1,0:T(8,128)S(1)} %add_add_fusion.1), channel_id=1, source_target_pairs={{0,16},{4,20},{64,80},{68,84},{128,144},{132,148},{192,208},{196,2... | collective-permute-start | bytes 983048 | tf_op jit(solution)/shard_map/ppermute | solution.py:221
  35.9 2.0 %collective-permute-start.5 = (f32[320,256]{1,0:T(8,128)S(1)}, f32[320,256]{1,0:T(8,128)}, u32[]{:S(2)}, u32[]{:S(2)}) collective-permute-start(f32[320,256]{1,0:T(8,128)S(1)} %add_add_fusion.1), channel_id=1, source_target_pairs={{0,32},{4,36},{64,96},{68,100},{128,160},{132,164},{192,224},{196,... | collective-permute-start | bytes 983048 | tf_op jit(solution)/shard_map/ppermute | solution.py:221
  37.9 6.7 %all-to-all-start = ((f32[64,8,256]{2,1,0:T(8,128)}), f32[64,8,256]{2,1,0:T(8,128)S(1)}, u32[]{:S(2)}, u32[]{:S(2)}) async-start(f32[64,8,256]{2,1,0:T(8,128)} %get-tuple-element.18), calls=%async_computation | async-start | bytes 1048576 | tf_op jit(solution)/shard_map/all_to_all | solution.py:267
  45.3 4.5 %collective-permute-done.5 = f32[320,256]{1,0:T(8,128)} collective-permute-done((f32[320,256]{1,0:T(8,128)S(1)}, f32[320,256]{1,0:T(8,128)}, u32[]{:S(2)}, u32[]{:S(2)}) %collective-permute-start.5) | collective-permute-done | bytes 327712 | tf_op jit(solution)/shard_map/ppermute | solution.py:221
  49.9 1.3 add_add_fusion
  51.1 2.0 %collective-permute-start.7 = (f32[320,256]{1,0:T(8,128)S(1)}, f32[320,256]{1,0:T(8,128)}, u32[]{:S(2)}, u32[]{:S(2)}) collective-permute-start(f32[320,256]{1,0:T(8,128)S(1)} %add_add_fusion), channel_id=1, source_target_pairs={{0,8},{4,12},{16,24},{20,28},{32,40},{36,44},{48,56},{52,60},{64,7... | collective-permute-start | bytes 983048 | tf_op jit(solution)/shard_map/ppermute | solution.py:221
  53.2 13.7 %collective-permute-done.7 = f32[320,256]{1,0:T(8,128)} collective-permute-done((f32[320,256]{1,0:T(8,128)S(1)}, f32[320,256]{1,0:T(8,128)}, u32[]{:S(2)}, u32[]{:S(2)}) %collective-permute-start.7) | collective-permute-done | bytes 327712 | tf_op jit(solution)/shard_map/ppermute | solution.py:221
  66.9 1.0 add.70
  78.7 4.4 %all-to-all-start.1 = ((f32[4,8,256]{2,1,0:T(8,128)}), f32[4,8,256]{2,1,0:T(8,128)S(1)}, u32[]{:S(2)}, u32[]{:S(2)}) async-start(f32[4,8,256]{2,1,0:T(8,128)} %pad_maximum_fusion.1), calls=%async_computation.1 | async-start | bytes 65536 | tf_op jit(solution)/shard_map/all_to_all | solution.py:275
  83.1 3.9 %collective-permute-done.8 = f32[320,256]{1,0:T(8,128)} collective-permute-done((f32[320,256]{1,0:T(8,128)S(1)}, f32[320,256]{1,0:T(8,128)}, u32[]{:S(2)}, u32[]{:S(2)}) %collective-permute-start.8) | collective-permute-done | bytes 327712 | tf_op jit(solution)/shard_map/ppermute | solution.py:249
  87.0 2.2 %pad_maximum_fusion.own_ref = f32[4,320,256]{2,1,0:T(8,128)} fusion(f32[1,320,256]{2,1,0:T(8,128)S(1)} %bitcast.27, f32[1,320,256]{2,1,0:T(8,128)} %bitcast.10, f32[1,320,256]{2,1,0:T(8,128)} %bitcast.9, f32[1,320,256]{2,1,0:T(8,128)S(1)} %bitcast.26), kind=kLoop, calls=%fused_computation.4 | loop fusion | flops 983040 | bytes 2621440 | tf_op jit(solution)/shard_map/stack | solution.py:249
  89.8 1.1 broadcast_in_dim.8
  90.9 11.3 %all-to-all-start.2 = ((f32[32,8,1024]{2,1,0:T(8,128)}), f32[32,8,1024]{2,1,0:T(8,128)S(1)}, u32[]{:S(2)}, u32[]{:S(2)}) async-start(f32[32,8,1024]{2,1,0:T(8,128)} %broadcast_in_dim.8), calls=%async_computation.2 | async-start | bytes 2097152 | tf_op jit(solution)/shard_map/all_to_all | solution.py:277
  105.2 1.3 stack.49.meta
  106.5 1.5 fusion.5
  108.0 24.9 %shard_map.59 = (f32[1536,512]{1,0:T(8,128)}, f32[4,128,128]{2,1,0:T(8,128)}) custom-call(s32[8]{0:T(128)} %stack.49.meta, f32[4,320,256]{2,1,0:T(8,128)} %pad_maximum_fusion.own_ref, f32[4,320,256]{2,1,0:T(8,128)} %collective-permute-done.11.other_ref, f32[512,512]{1,0:T(8,128)} %get-tuple-element.16.panel_ref), custom_call_target="tpu_custom_call" | custom-call | flops 10000000000 | bytes 8388608 | tf_op jit(solution)/shard_map/pallas_call | solution.py:198
  133.5 26.7 %shard_map.60 = (f32[1024,512]{1,0:T(8,128)}, f32[4,128,128]{2,1,0:T(8,128)}, f32[512,1024]{1,0:T(8,128)}) custom-call(s32[8]{0:T(128)} %stack.49.meta, f32[4,320,256]{2,1,0:T(8,128)} %pad_maximum_fusion.own_ref, f32[4,320,256]{2,1,0:T(8,128)} %collective-permute-done.11.other_ref, f32[512,512]{1,0:T(8,128)} %get-tuple-element.17.panel_ref, ...), custom_call_target="tpu_custom_call" | custom-call | flops 10000000000 | bytes 8388608 | tf_op jit(solution)/shard_map/pallas_call | solution.py:198
  160.3 1.0 copy-done.2
  161.3 13.3 %shard_map.61 = f32[512,512]{1,0:T(8,128)} custom-call(s32[8]{0:T(128)} %stack.49.meta, f32[32,8,1024]{2,1,0:T(8,128)} %copy-done.1, f32[32,8,1024]{2,1,0:T(8,128)} %copy-done.2, f32[1536,512]{1,0:T(8,128)} %get-tuple-element.10.f0_ref, f32[1024,512]{1,0:T(8,128)} %get-tuple-element.13.f1_ref, f32[4,128,128]{2,1,0:T(8,128)} %get-tuple-element.14.d0_ref, ...), custom_call_target="tpu_custom_call" | custom-call | flops 1000000000 | bytes 8388608 | tf_op jit(solution)/shard_map/pallas_call | solution.py:198
  (37 shorter events, 8.1 us)
Async XLA Ops:
  0.6 11.4 %copy-start = (f32[512,1024]{1,0:T(8,128)S(1)}, f32[512,1024]{1,0:T(8,128)}, u32[]{:S(2)}) copy-start(f32[512,1024]{1,0:T(8,128)} %param.4) | copy-start | bytes 6291460
  1.9 12.6 %collective-permute-start = (f32[256,512]{1,0:T(8,128)S(1)}, f32[256,512]{1,0:T(8,128)S(1)}, u32[]{:S(2)}, u32[]{:S(2)}) collective-permute-start(f32[256,512]{1,0:T(8,128)S(1)} %slice.62), channel_id=1, source_target_pairs={{4,0},{5,1},{6,2},{7,3}} | collective-permute-start | bytes 1572872 | tf_op jit(solution)/shard_map/ppermute | solution.py:269
  15.8 8.3 %collective-permute-start.3 = (f32[320,256]{1,0:T(8,128)S(1)}, f32[320,256]{1,0:T(8,128)S(1)}, u32[]{:S(2)}, u32[]{:S(2)}) collective-permute-start(f32[320,256]{1,0:T(8,128)S(1)} %fusion.4), channel_id=1, source_target_pairs={{0,192},{4,196},{1,193},{5,197},{2,194},{6,198},{3,195},{7,199}} | collective-permute-start | bytes 983048 | tf_op jit(solution)/shard_map/ppermute | solution.py:221
  17.1 8.3 %collective-permute-start.1 = (f32[320,256]{1,0:T(8,128)S(1)}, f32[320,256]{1,0:T(8,128)S(1)}, u32[]{:S(2)}, u32[]{:S(2)}) collective-permute-start(f32[320,256]{1,0:T(8,128)S(1)} %fusion.4), channel_id=1, source_target_pairs={{0,64},{4,68},{1,65},{5,69},{2,66},{6,70},{3,67},{7,71}} | collective-permute-start | bytes 983048 | tf_op jit(solution)/shard_map/ppermute | solution.py:221
  18.4 14.0 %collective-permute-start.2 = (f32[320,256]{1,0:T(8,128)S(1)}, f32[320,256]{1,0:T(8,128)S(1)}, u32[]{:S(2)}, u32[]{:S(2)}) collective-permute-start(f32[320,256]{1,0:T(8,128)S(1)} %fusion.4), channel_id=1, source_target_pairs={{0,128},{4,132},{1,129},{5,133},{2,130},{6,134},{3,131},{7,135}} | collective-permute-start | bytes 983048 | tf_op jit(solution)/shard_map/ppermute | solution.py:221
  32.5 12.1 %collective-permute-start.6 = (f32[320,256]{1,0:T(8,128)S(1)}, f32[320,256]{1,0:T(8,128)S(1)}, u32[]{:S(2)}, u32[]{:S(2)}) collective-permute-start(f32[320,256]{1,0:T(8,128)S(1)} %add_add_fusion.1), channel_id=1, source_target_pairs={{0,48},{4,52},{64,112},{68,116},{128,176},{132,180},{192,240},{196... | collective-permute-start | bytes 983048 | tf_op jit(solution)/shard_map/ppermute | solution.py:221
  33.8 10.8 %collective-permute-start.4 = (f32[320,256]{1,0:T(8,128)S(1)}, f32[320,256]{1,0:T(8,128)}, u32[]{:S(2)}, u32[]{:S(2)}) collective-permute-start(f32[320,256]{1,0:T(8,128)S(1)} %add_add_fusion.1), channel_id=1, source_target_pairs={{0,16},{4,20},{64,80},{68,84},{128,144},{132,148},{192,208},{196,2... | collective-permute-start | bytes 983048 | tf_op jit(solution)/shard_map/ppermute | solution.py:221
  35.9 14.0 %collective-permute-start.5 = (f32[320,256]{1,0:T(8,128)S(1)}, f32[320,256]{1,0:T(8,128)}, u32[]{:S(2)}, u32[]{:S(2)}) collective-permute-start(f32[320,256]{1,0:T(8,128)S(1)} %add_add_fusion.1), channel_id=1, source_target_pairs={{0,32},{4,36},{64,96},{68,100},{128,160},{132,164},{192,224},{196,... | collective-permute-start | bytes 983048 | tf_op jit(solution)/shard_map/ppermute | solution.py:221
  37.9 40.2 %all-to-all-start = ((f32[64,8,256]{2,1,0:T(8,128)}), f32[64,8,256]{2,1,0:T(8,128)S(1)}, u32[]{:S(2)}, u32[]{:S(2)}) async-start(f32[64,8,256]{2,1,0:T(8,128)} %get-tuple-element.18), calls=%async_computation | async-start | bytes 1048576 | tf_op jit(solution)/shard_map/all_to_all | solution.py:267
  44.6 25.2 %copy-start.4 = (s32[4]{0:T(128)S(1)}, s32[4]{0:T(128)}, u32[]{:S(2)}) copy-start(s32[4]{0:T(128)} %param.7) | copy-start | bytes 52
  44.6 0.7 copy-start.3
  51.1 15.7 %collective-permute-start.7 = (f32[320,256]{1,0:T(8,128)S(1)}, f32[320,256]{1,0:T(8,128)}, u32[]{:S(2)}, u32[]{:S(2)}) collective-permute-start(f32[320,256]{1,0:T(8,128)S(1)} %add_add_fusion), channel_id=1, source_target_pairs={{0,8},{4,12},{16,24},{20,28},{32,40},{36,44},{48,56},{52,60},{64,7... | collective-permute-start | bytes 983048 | tf_op jit(solution)/shard_map/ppermute | solution.py:221
  67.9 15.3 %collective-permute-start.10 = (f32[320,256]{1,0:T(8,128)S(1)}, f32[320,256]{1,0:T(8,128)S(1)}, u32[]{:S(2)}, u32[]{:S(2)}) collective-permute-start(f32[320,256]{1,0:T(8,128)S(1)} %add.70), channel_id=1, source_target_pairs={{0,3},{1,0},{2,1},{3,2},{4,7},{5,4},{6,5},{7,6},{8,11},{9,8},{10,9... | collective-permute-start | bytes 983048 | tf_op jit(solution)/shard_map/ppermute | solution.py:249
  68.8 14.4 %collective-permute-start.9 = (f32[320,256]{1,0:T(8,128)S(1)}, f32[320,256]{1,0:T(8,128)}, u32[]{:S(2)}, u32[]{:S(2)}) collective-permute-start(f32[320,256]{1,0:T(8,128)S(1)} %add.70), channel_id=1, source_target_pairs={{0,2},{1,3},{2,0},{3,1},{4,6},{5,7},{6,4},{7,5},{8,10},{9,11},{10,... | collective-permute-start | bytes 983048 | tf_op jit(solution)/shard_map/ppermute | solution.py:249
  69.1 17.9 %collective-permute-start.8 = (f32[320,256]{1,0:T(8,128)S(1)}, f32[320,256]{1,0:T(8,128)}, u32[]{:S(2)}, u32[]{:S(2)}) collective-permute-start(f32[320,256]{1,0:T(8,128)S(1)} %add.70), channel_id=1, source_target_pairs={{0,1},{1,2},{2,3},{3,0},{4,5},{5,6},{6,7},{7,4},{8,9},{9,10},{10,1... | collective-permute-start | bytes 983048 | tf_op jit(solution)/shard_map/ppermute | solution.py:249
  78.7 11.1 %all-to-all-start.1 = ((f32[4,8,256]{2,1,0:T(8,128)}), f32[4,8,256]{2,1,0:T(8,128)S(1)}, u32[]{:S(2)}, u32[]{:S(2)}) async-start(f32[4,8,256]{2,1,0:T(8,128)} %pad_maximum_fusion.1), calls=%async_computation.1 | async-start | bytes 65536 | tf_op jit(solution)/shard_map/all_to_all | solution.py:275
  89.3 18.8 %collective-permute-start.11 = (f32[4,320,256]{2,1,0:T(8,128)}, f32[4,320,256]{2,1,0:T(8,128)}, u32[]{:S(2)}, u32[]{:S(2)}) collective-permute-start(f32[4,320,256]{2,1,0:T(8,128)} %pad_maximum_fusion.own_ref), channel_id=1, source_target_pairs={{0,4},{4,0},{8,12},{12,8},{16,20},{20,16},{24,28},{28,24},{32,36},... | collective-permute-start | bytes 3932168 | tf_op jit(solution)/shard_map/ppermute | solution.py:221
  90.9 13.2 %copy-start.5 = (s32[64]{0:T(128)S(1)}, s32[64]{0:T(128)}, u32[]{:S(2)}) copy-start(s32[64]{0:T(128)} %param.6) | copy-start | bytes 772
  90.9 42.1 %all-to-all-start.2 = ((f32[32,8,1024]{2,1,0:T(8,128)}), f32[32,8,1024]{2,1,0:T(8,128)S(1)}, u32[]{:S(2)}, u32[]{:S(2)}) async-start(f32[32,8,1024]{2,1,0:T(8,128)} %broadcast_in_dim.8), calls=%async_computation.2 | async-start | bytes 2097152 | tf_op jit(solution)/shard_map/all_to_all | solution.py:277
  133.0 27.3 %copy-start.1 = (f32[32,8,1024]{2,1,0:T(8,128)}, f32[32,8,1024]{2,1,0:T(8,128)S(1)}, u32[]{:S(2)}) copy-start(f32[32,8,1024]{2,1,0:T(8,128)S(1)} %all-to-all-done.2.own_ref) | copy-start | bytes 3145732
  133.0 27.3 %collective-permute-start.12 = (f32[32,8,1024]{2,1,0:T(8,128)S(1)}, f32[32,8,1024]{2,1,0:T(8,128)S(1)}, u32[]{:S(2)}, u32[]{:S(2)}) collective-permute-start(f32[32,8,1024]{2,1,0:T(8,128)S(1)} %all-to-all-done.2.own_ref), channel_id=1, source_target_pairs={{0,4},{4,0},{8,12},{12,8},{16,20},{20,16},{24,28},{28,24},{32,36},... | collective-permute-start | bytes 3145736 | tf_op jit(solution)/shard_map/ppermute | solution.py:221
  160.3 1.0 copy-start.2
where the time goes:
time: 175 us
  Pallas kernels  64.9 us (37%)
  starting transfers between devices  41.9 us (24%)
  waiting for transfers between devices  34.8 us (20%)
  local copies, waits for them, and re-layouts  15.5 us (9%)
  between operations  10.8 us (6%)
  other arithmetic  6.5 us (4%)
    pallas_call x3, Pallas kernels, call(): pl.pallas_call(kernel, out_shape=[jax.ShapeDtypeStruct(s, F32) for s in o...  64.9 us
    ppermute x9, waiting for transfers between devices, move(): return lax.ppermute(v, 'rows', pairs)  30.9 us
    ppermute x9, starting transfers between devices, move(): return lax.ppermute(v, 'rows', pairs)  12.4 us
    all_to_all x1, starting transfers between devices, shards(): lax.all_to_all(jnp.broadcast_to(shard, (32,) + shard.shape), 'rows', 0, 0...  11.3 us
    unnamed x16, local copies, waits for them, and re-layouts  7.45 us
    all_to_all x1, starting transfers between devices, shards(): parts = lax.all_to_all(mine, 'rows', 0, 0)  6.73 us
    ppermute x1, starting transfers between devices, shards(): low = lax.ppermute(panel[H:, B:], 'rows', [(1, 0)])  5.18 us
    all_to_all x1, starting transfers between devices, shards(): quarters = lax.all_to_all(chosen, 'cols', 0, 0)  4.44 us
  transfers between devices with their start and end apart: 16, of which 6 were waited for; matrix products, arithmetic and copies ran while one was open for 10% of the time, Pallas kernels for 30%

commit v1 on v0

--- a/solution.py
+++ b/solution.py
@@ -117,12 +117,14 @@
 
 
 def place(meta, own_ref, other_ref, m_ref):
-    y, mine = meta[3], meta[2]
-    rows = own_ref.shape[1]
+    x, y, mine = meta[0], meta[3], meta[2]
     for dy in range(NY):
-        row = pl.multiple_of(lax.rem(y - dy + NY, NY) * rows, 8)
-        m_ref[mine, pl.ds(row, rows), :] = own_ref[dy]
-        m_ref[1 - mine, pl.ds(row, rows), :] = other_ref[dy]
+        for dx in range(NX):
+            row = lax.rem(y - dy + NY, NY) * 64 + lax.rem(x - dx + NX, NX) * 16
+            for b in range(5):
+                at = pl.ds(pl.multiple_of(row + b * H, 16), 16)
+                m_ref[mine, at, :] = own_ref[dy, dx, b * 16 : (b + 1) * 16]
+                m_ref[1 - mine, at, :] = other_ref[dy, dx, b * 16 : (b + 1) * 16]
 
 
 H = B // 2
@@ -240,14 +242,17 @@
 GROUPS = [[rid(x, z, c) for x in range(NX) for z in range(NZ)] for c in range(2)]
 
 
-def spread_static(v, x, z, y):
-    piece = lax.dynamic_slice_in_dim(v, y * (v.shape[0] // NY), v.shape[0] // NY, 0)
-    piece = jnp.where((x == 0) & (z == 0), piece, 0.0)
-    piece = piece + sum(by_x(piece, d, lambda x, z, c: x == 0 and z == 0) for d in range(1, NX))
+def spread_static(v, x, z):
+    root = (x == 0) & (z == 0)
+    piece = jnp.where(root, v[0], 0.0)
+    piece = piece + sum(by_x(v[d], d, lambda x, z, c: x == 0 and z == 0) for d in range(1, NX))
     piece = piece + sum(by_z(piece, d, lambda x, z, c: z == 0) for d in (2, 4, 6))
     piece = piece + by_z(piece, 1, lambda x, z, c: z % 2 == 0)
-    own = jnp.stack([piece] + [lax.ppermute(piece, "cols", [(i, (i + d) % NY) for i in range(NY)]) for d in range(1, NY)])
-    return own, swap_core(own)
+    return jnp.stack([piece] + [by_x(piece, d) for d in range(1, NX)])
+
+
+def gather_y(v):
+    return jnp.stack([v] + [lax.ppermute(v, "cols", [(i, (i + d) % NY) for i in range(NY)]) for d in range(1, NY)])
 
 
 def after(value, *others):
@@ -266,11 +271,19 @@
     mine = lax.dynamic_slice_in_dim(panel, y * width, width, 1).reshape(64, 8, width)
     parts = lax.all_to_all(mine, "rows", 0, 0)
 
-    low = lax.ppermute(panel[H:, B:], "rows", [(1, 0)])
-    first = jnp.concatenate([panel[:H, :H], panel[H:, :H], panel[H:, H:B], low[:, :H], low[:, H:]])
-    second = jnp.concatenate([panel[:H, :H], panel[:H, H:B], panel[H:, :H], panel[H:, H:B], panel[:H, B : B + H]])
-    own, other = spread_static(jnp.where(core == 0, first, second), x, z, y)
-
+    def rows_of(i):
+        return lax.dynamic_slice_in_dim(panel, i * H + y * 64, 64, 0).reshape(NX, 16, 2 * B)
+
+    top, bot = rows_of(0), rows_of(1)
+    low = lax.ppermute(bot[:, :, B:], "rows", [(1, 0)])
+    first = [top[:, :, :H], bot[:, :, :H], bot[:, :, H:B], low[:, :, :H], low[:, :, H:]]
+    second = [top[:, :, :H], top[:, :, H:B], bot[:, :, :H], bot[:, :, H:B], top[:, :, B : B + H]]
+    stack = jnp.concatenate([jnp.where(core == 0, f, s) for f, s in zip(first, second)], axis=1)
+    part = spread_static(stack, x, z)
+    own = gather_y(part)
+    other = swap_core(own)
+
+    parts = after(parts, part)
     chosen = jnp.stack([lax.dynamic_index_in_dim(parts, window_rows[c], 0, keepdims=False) for c in range(NY)])
     quarters = lax.all_to_all(chosen, "cols", 0, 0)
     shard = jnp.concatenate([quarters[q] for q in range(NY)], axis=1)

time: 175 us -> 157 us (0.90)
  waiting for transfers between devices: 34.8 us -> 17 us
  starting transfers between devices: 41.9 us -> 52 us
  local copies, waits for them, and re-layouts: 15.5 us -> 9.12 us
  other arithmetic: 6.5 us -> 1.94 us
    ppermute x9 -> x12, waiting for transfers between devices: 30.9 us -> 11.9 us  [move(): return lax.ppermute(v, 'rows', pairs)]
    ppermute x9 -> x12, starting transfers between devices: 12.4 us -> 22.2 us  [move(): return lax.ppermute(v, 'rows', pairs)]
    unnamed x16 -> x11, local copies, waits for them, and re-layouts: 7.45 us -> 1.02 us
    all_to_all x1, starting transfers between devices: 11.3 us -> 9.02 us  [shards(): lax.all_to_all(jnp.broadcast_to(shard, (32,) + shard.shape), 'rows', 0, 0...]
    ppermute x4, starting transfers between devices: 7.12 us -> 9 us  [the longest x1 5.15 us: shards(): low = lax.ppermute(bot[:, :, B:], 'rows', [(1, 0)])]
    all_to_all x1, starting transfers between devices: 6.73 us -> 8.5 us  [shards(): parts = lax.all_to_all(mine, 'rows', 0, 0)]
  transfers between devices with their start and end apart: 16 -> 19, of which waited for: 6 -> 8; matrix products, arithmetic and copies ran while one was open for 10% -> 6% of each run, Pallas kernels for 30% -> 33%
where the time goes in v1:
time: 157 us; the launch traced here: 156 us
  Pallas kernels  64.9 us (41%)
  starting transfers between devices  52 us (33%)
  waiting for transfers between devices  17 us (11%)
  between operations  10.9 us (7%)
  local copies, waits for them, and re-layouts  9.12 us (6%)
  other arithmetic  1.94 us (1%)
    pallas_call x3, Pallas kernels, call(): pl.pallas_call(kernel, out_shape=[jax.ShapeDtypeStruct(s, F32) for s in o...  64.9 us
    ppermute x12, starting transfers between devices, move(): return lax.ppermute(v, 'rows', pairs)  22.2 us
    ppermute x12, waiting for transfers between devices, move(): return lax.ppermute(v, 'rows', pairs)  11.9 us
    all_to_all x1, starting transfers between devices, shards(): lax.all_to_all(jnp.broadcast_to(shard, (32,) + shard.shape), 'rows', 0, 0...  9.02 us
    all_to_all x1, starting transfers between devices, shards(): parts = lax.all_to_all(mine, 'rows', 0, 0)  8.5 us
    ppermute x1, starting transfers between devices, shards(): low = lax.ppermute(bot[:, :, B:], 'rows', [(1, 0)])  5.15 us
    ppermute x3, waiting for transfers between devices, gather_y(): lax.ppermute(v, 'cols', [(i, (i + d) % NY) for i in range(NY)])  5.09 us
    ppermute x3, starting transfers between devices, gather_y(): lax.ppermute(v, 'cols', [(i, (i + d) % NY) for i in range(NY)])  3.85 us
  transfers between devices with their start and end apart: 19, of which 8 were waited for; matrix products, arithmetic and copies ran while one was open for 6% of the time, Pallas kernels for 33%

profile of v1, /device:TPU:1, one launch (start us, length us, event | category | flops | bytes accessed | tf_op | source)
XLA Modules:
  0.0 156.0 jit_solution(13631444936241080999)
XLA Ops:
  0.6 1.1 constant_dynamic-slice_fusion.4
  1.7 5.2 %collective-permute-start = (f32[4,16,512]{2,1,0:T(8,128)S(1)}, f32[4,16,512]{2,1,0:T(8,128)S(1)}, u32[]{:S(2)}, u32[]{:S(2)}) collective-permute-start(f32[4,16,512]{2,1,0:T(8,128)S(1)} %slice.95), channel_id=1, source_target_pairs={{4,0},{5,1},{6,2},{7,3}} | collective-permute-start | bytes 393224 | tf_op jit(solution)/shard_map/ppermute | solution.py:278
  6.9 1.9 %dynamic-slice_bitcast_fusion = f32[64,8,256]{2,1,0:T(8,128)} fusion(f32[512,1024]{1,0:T(8,128)} %param.4, s32[]{:T(128)S(6)} %select_n.104), kind=kLoop, calls=%fused_computation.1 | loop fusion | bytes 1048580 | tf_op jit(solution)/shard_map/reshape | solution.py:271
  8.8 8.5 %all-to-all-start = ((f32[64,8,256]{2,1,0:T(8,128)}), f32[64,8,256]{2,1,0:T(8,128)S(1)}, u32[]{:S(2)}, u32[]{:S(2)}) async-start(f32[64,8,256]{2,1,0:T(8,128)} %dynamic-slice_bitcast_fusion), calls=%async_computation | async-start | bytes 1048576 | tf_op jit(solution)/shard_map/all_to_all | solution.py:272
  17.4 4.7 %collective-permute-start.3 = (f32[80,256]{1,0:T(8,128)S(1)}, f32[80,256]{1,0:T(8,128)S(1)}, u32[]{:S(2)}, u32[]{:S(2)}) collective-permute-start(f32[80,256]{1,0:T(8,128)S(1)} %get-tuple-element.29), channel_id=1, source_target_pairs={{0,192},{4,196},{1,193},{5,197},{2,194},{6,198},{3,195},{7,199}} | collective-permute-start | bytes 245768 | tf_op jit(solution)/shard_map/ppermute | solution.py:223
  22.2 1.3 collective-permute-start.1
  23.5 1.3 collective-permute-start.2
  24.8 1.0 collective-permute-done.1
  25.8 3.4 %collective-permute-done.2 = f32[80,256]{1,0:T(8,128)S(1)} collective-permute-done((f32[80,256]{1,0:T(8,128)S(1)}, f32[80,256]{1,0:T(8,128)S(1)}, u32[]{:S(2)}, u32[]{:S(2)}) %collective-permute-start.2) | collective-permute-done | bytes 81952 | tf_op jit(solution)/shard_map/ppermute | solution.py:223
  29.3 1.3 collective-permute-start.6
  30.6 1.3 collective-permute-start.4
  31.9 1.3 collective-permute-start.5
  33.3 1.7 %collective-permute-done.5 = f32[80,256]{1,0:T(8,128)S(1)} collective-permute-done((f32[80,256]{1,0:T(8,128)S(1)}, f32[80,256]{1,0:T(8,128)S(1)}, u32[]{:S(2)}, u32[]{:S(2)}) %collective-permute-start.5) | collective-permute-done | bytes 81952 | tf_op jit(solution)/shard_map/ppermute | solution.py:223
  35.1 1.3 collective-permute-start.7
  36.4 1.5 collective-permute-done.7
  38.4 4.3 %collective-permute-start.9 = (f32[80,256]{1,0:T(8,128)S(1)}, f32[80,256]{1,0:T(8,128)S(1)}, u32[]{:S(2)}, u32[]{:S(2)}) collective-permute-start(f32[80,256]{1,0:T(8,128)S(1)} %add.80), channel_id=1, source_target_pairs={{0,128},{4,132},{8,136},{12,140},{16,144},{20,148},{24,152},{28,15... | collective-permute-start | bytes 245768 | tf_op jit(solution)/shard_map/ppermute | solution.py:223
  42.7 0.8 collective-permute-start.8
  43.5 1.1 collective-permute-done.9
  44.5 3.1 %collective-permute-done.8 = f32[80,256]{1,0:T(8,128)S(1)} collective-permute-done((f32[80,256]{1,0:T(8,128)S(1)}, f32[80,256]{1,0:T(8,128)S(1)}, u32[]{:S(2)}, u32[]{:S(2)}) %collective-permute-start.8) | collective-permute-done | bytes 81952 | tf_op jit(solution)/shard_map/ppermute | solution.py:223
  47.7 2.8 %collective-permute-start.13 = (f32[4,80,256]{2,1,0:T(8,128)S(1)}, f32[4,80,256]{2,1,0:T(8,128)S(1)}, u32[]{:S(2)}, u32[]{:S(2)}) collective-permute-start(f32[4,80,256]{2,1,0:T(8,128)S(1)} %get-tuple-element.27), channel_id=1, source_target_pairs={{0,3},{1,0},{2,1},{3,2},{4,7},{5,4},{6,5},{7,6},{8,11},{9,8},{10,9... | collective-permute-start | bytes 983048 | tf_op jit(solution)/shard_map/ppermute | solution.py:255
  60.2 3.3 %all-to-all-start.1 = ((f32[4,8,256]{2,1,0:T(8,128)}), f32[4,8,256]{2,1,0:T(8,128)S(1)}, u32[]{:S(2)}, u32[]{:S(2)}) async-start(f32[4,8,256]{2,1,0:T(8,128)} %pad_maximum_fusion.2), calls=%async_computation.1 | async-start | bytes 65536 | tf_op jit(solution)/shard_map/all_to_all | solution.py:288
  63.5 5.1 %collective-permute-done.11 = f32[4,80,256]{2,1,0:T(8,128)S(1)} collective-permute-done((f32[4,80,256]{2,1,0:T(8,128)S(1)}, f32[4,80,256]{2,1,0:T(8,128)S(1)}, u32[]{:S(2)}, u32[]{:S(2)}) %collective-permute-start.11) | collective-permute-done | bytes 327712 | tf_op jit(solution)/shard_map/ppermute | solution.py:255
  68.6 1.2 pad_maximum_fusion.own_ref
  70.5 1.1 broadcast_in_dim.8
  71.6 9.0 %all-to-all-start.2 = ((f32[32,8,1024]{2,1,0:T(8,128)}), f32[32,8,1024]{2,1,0:T(8,128)S(1)}, u32[]{:S(2)}, u32[]{:S(2)}) async-start(f32[32,8,1024]{2,1,0:T(8,128)} %broadcast_in_dim.8), calls=%async_computation.2 | async-start | bytes 2097152 | tf_op jit(solution)/shard_map/all_to_all | solution.py:290
  83.8 1.3 stack.64.meta
  85.1 1.5 fusion.6
  86.6 24.9 %shard_map.59 = (f32[1536,512]{1,0:T(8,128)}, f32[4,128,128]{2,1,0:T(8,128)}) custom-call(s32[8]{0:T(128)} %stack.64.meta, f32[4,4,80,256]{3,2,1,0:T(8,128)} %pad_maximum_fusion.own_ref, f32[4,4,80,256]{3,2,1,0:T(8,128)} %collective-permute-done.14.other_ref, f32[512,512]{1,0:T(8,128)} %get-tuple-element.18.panel_ref), custom_call_target="tpu_custom_call" | custom-call | flops 10000000000 | bytes 8388608 | tf_op jit(solution)/shard_map/pallas_call | solution.py:200
  111.6 3.4 %collective-permute-start.15 = (f32[32,8,1024]{2,1,0:T(8,128)S(1)}, f32[32,8,1024]{2,1,0:T(8,128)S(1)}, u32[]{:S(2)}, u32[]{:S(2)}) collective-permute-start(f32[32,8,1024]{2,1,0:T(8,128)S(1)} %all-to-all-done.2.own_ref), channel_id=1, source_target_pairs={{0,4},{4,0},{8,12},{12,8},{16,20},{20,16},{24,28},{28,24},{32,36},... | collective-permute-start | bytes 3145736 | tf_op jit(solution)/shard_map/ppermute | solution.py:223
  115.0 26.7 %shard_map.60 = (f32[1024,512]{1,0:T(8,128)}, f32[4,128,128]{2,1,0:T(8,128)}, f32[512,1024]{1,0:T(8,128)}) custom-call(s32[8]{0:T(128)} %stack.64.meta, f32[4,4,80,256]{3,2,1,0:T(8,128)} %pad_maximum_fusion.own_ref, f32[4,4,80,256]{3,2,1,0:T(8,128)} %collective-permute-done.14.other_ref, f32[512,512]{1,0:T(8,128)} %get-tuple-element.19.panel_ref, ...), custom_call_target="tpu_custom_call" | custom-call | flops 10000000000 | bytes 8388608 | tf_op jit(solution)/shard_map/pallas_call | solution.py:200
  141.7 1.0 copy-done.2
  142.7 13.3 %shard_map.61 = f32[512,512]{1,0:T(8,128)} custom-call(s32[8]{0:T(128)} %stack.64.meta, f32[32,8,1024]{2,1,0:T(8,128)} %copy-done.1, f32[32,8,1024]{2,1,0:T(8,128)} %copy-done.2, f32[1536,512]{1,0:T(8,128)} %get-tuple-element.12.f0_ref, f32[1024,512]{1,0:T(8,128)} %get-tuple-element.15.f1_ref, f32[4,128,128]{2,1,0:T(8,128)} %get-tuple-element.16.d0_ref, ...), custom_call_target="tpu_custom_call" | custom-call | flops 1000000000 | bytes 8388608 | tf_op jit(solution)/shard_map/pallas_call | solution.py:200
  (42 shorter events, 4.6 us)
Async XLA Ops:
  1.7 15.6 %collective-permute-start = (f32[4,16,512]{2,1,0:T(8,128)S(1)}, f32[4,16,512]{2,1,0:T(8,128)S(1)}, u32[]{:S(2)}, u32[]{:S(2)}) collective-permute-start(f32[4,16,512]{2,1,0:T(8,128)S(1)} %slice.95), channel_id=1, source_target_pairs={{4,0},{5,1},{6,2},{7,3}} | collective-permute-start | bytes 393224 | tf_op jit(solution)/shard_map/ppermute | solution.py:278
  8.8 50.8 %all-to-all-start = ((f32[64,8,256]{2,1,0:T(8,128)}), f32[64,8,256]{2,1,0:T(8,128)S(1)}, u32[]{:S(2)}, u32[]{:S(2)}) async-start(f32[64,8,256]{2,1,0:T(8,128)} %dynamic-slice_bitcast_fusion), calls=%async_computation | async-start | bytes 1048576 | tf_op jit(solution)/shard_map/all_to_all | solution.py:272
  17.4 34.2 %copy-start.3 = (s32[4]{0:T(128)S(1)}, s32[4]{0:T(128)}, u32[]{:S(2)}) copy-start(s32[4]{0:T(128)} %param.7) | copy-start | bytes 52
  17.4 7.4 %collective-permute-start.3 = (f32[80,256]{1,0:T(8,128)S(1)}, f32[80,256]{1,0:T(8,128)S(1)}, u32[]{:S(2)}, u32[]{:S(2)}) collective-permute-start(f32[80,256]{1,0:T(8,128)S(1)} %get-tuple-element.29), channel_id=1, source_target_pairs={{0,192},{4,196},{1,193},{5,197},{2,194},{6,198},{3,195},{7,199}} | collective-permute-start | bytes 245768 | tf_op jit(solution)/shard_map/ppermute | solution.py:223
  22.2 3.7 %collective-permute-start.1 = (f32[80,256]{1,0:T(8,128)S(1)}, f32[80,256]{1,0:T(8,128)S(1)}, u32[]{:S(2)}, u32[]{:S(2)}) collective-permute-start(f32[80,256]{1,0:T(8,128)S(1)} %get-tuple-element.30), channel_id=1, source_target_pairs={{0,64},{4,68},{1,65},{5,69},{2,66},{6,70},{3,67},{7,71}} | collective-permute-start | bytes 245768 | tf_op jit(solution)/shard_map/ppermute | solution.py:223
  23.5 5.8 %collective-permute-start.2 = (f32[80,256]{1,0:T(8,128)S(1)}, f32[80,256]{1,0:T(8,128)S(1)}, u32[]{:S(2)}, u32[]{:S(2)}) collective-permute-start(f32[80,256]{1,0:T(8,128)S(1)} %get-tuple-element.28), channel_id=1, source_target_pairs={{0,128},{4,132},{1,129},{5,133},{2,130},{6,134},{3,131},{7,135}} | collective-permute-start | bytes 245768 | tf_op jit(solution)/shard_map/ppermute | solution.py:223
  29.3 3.9 %collective-permute-start.6 = (f32[80,256]{1,0:T(8,128)S(1)}, f32[80,256]{1,0:T(8,128)S(1)}, u32[]{:S(2)}, u32[]{:S(2)}) collective-permute-start(f32[80,256]{1,0:T(8,128)S(1)} %fusion.1), channel_id=1, source_target_pairs={{0,48},{4,52},{64,112},{68,116},{128,176},{132,180},{192,240},{196... | collective-permute-start | bytes 245768 | tf_op jit(solution)/shard_map/ppermute | solution.py:223
  30.6 2.8 %collective-permute-start.4 = (f32[80,256]{1,0:T(8,128)S(1)}, f32[80,256]{1,0:T(8,128)S(1)}, u32[]{:S(2)}, u32[]{:S(2)}) collective-permute-start(f32[80,256]{1,0:T(8,128)S(1)} %fusion.1), channel_id=1, source_target_pairs={{0,16},{4,20},{64,80},{68,84},{128,144},{132,148},{192,208},{196,2... | collective-permute-start | bytes 245768 | tf_op jit(solution)/shard_map/ppermute | solution.py:223
  31.9 3.2 %collective-permute-start.5 = (f32[80,256]{1,0:T(8,128)S(1)}, f32[80,256]{1,0:T(8,128)S(1)}, u32[]{:S(2)}, u32[]{:S(2)}) collective-permute-start(f32[80,256]{1,0:T(8,128)S(1)} %fusion.1), channel_id=1, source_target_pairs={{0,32},{4,36},{64,96},{68,100},{128,160},{132,164},{192,224},{196,... | collective-permute-start | bytes 245768 | tf_op jit(solution)/shard_map/ppermute | solution.py:223
  35.1 2.8 %collective-permute-start.7 = (f32[80,256]{1,0:T(8,128)S(1)}, f32[80,256]{1,0:T(8,128)S(1)}, u32[]{:S(2)}, u32[]{:S(2)}) collective-permute-start(f32[80,256]{1,0:T(8,128)S(1)} %add_add_fusion), channel_id=1, source_target_pairs={{0,8},{4,12},{16,24},{20,28},{32,40},{36,44},{48,56},{52,60},{64,7... | collective-permute-start | bytes 245768 | tf_op jit(solution)/shard_map/ppermute | solution.py:223
  37.8 5.6 %collective-permute-start.10 = (f32[80,256]{1,0:T(8,128)S(1)}, f32[80,256]{1,0:T(8,128)S(1)}, u32[]{:S(2)}, u32[]{:S(2)}) collective-permute-start(f32[80,256]{1,0:T(8,128)S(1)} %add.80), channel_id=1, source_target_pairs={{0,192},{4,196},{8,200},{12,204},{16,208},{20,212},{24,216},{28,22... | collective-permute-start | bytes 245768 | tf_op jit(solution)/shard_map/ppermute | solution.py:223
  38.4 6.1 %collective-permute-start.9 = (f32[80,256]{1,0:T(8,128)S(1)}, f32[80,256]{1,0:T(8,128)S(1)}, u32[]{:S(2)}, u32[]{:S(2)}) collective-permute-start(f32[80,256]{1,0:T(8,128)S(1)} %add.80), channel_id=1, source_target_pairs={{0,128},{4,132},{8,136},{12,140},{16,144},{20,148},{24,152},{28,15... | collective-permute-start | bytes 245768 | tf_op jit(solution)/shard_map/ppermute | solution.py:223
  42.7 5.0 %collective-permute-start.8 = (f32[80,256]{1,0:T(8,128)S(1)}, f32[80,256]{1,0:T(8,128)S(1)}, u32[]{:S(2)}, u32[]{:S(2)}) collective-permute-start(f32[80,256]{1,0:T(8,128)S(1)} %add.80), channel_id=1, source_target_pairs={{0,64},{4,68},{8,72},{12,76},{16,80},{20,84},{24,88},{28,92},{32,9... | collective-permute-start | bytes 245768 | tf_op jit(solution)/shard_map/ppermute | solution.py:223
  47.7 15.8 %collective-permute-start.13 = (f32[4,80,256]{2,1,0:T(8,128)S(1)}, f32[4,80,256]{2,1,0:T(8,128)S(1)}, u32[]{:S(2)}, u32[]{:S(2)}) collective-permute-start(f32[4,80,256]{2,1,0:T(8,128)S(1)} %get-tuple-element.27), channel_id=1, source_target_pairs={{0,3},{1,0},{2,1},{3,2},{4,7},{5,4},{6,5},{7,6},{8,11},{9,8},{10,9... | collective-permute-start | bytes 983048 | tf_op jit(solution)/shard_map/ppermute | solution.py:255
  50.5 13.0 %collective-permute-start.12 = (f32[4,80,256]{2,1,0:T(8,128)S(1)}, f32[4,80,256]{2,1,0:T(8,128)S(1)}, u32[]{:S(2)}, u32[]{:S(2)}) collective-permute-start(f32[4,80,256]{2,1,0:T(8,128)S(1)} %get-tuple-element.27), channel_id=1, source_target_pairs={{0,2},{1,3},{2,0},{3,1},{4,6},{5,7},{6,4},{7,5},{8,10},{9,11},{10,... | collective-permute-start | bytes 983048 | tf_op jit(solution)/shard_map/ppermute | solution.py:255
  50.9 17.8 %collective-permute-start.11 = (f32[4,80,256]{2,1,0:T(8,128)S(1)}, f32[4,80,256]{2,1,0:T(8,128)S(1)}, u32[]{:S(2)}, u32[]{:S(2)}) collective-permute-start(f32[4,80,256]{2,1,0:T(8,128)S(1)} %get-tuple-element.27), channel_id=1, source_target_pairs={{0,1},{1,2},{2,3},{3,0},{4,5},{5,6},{6,7},{7,4},{8,9},{9,10},{10,1... | collective-permute-start | bytes 983048 | tf_op jit(solution)/shard_map/ppermute | solution.py:255
  60.2 10.3 %all-to-all-start.1 = ((f32[4,8,256]{2,1,0:T(8,128)}), f32[4,8,256]{2,1,0:T(8,128)S(1)}, u32[]{:S(2)}, u32[]{:S(2)}) async-start(f32[4,8,256]{2,1,0:T(8,128)} %pad_maximum_fusion.2), calls=%async_computation.1 | async-start | bytes 65536 | tf_op jit(solution)/shard_map/all_to_all | solution.py:288
  69.8 16.8 %collective-permute-start.14 = (f32[4,4,80,256]{3,2,1,0:T(8,128)}, f32[4,4,80,256]{3,2,1,0:T(8,128)}, u32[]{:S(2)}, u32[]{:S(2)}) collective-permute-start(f32[4,4,80,256]{3,2,1,0:T(8,128)} %pad_maximum_fusion.own_ref), channel_id=1, source_target_pairs={{0,4},{4,0},{8,12},{12,8},{16,20},{20,16},{24,28},{28,24},{32,36},... | collective-permute-start | bytes 3932168 | tf_op jit(solution)/shard_map/ppermute | solution.py:223
  71.6 10.9 %copy-start.4 = (s32[64]{0:T(128)S(1)}, s32[64]{0:T(128)}, u32[]{:S(2)}) copy-start(s32[64]{0:T(128)} %param.6) | copy-start | bytes 772
  71.6 13.5 %copy-start = (f32[512,1024]{1,0:T(8,128)S(1)}, f32[512,1024]{1,0:T(8,128)}, u32[]{:S(2)}) copy-start(f32[512,1024]{1,0:T(8,128)} %param.4) | copy-start | bytes 6291460
  71.6 39.9 %all-to-all-start.2 = ((f32[32,8,1024]{2,1,0:T(8,128)}), f32[32,8,1024]{2,1,0:T(8,128)S(1)}, u32[]{:S(2)}, u32[]{:S(2)}) async-start(f32[32,8,1024]{2,1,0:T(8,128)} %broadcast_in_dim.8), calls=%async_computation.2 | async-start | bytes 2097152 | tf_op jit(solution)/shard_map/all_to_all | solution.py:290
  111.6 30.1 %copy-start.1 = (f32[32,8,1024]{2,1,0:T(8,128)}, f32[32,8,1024]{2,1,0:T(8,128)S(1)}, u32[]{:S(2)}) copy-start(f32[32,8,1024]{2,1,0:T(8,128)S(1)} %all-to-all-done.2.own_ref) | copy-start | bytes 3145732
  111.6 30.1 %collective-permute-start.15 = (f32[32,8,1024]{2,1,0:T(8,128)S(1)}, f32[32,8,1024]{2,1,0:T(8,128)S(1)}, u32[]{:S(2)}, u32[]{:S(2)}) collective-permute-start(f32[32,8,1024]{2,1,0:T(8,128)S(1)} %all-to-all-done.2.own_ref), channel_id=1, source_target_pairs={{0,4},{4,0},{8,12},{12,8},{16,20},{20,16},{24,28},{28,24},{32,36},... | collective-permute-start | bytes 3145736 | tf_op jit(solution)/shard_map/ppermute | solution.py:223
  141.7 1.0 copy-start.2

commit v2 on v1

--- a/solution.py
+++ b/solution.py
@@ -10,6 +10,7 @@
 F32 = jnp.float32
 B = 512
 NB = 128
+H = B // 2
 NX, NZ, NY = 4, 8, 4
 VMEM_LIMIT = 56 << 20
 CONTRACT = (((1,), (1,)), ((), ()))
@@ -24,33 +25,44 @@
 
 
 def factor_block(V):
+    V = list(V)
     sub = lax.broadcasted_iota(jnp.int32, (8, NB), 0)
     lane = lax.broadcasted_iota(jnp.int32, (8, NB), 1)
     groups = NB // 8
     E = [jnp.where(lane == sub + 8 * k, 1.0, 0.0).astype(F32) for k in range(groups)]
     upper, inverse = [], []
+    block = [lanes(V[0], b) for b in range(8)]
     for k in range(groups):
+        near = list(range(k + 1, min(groups, k + 3)))
+        far = list(range(k + 3, groups))
         R = [sublanes(V[k], a) for a in range(8)]
         Q = [sublanes(E[k], a) for a in range(8)]
-        s = {(a, b): lanes(R[a], 8 * k + b) for a in range(8) for b in range(a + 1)}
-        C = {kk: [lanes(V[kk], 8 * k + b) for b in range(8)] for kk in range(k + 1, groups)}
+        C = {kk: [lanes(V[kk], 8 * k + b) for b in range(8)] for kk in near}
+        ahead = [lanes(V[k + 1], 8 * (k + 1) + b) for b in range(8)] if near else None
+        D = {kk: [lanes(V[kk], 8 * k + b) for b in range(8)] for kk in far}
+        l, invs = {}, []
         for b in range(8):
-            inv = lax.rsqrt(s[b, b])
-            l = {a: s[a, b] * inv for a in range(b + 1, 8)}
+            inv = lax.rsqrt(sublanes(block[b], b))
+            invs.append(inv)
+            col = block[b] * inv
             for a in range(b + 1, 8):
-                for c in range(b + 1, a + 1):
-                    s[a, c] = s[a, c] - l[a] * l[c]
+                l[a, b] = sublanes(col, a)
+            for c in range(b + 1, 8):
+                block[c] = block[c] - col * l[c, b]
+            for kk in near:
+                C[kk][b] = C[kk][b] * inv
+                for a in range(b + 1, 8):
+                    C[kk][a] = C[kk][a] - C[kk][b] * l[a, b]
+            if near:
+                x = C[k + 1][b]
+                for c in range(8):
+                    ahead[c] = ahead[c] - x * sublanes(x, c)
             R[b] = R[b] * inv
             Q[b] = Q[b] * inv
             for a in range(b + 1, 8):
-                R[a] = R[a] - l[a] * R[b]
-                Q[a] = Q[a] - l[a] * Q[b]
-            for kk in C:
-                C[kk][b] = C[kk][b] * inv
-                for a in range(b + 1, 8):
-                    C[kk][a] = C[kk][a] - C[kk][b] * l[a]
-        for kk in C:
-            for b in range(8):
+                R[a] = R[a] - l[a, b] * R[b]
+                Q[a] = Q[a] - l[a, b] * Q[b]
+            for kk in near:
                 V[kk] = V[kk] - C[kk][b] * R[b]
                 E[kk] = E[kk] - C[kk][b] * Q[b]
         u, x = R[0], Q[0]
@@ -59,6 +71,19 @@
             x = jnp.where(sub == a, Q[a], x)
         upper.append(jnp.where(lane >= sub + 8 * k, u, 0.0))
         inverse.append(x)
+        if far:
+            W, Y = list(R), list(Q)
+            for b in reversed(range(8)):
+                W[b] = W[b] * invs[b]
+                Y[b] = Y[b] * invs[b]
+                for a in range(b):
+                    W[a] = W[a] - l[b, a] * W[b]
+                    Y[a] = Y[a] - l[b, a] * Y[b]
+            for kk in far:
+                for b in range(8):
+                    V[kk] = V[kk] - D[kk][b] * W[b]
+                    E[kk] = E[kk] - D[kk][b] * Y[b]
+        block = ahead
     return upper, inverse
 
 
@@ -100,8 +125,9 @@
                 o = NB * kk
                 e = o + NB
                 f_ref[o:e, o:e] = low
-                Lp = mul_t(a_ref[e:, o:e], X)
-                f_ref[e:, o:e] = Lp
+                if e < m:
+                    Lp = mul_t(a_ref[e:, o:e], X)
+                    f_ref[e:, o:e] = Lp
                 if e < n:
                     f_ref[o:e, e:] = jnp.zeros((NB, n - e), F32)
                     T = a_ref[e:, e:] - mul_t(Lp, Lp[: n - e])
@@ -116,8 +142,13 @@
     lax.fori_loop(0, nb, body, 0)
 
 
-def place(meta, own_ref, other_ref, m_ref):
-    x, y, mine = meta[0], meta[3], meta[2]
+def coords():
+    row = lax.axis_index("rows")
+    return row // (2 * NZ), lax.axis_index("cols"), lax.rem(row, 2)
+
+
+def place(own_ref, other_ref, m_ref):
+    x, y, mine = coords()
     for dy in range(NY):
         for dx in range(NX):
             row = lax.rem(y - dy + NY, NY) * 64 + lax.rem(x - dx + NX, NX) * 16
@@ -127,11 +158,8 @@
                 m_ref[1 - mine, at, :] = other_ref[dy, dx, b * 16 : (b + 1) * 16]
 
 
-H = B // 2
-
-
-def kernel_a(meta, own_ref, other_ref, panel_ref, f_ref, dinv_ref, m_ref, a_ref, d_ref):
-    place(meta, own_ref, other_ref, m_ref)
+def kernel_a(own_ref, other_ref, f_ref, dinv_ref, m_ref, a_ref, d_ref):
+    place(own_ref, other_ref, m_ref)
     a_ref[:H, :H] = m_ref[0, :H, :]
     a_ref[:H, H:] = jnp.zeros((H, H), F32)
     a_ref[H:B, :H] = m_ref[0, H : 2 * H, :]
@@ -140,56 +168,62 @@
         for j in range(2):
             o = (2 * i + j) * H
             a_ref[B + i * H : B + (i + 1) * H, j * H : (j + 1) * H] = m_ref[1, o : o + H, :]
-    a_ref[2 * B :, :] = panel_ref[...] * meta[5].astype(F32)
     tall_factor(a_ref, f_ref, dinv_ref, d_ref)
 
 
-def kernel_b(meta, own_ref, other_ref, panel_ref, f0_ref, f1_ref, dinv_ref, factor_ref, m_ref, a_ref, d_ref):
-    place(meta, own_ref, other_ref, m_ref)
+def kernel_b(own_ref, other_ref, f0_ref, f1_ref, dinv_ref, m_ref, a_ref, d_ref):
+    place(own_ref, other_ref, m_ref)
     a_ref[:H, :H] = m_ref[1, 4 * H :, :]
     a_ref[:H, H:] = jnp.zeros((H, H), F32)
-    a_ref[H:B, :H] = m_ref[0, 3 * H : 4 * H, :]
-    a_ref[H:B, H:] = m_ref[0, 4 * H :, :]
-    a_ref[B:, :] = panel_ref[...] * meta[5].astype(F32)
-    low = f0_ref[B : 2 * B, :]
-    a_ref[...] = a_ref[...] - mul_t(f0_ref[B:, :], low)
+    a_ref[H:, :H] = m_ref[0, 3 * H : 4 * H, :]
+    a_ref[H:, H:] = m_ref[0, 4 * H :, :]
+    low = f0_ref[B:, :]
+    a_ref[...] = a_ref[...] - mul_t(low, low)
     tall_factor(a_ref, f1_ref, dinv_ref, d_ref)
-    row = meta[4]
+
+
+def pair_inverse(d_ref, j, low):
+    x0, x1 = d_ref[j], d_ref[j + 1]
+    corner = -mul_t(mul_t(x1, low.T), x0.T)
+    top = jnp.concatenate([x0, jnp.zeros((NB, NB), F32)], axis=1)
+    return jnp.concatenate([top, jnp.concatenate([corner, x1], axis=1)], axis=0)
+
+
+def kernel_c(live_ref, rows_ref, own_ref, other_ref, f0_ref, f1_ref, d0_ref, d1_ref, panel_ref, window_ref, factor_ref, out_ref, s_ref):
+    row = lax.axis_index("rows")
+    _, y, mine = coords()
+    live_t = live_ref[rows_ref[y]].astype(F32)
+    live = jnp.where(row < 2, 1, live_ref[row]).astype(F32)
+    s_ref[:B, :] = panel_ref[...] * live
+    for j in range(NX * NZ):
+        s_ref[pl.ds(pl.multiple_of(B + (2 * j + mine) * 8, 8), 8), :] = own_ref[j] * live_t
+        s_ref[pl.ds(pl.multiple_of(B + (2 * j + 1 - mine) * 8, 8), 8), :] = other_ref[j] * live_t
+    for k in range(4):
+        o, e = k * H, (k + 1) * H
+        f_ref, d_ref, base = (f0_ref, d0_ref, 0) if k < 2 else (f1_ref, d1_ref, B)
+        p = o - base
+        inv = pair_inverse(d_ref, 2 * (k % 2), f_ref[p + NB : p + H, p : p + NB])
+        X = mul_t(s_ref[:, o:e], inv)
+        s_ref[:, o:e] = X
+        if k < 3:
+            s_ref[:, e:] = s_ref[:, e:] - mul_t(X, f_ref[p + H :, p : p + H])
 
     @pl.when(row == 0)
     def _():
-        factor_ref[:, :B] = f0_ref[:B, :]
-        factor_ref[:, B:] = jnp.zeros((B, B), F32)
+        s_ref[:B, :B] = f0_ref[:B, :]
+        s_ref[:B, B:] = jnp.zeros((B, B), F32)
 
     @pl.when(row == 1)
     def _():
-        factor_ref[:, :B] = f0_ref[B : 2 * B, :]
-        factor_ref[:, B:] = f1_ref[:B, :]
-
-    @pl.when(row > 1)
-    def _():
-        factor_ref[:, :B] = f0_ref[2 * B :, :]
-        factor_ref[:, B:] = f1_ref[B:, :]
-
-
-def kernel_c(meta, own_ref, other_ref, f0_ref, f1_ref, d0_ref, d1_ref, factor_ref, window_ref, out_ref, s_ref):
-    mine = meta[2]
-    live = meta[6].astype(F32)
-    for j in range(NX * NZ):
-        s_ref[pl.ds(pl.multiple_of((2 * j + mine) * 8, 8), 8), :] = own_ref[j] * live
-        s_ref[pl.ds(pl.multiple_of((2 * j + 1 - mine) * 8, 8), 8), :] = other_ref[j] * live
-    for k in range(4):
-        o, e = k * NB, k * NB + NB
-        X = mul_t(s_ref[:, o:e], d0_ref[k])
-        s_ref[:, o:e] = X
-        s_ref[:, e:] = s_ref[:, e:] - mul_t(X, f0_ref[e : 2 * B, o:e])
-    for k in range(4):
-        o, e = k * NB, k * NB + NB
-        X = mul_t(s_ref[:, B + o : B + e], d1_ref[k])
-        s_ref[:, B + o : B + e] = X
-        if e < B:
-            s_ref[:, B + e :] = s_ref[:, B + e :] - mul_t(X, f1_ref[e:B, o:e])
-    out_ref[...] = window_ref[...] - mul_t(factor_ref[...], s_ref[...])
+        s_ref[:B, :B] = f0_ref[B:, :]
+        s_ref[:B, B:] = f1_ref[...]
+
+    factor_ref[...] = s_ref[:B, :]
+    out_ref[...] = window_ref[...] - mul_t(s_ref[:B, :], s_ref[B:, :])
+
+
+def kernel_pick(rows_ref, parts_ref, out_ref):
+    out_ref[...] = parts_ref[...]
 
 
 SMEM = pl.BlockSpec(memory_space=pltpu.SMEM)
@@ -200,12 +234,26 @@
     return pl.pallas_call(
         kernel,
         out_shape=[jax.ShapeDtypeStruct(s, F32) for s in outs],
-        in_specs=[SMEM] + [VM] * (len(args) - 1),
+        in_specs=[SMEM if a.dtype == jnp.int32 else VM for a in args],
         out_specs=[VM] * len(outs),
         scratch_shapes=[pltpu.VMEM(s, F32) for s in scratch],
         compiler_params=pltpu.CompilerParams(vmem_limit_bytes=VMEM_LIMIT),
         cost_estimate=pl.CostEstimate(flops=flops, transcendentals=0, bytes_accessed=8 << 20),
     )(*args)
+
+
+def pick(window_rows, parts):
+    block = (1,) + parts.shape[1:]
+    return pl.pallas_call(
+        kernel_pick,
+        out_shape=jax.ShapeDtypeStruct((NY,) + parts.shape[1:], F32),
+        grid_spec=pltpu.PrefetchScalarGridSpec(
+            num_scalar_prefetch=1,
+            grid=(NY,),
+            in_specs=[pl.BlockSpec(block, lambda i, rows: (rows[i], 0, 0))],
+            out_specs=pl.BlockSpec(block, lambda i, rows: (i, 0, 0)),
+        ),
+    )(window_rows, parts)
 
 
 def rid(x, z, c):
@@ -263,10 +311,6 @@
     row = lax.axis_index("rows")
     y = lax.axis_index("cols")
     x, z, core = row // (2 * NZ), (row // 2) % NZ, row % 2
-    target = window_rows[y]
-    live = jnp.where(row < 2, 1, row_live[row])
-    meta = jnp.stack([x, z, core, y, row, live, row_live[target], 0]).astype(jnp.int32)
-
     width = 2 * B // NY
     mine = lax.dynamic_slice_in_dim(panel, y * width, width, 1).reshape(64, 8, width)
     parts = lax.all_to_all(mine, "rows", 0, 0)
@@ -284,27 +328,19 @@
     other = swap_core(own)
 
     parts = after(parts, part)
-    chosen = jnp.stack([lax.dynamic_index_in_dim(parts, window_rows[c], 0, keepdims=False) for c in range(NY)])
+    chosen = pick(window_rows, parts)
     quarters = lax.all_to_all(chosen, "cols", 0, 0)
     shard = jnp.concatenate([quarters[q] for q in range(NY)], axis=1)
     t_own = lax.all_to_all(jnp.broadcast_to(shard, (32,) + shard.shape), "rows", 0, 0, axis_index_groups=GROUPS)
 
-    meta_a = after(meta, shard)
-    f0, d0 = call(
-        kernel_a, 10**10, [(3 * B, B), (4, NB, NB)], [(2, 5 * H, H), (3 * B, B), (NB, NB)], meta_a, own, other, panel[:, :B]
+    own = after(own, shard)
+    f0, d0 = call(kernel_a, 10**10, [(2 * B, B), (4, NB, NB)], [(2, 5 * H, H), (2 * B, B), (NB, NB)], own, other)
+    t_other = swap_core(after(t_own, f0))
+    f1, d1 = call(kernel_b, 10**10, [(B, B), (4, NB, NB)], [(2, 5 * H, H), (B, B), (NB, NB)], own, other, f0)
+    return call(
+        kernel_c, 10**9, [(B, 2 * B), (B, B)], [(2 * B, 2 * B)],
+        row_live, window_rows, t_own, t_other, f0, f1, d0, d1, panel, window_block,
     )
-    t_other = swap_core(after(t_own, f0))
-    f1, d1, factor = call(
-        kernel_b,
-        10**10,
-        [(2 * B, B), (4, NB, NB), (B, 2 * B)],
-        [(2, 5 * H, H), (2 * B, B), (NB, NB)],
-        meta, own, other, panel[:, B:], f0,
-    )
-    (updated,) = call(
-        kernel_c, 10**9, [(B, B)], [(B, 2 * B)], meta, t_own, t_other, f0, f1, d0, d1, factor, window_block
-    )
-    return factor, updated
 
 
 def solution(mesh):

time: 157 us -> 137 us (0.87)
  Pallas kernels: 64.9 us -> 53.7 us
  between operations: 10.9 us -> 0.93 us
  starting transfers between devices: 52 us -> 56.6 us
  local copies, waits for them, and re-layouts: 9.12 us -> 5.87 us
  other arithmetic: 1.94 us -> 0.27 us
    pallas_call x3, Pallas kernels: 64.9 us -> 50.5 us  [call(): pl.pallas_call(kernel, out_shape=[jax.ShapeDtypeStruct(s, F32) for s in o...]
    ppermute x12, starting transfers between devices: 22.2 us -> 29.6 us  [move(): return lax.ppermute(v, 'rows', pairs)]
    pallas_call x0 -> x1, Pallas kernels: none -> 3.26 us  [pick(): pl.pallas_call(kernel_pick, out_shape=jax.ShapeDtypeStruct((NY,) + parts....]
    all_to_all x1, starting transfers between devices: 8.5 us -> 5.74 us  [shards(): parts = lax.all_to_all(mine, 'rows', 0, 0)]
    all_to_all x1, waiting for transfers between devices: 0.01 us -> 2.47 us  [shards(): lax.all_to_all(jnp.broadcast_to(shard, (32,) + shard.shape), 'rows', 0, 0...]
    slice x2 -> x0, local copies, waits for them, and re-layouts: 2.13 us -> none  [the longest x1 1.5 us: shards(): panel[:, :B]]
    all_to_all x1, starting transfers between devices: 9.02 us -> 7.12 us  [shards(): lax.all_to_all(jnp.broadcast_to(shard, (32,) + shard.shape), 'rows', 0, 0...]
    ppermute x3, starting transfers between devices: 3.85 us -> 5.68 us  [gather_y(): lax.ppermute(v, 'cols', [(i, (i + d) % NY) for i in range(NY)])]
  transfers between devices with their start and end apart: 19 -> 19, of which waited for: 8 -> 9; matrix products, arithmetic and copies ran while one was open for 6% -> 2% of each run, Pallas kernels for 33% -> 29%
where the time goes in v2:
time: 137 us; the launch traced here: 136 us
  starting transfers between devices  56.6 us (41%)
  Pallas kernels  53.7 us (39%)
  waiting for transfers between devices  18.5 us (14%)
  local copies, waits for them, and re-layouts  5.87 us (4%)
    pallas_call x3, Pallas kernels, call(): pl.pallas_call(kernel, out_shape=[jax.ShapeDtypeStruct(s, F32) for s in o...  50.5 us
    ppermute x12, starting transfers between devices, move(): return lax.ppermute(v, 'rows', pairs)  29.6 us
    ppermute x12, waiting for transfers between devices, move(): return lax.ppermute(v, 'rows', pairs)  11.3 us
    all_to_all x1, starting transfers between devices, shards(): lax.all_to_all(jnp.broadcast_to(shard, (32,) + shard.shape), 'rows', 0, 0...  7.12 us
    all_to_all x1, starting transfers between devices, shards(): parts = lax.all_to_all(mine, 'rows', 0, 0)  5.74 us
    ppermute x3, starting transfers between devices, gather_y(): lax.ppermute(v, 'cols', [(i, (i + d) % NY) for i in range(NY)])  5.68 us
    ppermute x1, starting transfers between devices, shards(): low = lax.ppermute(bot[:, :, B:], 'rows', [(1, 0)])  5.15 us
    ppermute x3, waiting for transfers between devices, gather_y(): lax.ppermute(v, 'cols', [(i, (i + d) % NY) for i in range(NY)])  3.82 us
  transfers between devices with their start and end apart: 19, of which 9 were waited for; matrix products, arithmetic and copies ran while one was open for 2% of the time, Pallas kernels for 29%

profile of v2, /device:TPU:1, one launch (start us, length us, event | category | flops | bytes accessed | tf_op | source)
XLA Modules:
  0.0 135.9 jit_solution(7938005018005637419)
XLA Ops:
  0.6 1.1 constant_dynamic-slice_fusion
  1.7 5.2 %collective-permute-start = (f32[4,16,512]{2,1,0:T(8,128)S(1)}, f32[4,16,512]{2,1,0:T(8,128)S(1)}, u32[]{:S(2)}, u32[]{:S(2)}) collective-permute-start(f32[4,16,512]{2,1,0:T(8,128)S(1)} %slice.71), channel_id=1, source_target_pairs={{4,0},{5,1},{6,2},{7,3}} | collective-permute-start | bytes 393224 | tf_op jit(solution)/shard_map/ppermute | solution.py:322
  7.0 0.9 collective-permute-done
  7.9 1.3 collective-permute-start.2
  9.2 1.3 collective-permute-start.3
  10.5 1.3 collective-permute-start.1
  11.8 1.9 %dynamic-slice_bitcast_fusion = f32[64,8,256]{2,1,0:T(8,128)} fusion(f32[512,1024]{1,0:T(8,128)} %panel_ref.1, s32[]{:T(128)S(6)} %select_n.60), kind=kLoop, calls=%fused_computation.1 | loop fusion | bytes 1048580 | tf_op jit(solution)/shard_map/reshape | solution.py:315
  13.7 5.7 %all-to-all-start = ((f32[64,8,256]{2,1,0:T(8,128)}), f32[64,8,256]{2,1,0:T(8,128)S(1)}, u32[]{:S(2)}, u32[]{:S(2)}) async-start(f32[64,8,256]{2,1,0:T(8,128)} %dynamic-slice_bitcast_fusion), calls=%async_computation | async-start | bytes 1048576 | tf_op jit(solution)/shard_map/all_to_all | solution.py:316
  19.5 5.4 %collective-permute-start.6 = (f32[80,256]{1,0:T(8,128)S(1)}, f32[80,256]{1,0:T(8,128)S(1)}, u32[]{:S(2)}, u32[]{:S(2)}) collective-permute-start(f32[80,256]{1,0:T(8,128)S(1)} %fusion.1), channel_id=1, source_target_pairs={{0,48},{4,52},{64,112},{68,116},{128,176},{132,180},{192,240},{196... | collective-permute-start | bytes 245768 | tf_op jit(solution)/shard_map/ppermute | solution.py:271
  25.0 2.5 %collective-permute-start.5 = (f32[80,256]{1,0:T(8,128)S(1)}, f32[80,256]{1,0:T(8,128)S(1)}, u32[]{:S(2)}, u32[]{:S(2)}) collective-permute-start(f32[80,256]{1,0:T(8,128)S(1)} %fusion.1), channel_id=1, source_target_pairs={{0,32},{4,36},{64,96},{68,100},{128,160},{132,164},{192,224},{196,... | collective-permute-start | bytes 245768 | tf_op jit(solution)/shard_map/ppermute | solution.py:271
  27.4 1.3 collective-permute-start.4
  28.7 3.2 %collective-permute-done.6 = f32[80,256]{1,0:T(8,128)S(1)} collective-permute-done((f32[80,256]{1,0:T(8,128)S(1)}, f32[80,256]{1,0:T(8,128)S(1)}, u32[]{:S(2)}, u32[]{:S(2)}) %collective-permute-start.6) | collective-permute-done | bytes 81952 | tf_op jit(solution)/shard_map/ppermute | solution.py:271
  31.9 2.0 %collective-permute-done.4 = f32[80,256]{1,0:T(8,128)S(1)} collective-permute-done((f32[80,256]{1,0:T(8,128)S(1)}, f32[80,256]{1,0:T(8,128)S(1)}, u32[]{:S(2)}, u32[]{:S(2)}) %collective-permute-start.4) | collective-permute-done | bytes 81952 | tf_op jit(solution)/shard_map/ppermute | solution.py:271
  34.0 1.3 collective-permute-start.7
  35.3 1.5 %collective-permute-done.7 = f32[80,256]{1,0:T(8,128)S(1)} collective-permute-done((f32[80,256]{1,0:T(8,128)S(1)}, f32[80,256]{1,0:T(8,128)S(1)}, u32[]{:S(2)}, u32[]{:S(2)}) %collective-permute-start.7) | collective-permute-done | bytes 81952 | tf_op jit(solution)/shard_map/ppermute | solution.py:271
  36.8 2.8 %collective-permute-start.10 = (f32[80,256]{1,0:T(8,128)S(1)}, f32[80,256]{1,0:T(8,128)S(1)}, u32[]{:S(2)}, u32[]{:S(2)}) collective-permute-start(f32[80,256]{1,0:T(8,128)S(1)} %add.56), channel_id=1, source_target_pairs={{0,192},{4,196},{8,200},{12,204},{16,208},{20,212},{24,216},{28,22... | collective-permute-start | bytes 245768 | tf_op jit(solution)/shard_map/ppermute | solution.py:271
  41.1 3.4 %collective-permute-done.9 = f32[80,256]{1,0:T(8,128)S(1)} collective-permute-done((f32[80,256]{1,0:T(8,128)S(1)}, f32[80,256]{1,0:T(8,128)S(1)}, u32[]{:S(2)}, u32[]{:S(2)}) %collective-permute-start.9) | collective-permute-done | bytes 81952 | tf_op jit(solution)/shard_map/ppermute | solution.py:271
  44.5 0.8 collective-permute-done.8
  45.3 3.0 %collective-permute-start.12 = (f32[4,80,256]{2,1,0:T(8,128)S(1)}, f32[4,80,256]{2,1,0:T(8,128)S(1)}, u32[]{:S(2)}, u32[]{:S(2)}) collective-permute-start(f32[4,80,256]{2,1,0:T(8,128)S(1)} %get-tuple-element.19), channel_id=1, source_target_pairs={{0,2},{1,3},{2,0},{3,1},{4,6},{5,7},{6,4},{7,5},{8,10},{9,11},{10,... | collective-permute-start | bytes 983048 | tf_op jit(solution)/shard_map/ppermute | solution.py:303
  48.7 2.3 %collective-permute-start.13 = (f32[4,80,256]{2,1,0:T(8,128)S(1)}, f32[4,80,256]{2,1,0:T(8,128)S(1)}, u32[]{:S(2)}, u32[]{:S(2)}) collective-permute-start(f32[4,80,256]{2,1,0:T(8,128)S(1)} %get-tuple-element.19), channel_id=1, source_target_pairs={{0,3},{1,0},{2,1},{3,2},{4,7},{5,4},{6,5},{7,6},{8,11},{9,8},{10,9... | collective-permute-start | bytes 983048 | tf_op jit(solution)/shard_map/ppermute | solution.py:303
  51.8 3.3 %shard_map.59 = f32[4,8,256]{2,1,0:T(8,128)} custom-call(s32[4]{0:T(128)} %rows_ref.3, f32[64,8,256]{2,1,0:T(8,128)} %copy-done.1), custom_call_target="tpu_custom_call" | custom-call | tf_op jit(solution)/shard_map/pallas_call | solution.py:247
  55.1 3.3 %all-to-all-start.1 = ((f32[4,8,256]{2,1,0:T(8,128)}), f32[4,8,256]{2,1,0:T(8,128)S(1)}, u32[]{:S(2)}, u32[]{:S(2)}) async-start(f32[4,8,256]{2,1,0:T(8,128)} %shard_map.59), calls=%async_computation.1 | async-start | bytes 65536 | tf_op jit(solution)/shard_map/all_to_all | solution.py:332
  58.3 3.8 %collective-permute-done.11 = f32[4,80,256]{2,1,0:T(8,128)S(1)} collective-permute-done((f32[4,80,256]{2,1,0:T(8,128)S(1)}, f32[4,80,256]{2,1,0:T(8,128)S(1)}, u32[]{:S(2)}, u32[]{:S(2)}) %collective-permute-start.11) | collective-permute-done | bytes 327712 | tf_op jit(solution)/shard_map/ppermute | solution.py:303
  62.3 2.5 %collective-permute-start.14 = (f32[4,4,80,256]{3,2,1,0:T(8,128)S(1)}, f32[4,4,80,256]{3,2,1,0:T(8,128)}, u32[]{:S(2)}, u32[]{:S(2)}) collective-permute-start(f32[4,4,80,256]{3,2,1,0:T(8,128)S(1)} %pad_maximum_fusion.own_ref), channel_id=1, source_target_pairs={{0,4},{4,0},{8,12},{12,8},{16,20},{20,16},{24,28},{28,24},{32,36},... | collective-permute-start | bytes 3932168 | tf_op jit(solution)/shard_map/ppermute | solution.py:271
  64.8 1.1 broadcast_in_dim.8
  65.9 7.1 %all-to-all-start.2 = ((f32[32,8,1024]{2,1,0:T(8,128)}), f32[32,8,1024]{2,1,0:T(8,128)S(1)}, u32[]{:S(2)}, u32[]{:S(2)}) async-start(f32[32,8,1024]{2,1,0:T(8,128)} %broadcast_in_dim.8), calls=%async_computation.2 | async-start | bytes 2097152 | tf_op jit(solution)/shard_map/all_to_all | solution.py:334
  73.1 18.1 %shard_map.60 = (f32[1024,512]{1,0:T(8,128)}, f32[4,128,128]{2,1,0:T(8,128)}) custom-call(f32[4,4,80,256]{3,2,1,0:T(8,128)} %copy-done.2, f32[4,4,80,256]{3,2,1,0:T(8,128)} %collective-permute-done.14.other_ref), custom_call_target="tpu_custom_call" | custom-call | flops 10000000000 | bytes 8388608 | tf_op jit(solution)/shard_map/pallas_call | solution.py:234
  91.2 2.5 %all-to-all-done.2.own_ref = f32[32,8,1024]{2,1,0:T(8,128)S(1)} async-done(((f32[32,8,1024]{2,1,0:T(8,128)}), f32[32,8,1024]{2,1,0:T(8,128)S(1)}, u32[]{:S(2)}, u32[]{:S(2)}) %all-to-all-start.2) | async-done | bytes 1048608 | tf_op jit(solution)/shard_map/all_to_all | solution.py:334
  93.6 8.9 %collective-permute-start.15 = (f32[32,8,1024]{2,1,0:T(8,128)S(1)}, f32[32,8,1024]{2,1,0:T(8,128)S(1)}, u32[]{:S(2)}, u32[]{:S(2)}) collective-permute-start(f32[32,8,1024]{2,1,0:T(8,128)S(1)} %all-to-all-done.2.own_ref), channel_id=1, source_target_pairs={{0,4},{4,0},{8,12},{12,8},{16,20},{20,16},{24,28},{28,24},{32,36},... | collective-permute-start | bytes 3145736 | tf_op jit(solution)/shard_map/ppermute | solution.py:271
  102.5 17.5 %shard_map.61 = (f32[512,512]{1,0:T(8,128)}, f32[4,128,128]{2,1,0:T(8,128)}) custom-call(f32[4,4,80,256]{3,2,1,0:T(8,128)} %copy-done.2, f32[4,4,80,256]{3,2,1,0:T(8,128)} %collective-permute-done.14.other_ref, f32[1024,512]{1,0:T(8,128)} %get-tuple-element.11.f0_ref), custom_call_target="tpu_custom_call" | custom-call | flops 10000000000 | bytes 8388608 | tf_op jit(solution)/shard_map/pallas_call | solution.py:234
  120.1 1.0 copy-done.3
  121.0 14.8 %shard_map.62 = (f32[512,1024]{1,0:T(8,128)}, f32[512,512]{1,0:T(8,128)}) custom-call(s32[64]{0:T(128)} %live_ref.1, s32[4]{0:T(128)} %rows_ref.3, f32[32,8,1024]{2,1,0:T(8,128)} %copy-done, f32[32,8,1024]{2,1,0:T(8,128)} %copy-done.3, f32[1024,512]{1,0:T(8,128)} %get-tuple-element.11.f0_ref, f32[512,512]{1,0:T(8,128)} %get-tuple-element.13.f1_ref, ...), custom_call_target="tpu_custom_call" | custom-call | flops 1000000000 | bytes 8388608 | tf_op jit(solution)/shard_map/pallas_call | solution.py:234
  (35 shorter events, 3.0 us)
Async XLA Ops:
  1.7 6.1 %collective-permute-start = (f32[4,16,512]{2,1,0:T(8,128)S(1)}, f32[4,16,512]{2,1,0:T(8,128)S(1)}, u32[]{:S(2)}, u32[]{:S(2)}) collective-permute-start(f32[4,16,512]{2,1,0:T(8,128)S(1)} %slice.71), channel_id=1, source_target_pairs={{4,0},{5,1},{6,2},{7,3}} | collective-permute-start | bytes 393224 | tf_op jit(solution)/shard_map/ppermute | solution.py:322
  7.9 11.6 %collective-permute-start.2 = (f32[80,256]{1,0:T(8,128)S(1)}, f32[80,256]{1,0:T(8,128)S(1)}, u32[]{:S(2)}, u32[]{:S(2)}) collective-permute-start(f32[80,256]{1,0:T(8,128)S(1)} %get-tuple-element.20), channel_id=1, source_target_pairs={{0,128},{4,132},{1,129},{5,133},{2,130},{6,134},{3,131},{7,135}} | collective-permute-start | bytes 245768 | tf_op jit(solution)/shard_map/ppermute | solution.py:271
  9.2 10.3 %collective-permute-start.3 = (f32[80,256]{1,0:T(8,128)S(1)}, f32[80,256]{1,0:T(8,128)S(1)}, u32[]{:S(2)}, u32[]{:S(2)}) collective-permute-start(f32[80,256]{1,0:T(8,128)S(1)} %get-tuple-element.21), channel_id=1, source_target_pairs={{0,192},{4,196},{1,193},{5,197},{2,194},{6,198},{3,195},{7,199}} | collective-permute-start | bytes 245768 | tf_op jit(solution)/shard_map/ppermute | solution.py:271
  10.5 9.0 %collective-permute-start.1 = (f32[80,256]{1,0:T(8,128)S(1)}, f32[80,256]{1,0:T(8,128)S(1)}, u32[]{:S(2)}, u32[]{:S(2)}) collective-permute-start(f32[80,256]{1,0:T(8,128)S(1)} %get-tuple-element.22), channel_id=1, source_target_pairs={{0,64},{4,68},{1,65},{5,69},{2,66},{6,70},{3,67},{7,71}} | collective-permute-start | bytes 245768 | tf_op jit(solution)/shard_map/ppermute | solution.py:271
  13.7 37.3 %all-to-all-start = ((f32[64,8,256]{2,1,0:T(8,128)}), f32[64,8,256]{2,1,0:T(8,128)S(1)}, u32[]{:S(2)}, u32[]{:S(2)}) async-start(f32[64,8,256]{2,1,0:T(8,128)} %dynamic-slice_bitcast_fusion), calls=%async_computation | async-start | bytes 1048576 | tf_op jit(solution)/shard_map/all_to_all | solution.py:316
  19.5 12.4 %collective-permute-start.6 = (f32[80,256]{1,0:T(8,128)S(1)}, f32[80,256]{1,0:T(8,128)S(1)}, u32[]{:S(2)}, u32[]{:S(2)}) collective-permute-start(f32[80,256]{1,0:T(8,128)S(1)} %fusion.1), channel_id=1, source_target_pairs={{0,48},{4,52},{64,112},{68,116},{128,176},{132,180},{192,240},{196... | collective-permute-start | bytes 245768 | tf_op jit(solution)/shard_map/ppermute | solution.py:271
  25.0 7.0 %collective-permute-start.5 = (f32[80,256]{1,0:T(8,128)S(1)}, f32[80,256]{1,0:T(8,128)S(1)}, u32[]{:S(2)}, u32[]{:S(2)}) collective-permute-start(f32[80,256]{1,0:T(8,128)S(1)} %fusion.1), channel_id=1, source_target_pairs={{0,32},{4,36},{64,96},{68,100},{128,160},{132,164},{192,224},{196,... | collective-permute-start | bytes 245768 | tf_op jit(solution)/shard_map/ppermute | solution.py:271
  27.4 6.5 %collective-permute-start.4 = (f32[80,256]{1,0:T(8,128)S(1)}, f32[80,256]{1,0:T(8,128)S(1)}, u32[]{:S(2)}, u32[]{:S(2)}) collective-permute-start(f32[80,256]{1,0:T(8,128)S(1)} %fusion.1), channel_id=1, source_target_pairs={{0,16},{4,20},{64,80},{68,84},{128,144},{132,148},{192,208},{196,2... | collective-permute-start | bytes 245768 | tf_op jit(solution)/shard_map/ppermute | solution.py:271
  34.0 2.8 %collective-permute-start.7 = (f32[80,256]{1,0:T(8,128)S(1)}, f32[80,256]{1,0:T(8,128)S(1)}, u32[]{:S(2)}, u32[]{:S(2)}) collective-permute-start(f32[80,256]{1,0:T(8,128)S(1)} %add_add_fusion), channel_id=1, source_target_pairs={{0,8},{4,12},{16,24},{20,28},{32,40},{36,44},{48,56},{52,60},{64,7... | collective-permute-start | bytes 245768 | tf_op jit(solution)/shard_map/ppermute | solution.py:271
  36.8 4.3 %collective-permute-start.10 = (f32[80,256]{1,0:T(8,128)S(1)}, f32[80,256]{1,0:T(8,128)S(1)}, u32[]{:S(2)}, u32[]{:S(2)}) collective-permute-start(f32[80,256]{1,0:T(8,128)S(1)} %add.56), channel_id=1, source_target_pairs={{0,192},{4,196},{8,200},{12,204},{16,208},{20,212},{24,216},{28,22... | collective-permute-start | bytes 245768 | tf_op jit(solution)/shard_map/ppermute | solution.py:271
  39.6 4.9 %collective-permute-start.9 = (f32[80,256]{1,0:T(8,128)S(1)}, f32[80,256]{1,0:T(8,128)S(1)}, u32[]{:S(2)}, u32[]{:S(2)}) collective-permute-start(f32[80,256]{1,0:T(8,128)S(1)} %add.56), channel_id=1, source_target_pairs={{0,128},{4,132},{8,136},{12,140},{16,144},{20,148},{24,152},{28,15... | collective-permute-start | bytes 245768 | tf_op jit(solution)/shard_map/ppermute | solution.py:271
  40.0 5.3 %collective-permute-start.8 = (f32[80,256]{1,0:T(8,128)S(1)}, f32[80,256]{1,0:T(8,128)S(1)}, u32[]{:S(2)}, u32[]{:S(2)}) collective-permute-start(f32[80,256]{1,0:T(8,128)S(1)} %add.56), channel_id=1, source_target_pairs={{0,64},{4,68},{8,72},{12,76},{16,80},{20,84},{24,88},{28,92},{32,9... | collective-permute-start | bytes 245768 | tf_op jit(solution)/shard_map/ppermute | solution.py:271
  45.3 13.0 %collective-permute-start.12 = (f32[4,80,256]{2,1,0:T(8,128)S(1)}, f32[4,80,256]{2,1,0:T(8,128)S(1)}, u32[]{:S(2)}, u32[]{:S(2)}) collective-permute-start(f32[4,80,256]{2,1,0:T(8,128)S(1)} %get-tuple-element.19), channel_id=1, source_target_pairs={{0,2},{1,3},{2,0},{3,1},{4,6},{5,7},{6,4},{7,5},{8,10},{9,11},{10,... | collective-permute-start | bytes 983048 | tf_op jit(solution)/shard_map/ppermute | solution.py:303
  48.3 13.8 %collective-permute-start.11 = (f32[4,80,256]{2,1,0:T(8,128)S(1)}, f32[4,80,256]{2,1,0:T(8,128)S(1)}, u32[]{:S(2)}, u32[]{:S(2)}) collective-permute-start(f32[4,80,256]{2,1,0:T(8,128)S(1)} %get-tuple-element.19), channel_id=1, source_target_pairs={{0,1},{1,2},{2,3},{3,0},{4,5},{5,6},{6,7},{7,4},{8,9},{9,10},{10,1... | collective-permute-start | bytes 983048 | tf_op jit(solution)/shard_map/ppermute | solution.py:303
  48.7 13.4 %collective-permute-start.13 = (f32[4,80,256]{2,1,0:T(8,128)S(1)}, f32[4,80,256]{2,1,0:T(8,128)S(1)}, u32[]{:S(2)}, u32[]{:S(2)}) collective-permute-start(f32[4,80,256]{2,1,0:T(8,128)S(1)} %get-tuple-element.19), channel_id=1, source_target_pairs={{0,3},{1,0},{2,1},{3,2},{4,7},{5,4},{6,5},{7,6},{8,11},{9,8},{10,9... | collective-permute-start | bytes 983048 | tf_op jit(solution)/shard_map/ppermute | solution.py:303
  51.0 0.8 copy-start.1
  55.1 9.7 %all-to-all-start.1 = ((f32[4,8,256]{2,1,0:T(8,128)}), f32[4,8,256]{2,1,0:T(8,128)S(1)}, u32[]{:S(2)}, u32[]{:S(2)}) async-start(f32[4,8,256]{2,1,0:T(8,128)} %shard_map.59), calls=%async_computation.1 | async-start | bytes 65536 | tf_op jit(solution)/shard_map/all_to_all | solution.py:332
  62.3 3.6 %copy-start.2 = (f32[4,4,80,256]{3,2,1,0:T(8,128)}, f32[4,4,80,256]{3,2,1,0:T(8,128)S(1)}, u32[]{:S(2)}) copy-start(f32[4,4,80,256]{3,2,1,0:T(8,128)S(1)} %pad_maximum_fusion.own_ref) | copy-start | bytes 3932164
  62.3 10.7 %collective-permute-start.14 = (f32[4,4,80,256]{3,2,1,0:T(8,128)S(1)}, f32[4,4,80,256]{3,2,1,0:T(8,128)}, u32[]{:S(2)}, u32[]{:S(2)}) collective-permute-start(f32[4,4,80,256]{3,2,1,0:T(8,128)S(1)} %pad_maximum_fusion.own_ref), channel_id=1, source_target_pairs={{0,4},{4,0},{8,12},{12,8},{16,20},{20,16},{24,28},{28,24},{32,36},... | collective-permute-start | bytes 3932168 | tf_op jit(solution)/shard_map/ppermute | solution.py:271
  65.9 27.7 %all-to-all-start.2 = ((f32[32,8,1024]{2,1,0:T(8,128)}), f32[32,8,1024]{2,1,0:T(8,128)S(1)}, u32[]{:S(2)}, u32[]{:S(2)}) async-start(f32[32,8,1024]{2,1,0:T(8,128)} %broadcast_in_dim.8), calls=%async_computation.2 | async-start | bytes 2097152 | tf_op jit(solution)/shard_map/all_to_all | solution.py:334
  93.6 26.4 %copy-start = (f32[32,8,1024]{2,1,0:T(8,128)}, f32[32,8,1024]{2,1,0:T(8,128)S(1)}, u32[]{:S(2)}) copy-start(f32[32,8,1024]{2,1,0:T(8,128)S(1)} %all-to-all-done.2.own_ref) | copy-start | bytes 3145732
  93.6 26.4 %collective-permute-start.15 = (f32[32,8,1024]{2,1,0:T(8,128)S(1)}, f32[32,8,1024]{2,1,0:T(8,128)S(1)}, u32[]{:S(2)}, u32[]{:S(2)}) collective-permute-start(f32[32,8,1024]{2,1,0:T(8,128)S(1)} %all-to-all-done.2.own_ref), channel_id=1, source_target_pairs={{0,4},{4,0},{8,12},{12,8},{16,20},{20,16},{24,28},{28,24},{32,36},... | collective-permute-start | bytes 3145736 | tf_op jit(solution)/shard_map/ppermute | solution.py:271
  120.1 1.0 copy-start.3

commit v3 on v2

--- a/solution.py
+++ b/solution.py
@@ -12,7 +12,6 @@
 NB = 128
 H = B // 2
 NX, NZ, NY = 4, 8, 4
-VMEM_LIMIT = 56 << 20
 CONTRACT = (((1,), (1,)), ((), ()))
 
 
@@ -189,37 +188,44 @@
     return jnp.concatenate([top, jnp.concatenate([corner, x1], axis=1)], axis=0)
 
 
-def kernel_c(live_ref, rows_ref, own_ref, other_ref, f0_ref, f1_ref, d0_ref, d1_ref, panel_ref, window_ref, factor_ref, out_ref, s_ref):
-    row = lax.axis_index("rows")
-    _, y, mine = coords()
-    live_t = live_ref[rows_ref[y]].astype(F32)
-    live = jnp.where(row < 2, 1, live_ref[row]).astype(F32)
-    s_ref[:B, :] = panel_ref[...] * live
-    for j in range(NX * NZ):
-        s_ref[pl.ds(pl.multiple_of(B + (2 * j + mine) * 8, 8), 8), :] = own_ref[j] * live_t
-        s_ref[pl.ds(pl.multiple_of(B + (2 * j + 1 - mine) * 8, 8), 8), :] = other_ref[j] * live_t
+def solve_rows(s_ref, inv, f0_ref, f1_ref):
     for k in range(4):
         o, e = k * H, (k + 1) * H
-        f_ref, d_ref, base = (f0_ref, d0_ref, 0) if k < 2 else (f1_ref, d1_ref, B)
-        p = o - base
-        inv = pair_inverse(d_ref, 2 * (k % 2), f_ref[p + NB : p + H, p : p + NB])
-        X = mul_t(s_ref[:, o:e], inv)
+        f_ref, p = (f0_ref, o) if k < 2 else (f1_ref, o - B)
+        X = mul_t(s_ref[:, o:e], inv(k))
         s_ref[:, o:e] = X
         if k < 3:
             s_ref[:, e:] = s_ref[:, e:] - mul_t(X, f_ref[p + H :, p : p + H])
 
+
+def kernel_own(live_ref, f0_ref, f1_ref, d0_ref, d1_ref, panel_ref, factor_ref, inv_ref):
+    row = lax.axis_index("rows")
+    live = jnp.where(row < 2, 1, live_ref[row]).astype(F32)
+    factor_ref[...] = panel_ref[...] * live
+    for k in range(4):
+        f_ref, d_ref, p = (f0_ref, d0_ref, k * H) if k < 2 else (f1_ref, d1_ref, k * H - B)
+        inv_ref[k] = pair_inverse(d_ref, 2 * (k % 2), f_ref[p + NB : p + H, p : p + NB])
+    solve_rows(factor_ref, lambda k: inv_ref[k], f0_ref, f1_ref)
+
     @pl.when(row == 0)
     def _():
-        s_ref[:B, :B] = f0_ref[:B, :]
-        s_ref[:B, B:] = jnp.zeros((B, B), F32)
+        factor_ref[:, :B] = f0_ref[:B, :]
+        factor_ref[:, B:] = jnp.zeros((B, B), F32)
 
     @pl.when(row == 1)
     def _():
-        s_ref[:B, :B] = f0_ref[B:, :]
-        s_ref[:B, B:] = f1_ref[...]
-
-    factor_ref[...] = s_ref[:B, :]
-    out_ref[...] = window_ref[...] - mul_t(s_ref[:B, :], s_ref[B:, :])
+        factor_ref[:, :B] = f0_ref[B:, :]
+        factor_ref[:, B:] = f1_ref[...]
+
+
+def kernel_window(live_ref, rows_ref, own_ref, other_ref, f0_ref, f1_ref, inv_ref, factor_ref, window_ref, out_ref, s_ref):
+    _, y, mine = coords()
+    live_t = live_ref[rows_ref[y]].astype(F32)
+    for j in range(NX * NZ):
+        s_ref[pl.ds(pl.multiple_of((2 * j + mine) * 8, 8), 8), :] = own_ref[j] * live_t
+        s_ref[pl.ds(pl.multiple_of((2 * j + 1 - mine) * 8, 8), 8), :] = other_ref[j] * live_t
+    solve_rows(s_ref, lambda k: inv_ref[k], f0_ref, f1_ref)
+    out_ref[...] = window_ref[...] - mul_t(factor_ref[...], s_ref[...])
 
 
 def kernel_pick(rows_ref, parts_ref, out_ref):
@@ -230,14 +236,14 @@
 VM = pl.BlockSpec(memory_space=pltpu.VMEM)
 
 
-def call(kernel, flops, outs, scratch, *args):
+def call(kernel, flops, vmem, outs, scratch, *args):
     return pl.pallas_call(
         kernel,
         out_shape=[jax.ShapeDtypeStruct(s, F32) for s in outs],
         in_specs=[SMEM if a.dtype == jnp.int32 else VM for a in args],
         out_specs=[VM] * len(outs),
         scratch_shapes=[pltpu.VMEM(s, F32) for s in scratch],
-        compiler_params=pltpu.CompilerParams(vmem_limit_bytes=VMEM_LIMIT),
+        compiler_params=pltpu.CompilerParams(vmem_limit_bytes=vmem << 20),
         cost_estimate=pl.CostEstimate(flops=flops, transcendentals=0, bytes_accessed=8 << 20),
     )(*args)
 
@@ -296,7 +302,7 @@
     piece = piece + sum(by_x(v[d], d, lambda x, z, c: x == 0 and z == 0) for d in range(1, NX))
     piece = piece + sum(by_z(piece, d, lambda x, z, c: z == 0) for d in (2, 4, 6))
     piece = piece + by_z(piece, 1, lambda x, z, c: z % 2 == 0)
-    return jnp.stack([piece] + [by_x(piece, d) for d in range(1, NX)])
+    return piece, jnp.stack([piece] + [by_x(piece, d) for d in range(1, NX)])
 
 
 def gather_y(v):
@@ -323,24 +329,27 @@
     first = [top[:, :, :H], bot[:, :, :H], bot[:, :, H:B], low[:, :, :H], low[:, :, H:]]
     second = [top[:, :, :H], top[:, :, H:B], bot[:, :, :H], bot[:, :, H:B], top[:, :, B : B + H]]
     stack = jnp.concatenate([jnp.where(core == 0, f, s) for f, s in zip(first, second)], axis=1)
-    part = spread_static(stack, x, z)
-    own = gather_y(part)
-    other = swap_core(own)
-
-    parts = after(parts, part)
+    piece, part = spread_static(stack, x, z)
+
+    parts = after(parts, piece)
     chosen = pick(window_rows, parts)
     quarters = lax.all_to_all(chosen, "cols", 0, 0)
     shard = jnp.concatenate([quarters[q] for q in range(NY)], axis=1)
-    t_own = lax.all_to_all(jnp.broadcast_to(shard, (32,) + shard.shape), "rows", 0, 0, axis_index_groups=GROUPS)
-
-    own = after(own, shard)
-    f0, d0 = call(kernel_a, 10**10, [(2 * B, B), (4, NB, NB)], [(2, 5 * H, H), (2 * B, B), (NB, NB)], own, other)
-    t_other = swap_core(after(t_own, f0))
-    f1, d1 = call(kernel_b, 10**10, [(B, B), (4, NB, NB)], [(2, 5 * H, H), (B, B), (NB, NB)], own, other, f0)
-    return call(
-        kernel_c, 10**9, [(B, 2 * B), (B, B)], [(2 * B, 2 * B)],
-        row_live, window_rows, t_own, t_other, f0, f1, d0, d1, panel, window_block,
+    own = gather_y(after(part, shard))
+    other = swap_core(own)
+    t_own = lax.all_to_all(jnp.broadcast_to(after(shard, part), (32,) + shard.shape), "rows", 0, 0, axis_index_groups=GROUPS)
+
+    f0, d0 = call(kernel_a, 25 * 10**8, 24, [(2 * B, B), (4, NB, NB)], [(2, 5 * H, H), (2 * B, B), (NB, NB)], own, other)
+    f1, d1 = call(kernel_b, 25 * 10**8, 20, [(B, B), (4, NB, NB)], [(2, 5 * H, H), (B, B), (NB, NB)], own, other, f0)
+    t_other = swap_core(after(t_own, f1))
+    factor, inv = call(
+        kernel_own, 10**8, 28, [(B, 2 * B), (4, H, H)], [], row_live, f0, f1, d0, d1, panel
     )
+    (updated,) = call(
+        kernel_window, 10**9, 32, [(B, B)], [(B, 2 * B)],
+        row_live, window_rows, t_own, t_other, f0, f1, inv, factor, window_block,
+    )
+    return factor, updated
 
 
 def solution(mesh):

time: 137 us -> 129 us (0.942)
  starting transfers between devices: 56.6 us -> 48.7 us
  Pallas kernels: 53.7 us -> 46 us
  local copies, waits for them, and re-layouts: 5.87 us -> 11.9 us
  waiting for transfers between devices: 18.5 us -> 20 us
    ppermute x12, starting transfers between devices: 29.6 us -> 20 us  [move(): return lax.ppermute(v, 'rows', pairs)]
    pallas_call x3 -> x4, Pallas kernels: 50.5 us -> 42.7 us  [call(): pl.pallas_call(kernel, out_shape=[jax.ShapeDtypeStruct(s, F32) for s in o...]
    unnamed x9 -> x23, local copies, waits for them, and re-layouts: 1.8 us -> 7.83 us
    all_to_all x1, waiting for transfers between devices: 0.01 us -> 4.25 us  [shards(): quarters = lax.all_to_all(chosen, 'cols', 0, 0)]
    ppermute x3, starting transfers between devices: 5.68 us -> 2.14 us  [gather_y(): lax.ppermute(v, 'cols', [(i, (i + d) % NY) for i in range(NY)])]
    all_to_all x1, starting transfers between devices: 5.74 us -> 8.5 us  [shards(): parts = lax.all_to_all(mine, 'rows', 0, 0)]
    all_to_all x1, waiting for transfers between devices: 2.47 us -> 0.01 us  [shards(): lax.all_to_all(jnp.broadcast_to(after(shard, part), (32,) + shard.shape),...]
    ppermute x3, waiting for transfers between devices: 3.82 us -> 5.52 us  [gather_y(): lax.ppermute(v, 'cols', [(i, (i + d) % NY) for i in range(NY)])]
  transfers between devices with their start and end apart: 19 -> 19, of which waited for: 9 -> 9; matrix products, arithmetic and copies ran while one was open for 2% -> 3% of each run, Pallas kernels for 29% -> 30%
where the time goes in v3:
time: 129 us; the launch traced here: 128 us
  starting transfers between devices  48.7 us (38%)
  Pallas kernels  46 us (36%)
  waiting for transfers between devices  20 us (16%)
  local copies, waits for them, and re-layouts  11.9 us (9%)
    pallas_call x4, Pallas kernels, call(): pl.pallas_call(kernel, out_shape=[jax.ShapeDtypeStruct(s, F32) for s in o...  42.7 us
    ppermute x12, starting transfers between devices, move(): return lax.ppermute(v, 'rows', pairs)  20 us
    ppermute x12, waiting for transfers between devices, move(): return lax.ppermute(v, 'rows', pairs)  10.2 us
    all_to_all x1, starting transfers between devices, shards(): lax.all_to_all(jnp.broadcast_to(after(shard, part), (32,) + shard.shape),...  8.67 us
    all_to_all x1, starting transfers between devices, shards(): parts = lax.all_to_all(mine, 'rows', 0, 0)  8.5 us
    unnamed x23, local copies, waits for them, and re-layouts  7.83 us
    ppermute x3, waiting for transfers between devices, gather_y(): lax.ppermute(v, 'cols', [(i, (i + d) % NY) for i in range(NY)])  5.52 us
    ppermute x1, starting transfers between devices, shards(): low = lax.ppermute(bot[:, :, B:], 'rows', [(1, 0)])  5.15 us
  transfers between devices with their start and end apart: 19, of which 9 were waited for; matrix products, arithmetic and copies ran while one was open for 3% of the time, Pallas kernels for 30%

profile of v3, /device:TPU:1, one launch (start us, length us, event | category | flops | bytes accessed | tf_op | source)
XLA Modules:
  0.0 127.8 jit_solution(17925621465026056940)
XLA Ops:
  0.6 1.1 constant_dynamic-slice_fusion
  1.7 5.2 %collective-permute-start = (f32[4,16,512]{2,1,0:T(8,128)S(1)}, f32[4,16,512]{2,1,0:T(8,128)S(1)}, u32[]{:S(2)}, u32[]{:S(2)}) collective-permute-start(f32[4,16,512]{2,1,0:T(8,128)S(1)} %slice.71), channel_id=1, source_target_pairs={{4,0},{5,1},{6,2},{7,3}} | collective-permute-start | bytes 393224 | tf_op jit(solution)/shard_map/ppermute | solution.py:328
  6.9 1.9 %dynamic-slice_bitcast_fusion = f32[64,8,256]{2,1,0:T(8,128)} fusion(f32[512,1024]{1,0:T(8,128)} %panel_ref.1, s32[]{:T(128)S(6)} %select_n.74), kind=kLoop, calls=%fused_computation.1 | loop fusion | bytes 1048580 | tf_op jit(solution)/shard_map/reshape | solution.py:321
  8.8 8.5 %all-to-all-start = ((f32[64,8,256]{2,1,0:T(8,128)}), f32[64,8,256]{2,1,0:T(8,128)S(1)}, u32[]{:S(2)}, u32[]{:S(2)}) async-start(f32[64,8,256]{2,1,0:T(8,128)} %dynamic-slice_bitcast_fusion), calls=%async_computation | async-start | bytes 1048576 | tf_op jit(solution)/shard_map/all_to_all | solution.py:322
  17.4 4.9 %collective-permute-start.2 = (f32[80,256]{1,0:T(8,128)S(1)}, f32[80,256]{1,0:T(8,128)S(1)}, u32[]{:S(2)}, u32[]{:S(2)}) collective-permute-start(f32[80,256]{1,0:T(8,128)S(1)} %get-tuple-element.24), channel_id=1, source_target_pairs={{0,128},{4,132},{1,129},{5,133},{2,130},{6,134},{3,131},{7,135}} | collective-permute-start | bytes 245768 | tf_op jit(solution)/shard_map/ppermute | solution.py:277
  22.3 1.3 %collective-permute-start.3 = (f32[80,256]{1,0:T(8,128)S(1)}, f32[80,256]{1,0:T(8,128)S(1)}, u32[]{:S(2)}, u32[]{:S(2)}) collective-permute-start(f32[80,256]{1,0:T(8,128)S(1)} %get-tuple-element.25), channel_id=1, source_target_pairs={{0,192},{4,196},{1,193},{5,197},{2,194},{6,198},{3,195},{7,199}} | collective-permute-start | bytes 245768 | tf_op jit(solution)/shard_map/ppermute | solution.py:277
  23.6 1.3 %collective-permute-start.1 = (f32[80,256]{1,0:T(8,128)S(1)}, f32[80,256]{1,0:T(8,128)S(1)}, u32[]{:S(2)}, u32[]{:S(2)}) collective-permute-start(f32[80,256]{1,0:T(8,128)S(1)} %get-tuple-element.26), channel_id=1, source_target_pairs={{0,64},{4,68},{1,65},{5,69},{2,66},{6,70},{3,67},{7,71}} | collective-permute-start | bytes 245768 | tf_op jit(solution)/shard_map/ppermute | solution.py:277
  25.7 3.2 %collective-permute-done.1 = f32[80,256]{1,0:T(8,128)S(1)} collective-permute-done((f32[80,256]{1,0:T(8,128)S(1)}, f32[80,256]{1,0:T(8,128)S(1)}, u32[]{:S(2)}, u32[]{:S(2)}) %collective-permute-start.1) | collective-permute-done | bytes 81952 | tf_op jit(solution)/shard_map/ppermute | solution.py:277
  28.9 1.3 %collective-permute-start.6 = (f32[80,256]{1,0:T(8,128)S(1)}, f32[80,256]{1,0:T(8,128)S(1)}, u32[]{:S(2)}, u32[]{:S(2)}) collective-permute-start(f32[80,256]{1,0:T(8,128)S(1)} %fusion.1), channel_id=1, source_target_pairs={{0,48},{4,52},{64,112},{68,116},{128,176},{132,180},{192,240},{196... | collective-permute-start | bytes 245768 | tf_op jit(solution)/shard_map/ppermute | solution.py:277
  30.2 1.3 %collective-permute-start.5 = (f32[80,256]{1,0:T(8,128)S(1)}, f32[80,256]{1,0:T(8,128)S(1)}, u32[]{:S(2)}, u32[]{:S(2)}) collective-permute-start(f32[80,256]{1,0:T(8,128)S(1)} %fusion.1), channel_id=1, source_target_pairs={{0,32},{4,36},{64,96},{68,100},{128,160},{132,164},{192,224},{196,... | collective-permute-start | bytes 245768 | tf_op jit(solution)/shard_map/ppermute | solution.py:277
  31.5 1.3 %collective-permute-start.4 = (f32[80,256]{1,0:T(8,128)S(1)}, f32[80,256]{1,0:T(8,128)S(1)}, u32[]{:S(2)}, u32[]{:S(2)}) collective-permute-start(f32[80,256]{1,0:T(8,128)S(1)} %fusion.1), channel_id=1, source_target_pairs={{0,16},{4,20},{64,80},{68,84},{128,144},{132,148},{192,208},{196,2... | collective-permute-start | bytes 245768 | tf_op jit(solution)/shard_map/ppermute | solution.py:277
  33.0 2.0 %collective-permute-done.4 = f32[80,256]{1,0:T(8,128)S(1)} collective-permute-done((f32[80,256]{1,0:T(8,128)S(1)}, f32[80,256]{1,0:T(8,128)S(1)}, u32[]{:S(2)}, u32[]{:S(2)}) %collective-permute-start.4) | collective-permute-done | bytes 81952 | tf_op jit(solution)/shard_map/ppermute | solution.py:277
  35.0 1.3 %collective-permute-start.7 = (f32[80,256]{1,0:T(8,128)S(1)}, f32[80,256]{1,0:T(8,128)S(1)}, u32[]{:S(2)}, u32[]{:S(2)}) collective-permute-start(f32[80,256]{1,0:T(8,128)S(1)} %add_add_fusion), channel_id=1, source_target_pairs={{0,8},{4,12},{16,24},{20,28},{32,40},{36,44},{48,56},{52,60},{64,7... | collective-permute-start | bytes 245768 | tf_op jit(solution)/shard_map/ppermute | solution.py:277
  36.3 1.5 %collective-permute-done.7 = f32[80,256]{1,0:T(8,128)S(1)} collective-permute-done((f32[80,256]{1,0:T(8,128)S(1)}, f32[80,256]{1,0:T(8,128)S(1)}, u32[]{:S(2)}, u32[]{:S(2)}) %collective-permute-start.7) | collective-permute-done | bytes 81952 | tf_op jit(solution)/shard_map/ppermute | solution.py:277
  38.6 3.7 %collective-permute-start.9 = (f32[80,256]{1,0:T(8,128)S(1)}, f32[80,256]{1,0:T(8,128)S(1)}, u32[]{:S(2)}, u32[]{:S(2)}) collective-permute-start(f32[80,256]{1,0:T(8,128)S(1)} %add.55), channel_id=1, source_target_pairs={{0,128},{4,132},{8,136},{12,140},{16,144},{20,148},{24,152},{28,15... | collective-permute-start | bytes 245768 | tf_op jit(solution)/shard_map/ppermute | solution.py:277
  43.1 3.3 %shard_map.59 = f32[4,8,256]{2,1,0:T(8,128)} custom-call(s32[4]{0:T(128)} %rows_ref.3, f32[64,8,256]{2,1,0:T(8,128)} %copy-done.10), custom_call_target="tpu_custom_call" | custom-call | tf_op jit(solution)/shard_map/pallas_call | solution.py:253
  46.4 4.2 %all-to-all-start.1 = ((f32[4,8,256]{2,1,0:T(8,128)}), f32[4,8,256]{2,1,0:T(8,128)S(1)}, u32[]{:S(2)}, u32[]{:S(2)}) async-start(f32[4,8,256]{2,1,0:T(8,128)} %shard_map.59), calls=%async_computation.1 | async-start | bytes 65536 | tf_op jit(solution)/shard_map/all_to_all | solution.py:336
  50.6 4.2 %all-to-all-done.1 = f32[4,8,256]{2,1,0:T(8,128)S(1)} async-done(((f32[4,8,256]{2,1,0:T(8,128)}), f32[4,8,256]{2,1,0:T(8,128)S(1)}, u32[]{:S(2)}, u32[]{:S(2)}) %all-to-all-start.1) | async-done | bytes 32800 | tf_op jit(solution)/shard_map/all_to_all | solution.py:336
  55.9 1.2 collective-permute-start.12
  57.0 1.1 broadcast_in_dim.8
  58.1 8.7 %all-to-all-start.2 = ((f32[32,8,1024]{2,1,0:T(8,128)}), f32[32,8,1024]{2,1,0:T(8,128)S(1)}, u32[]{:S(2)}, u32[]{:S(2)}) async-start(f32[32,8,1024]{2,1,0:T(8,128)} %broadcast_in_dim.8), calls=%async_computation.2 | async-start | bytes 2097152 | tf_op jit(solution)/shard_map/all_to_all | solution.py:340
  66.8 5.5 %collective-permute-done.11 = f32[4,80,256]{2,1,0:T(8,128)S(1)} collective-permute-done((f32[4,80,256]{2,1,0:T(8,128)S(1)}, f32[4,80,256]{2,1,0:T(8,128)S(1)}, u32[]{:S(2)}, u32[]{:S(2)}) %collective-permute-start.11) | collective-permute-done | bytes 327712 | tf_op jit(solution)/shard_map/ppermute | solution.py:309
  72.5 2.4 %collective-permute-start.14 = (f32[4,4,80,256]{3,2,1,0:T(8,128)S(1)}, f32[4,4,80,256]{3,2,1,0:T(8,128)S(1)}, u32[]{:S(2)}, u32[]{:S(2)}) collective-permute-start(f32[4,4,80,256]{3,2,1,0:T(8,128)S(1)} %pad_maximum_fusion.own_ref), channel_id=1, source_target_pairs={{0,4},{4,0},{8,12},{12,8},{16,20},{20,16},{24,28},{28,24},{32,36},... | collective-permute-start | bytes 3932168 | tf_op jit(solution)/shard_map/ppermute | solution.py:277
  74.9 2.7 %collective-permute-done.14.other_ref = f32[4,4,80,256]{3,2,1,0:T(8,128)S(1)} collective-permute-done((f32[4,4,80,256]{3,2,1,0:T(8,128)S(1)}, f32[4,4,80,256]{3,2,1,0:T(8,128)S(1)}, u32[]{:S(2)}, u32[]{:S(2)}) %collective-permute-start.14) | collective-permute-done | bytes 1310752 | tf_op jit(solution)/shard_map/ppermute | solution.py:277
  77.5 14.9 %shard_map.60 = (f32[1024,512]{1,0:T(8,128)S(1)}, f32[4,128,128]{2,1,0:T(8,128)S(1)}) custom-call(f32[4,4,80,256]{3,2,1,0:T(8,128)S(1)} %pad_maximum_fusion.own_ref, f32[4,4,80,256]{3,2,1,0:T(8,128)S(1)} %collective-permute-done.14.other_ref), custom_call_target="tpu_custom_call" | custom-call | flops 2500000000 | bytes 8388608 | tf_op jit(solution)/shard_map/pallas_call | solution.py:240
  92.5 14.0 %shard_map.61 = (f32[512,512]{1,0:T(8,128)S(1)}, f32[4,128,128]{2,1,0:T(8,128)S(1)}) custom-call(f32[4,4,80,256]{3,2,1,0:T(8,128)S(1)} %pad_maximum_fusion.own_ref, f32[4,4,80,256]{3,2,1,0:T(8,128)S(1)} %collective-permute-done.14.other_ref, f32[1024,512]{1,0:T(8,128)S(1)} %get-tuple-element.14.f0_ref), custom_call_target="tpu_custom_call" | custom-call | flops 2500000000 | bytes 8388608 | tf_op jit(solution)/shard_map/pallas_call | solution.py:240
  106.6 1.0 copy-done.1
  108.6 1.6 %copy-done = f32[512,1024]{1,0:T(8,128)S(1)} copy-done((f32[512,1024]{1,0:T(8,128)S(1)}, f32[512,1024]{1,0:T(8,128)}, u32[]{:S(2)}) %copy-start) | copy-done | bytes 2097176
  110.2 1.2 copy-done.2
  112.4 6.3 %shard_map.62 = (f32[512,1024]{1,0:T(8,128)}, f32[4,256,256]{2,1,0:T(8,128)S(1)}) custom-call(s32[64]{0:T(128)S(1)} %copy-done.8, f32[1024,512]{1,0:T(8,128)S(1)} %get-tuple-element.14.f0_ref, f32[512,512]{1,0:T(8,128)S(1)} %copy-done.2, f32[4,128,128]{2,1,0:T(8,128)S(1)} %get-tuple-element.16.d0_ref, f32[4,128,128]{2,1,0:T(8,128)S(1)} %copy-done.7, ...), custom_call_target="tpu_custom_call" | custom-call | flops 100000000 | bytes 8388608 | tf_op jit(solution)/shard_map/pallas_call | solution.py:240
  118.8 1.6 %copy-done.4 = f32[512,1024]{1,0:T(8,128)S(1)} copy-done((f32[512,1024]{1,0:T(8,128)S(1)}, f32[512,1024]{1,0:T(8,128)}, u32[]{:S(2)}) %copy-start.4) | copy-done | bytes 2097176
  120.3 7.4 %shard_map.63 = f32[512,512]{1,0:T(8,128)} custom-call(s32[64]{0:T(128)S(1)} %copy-done.8, s32[4]{0:T(128)S(1)} %copy-done.9, f32[32,8,1024]{2,1,0:T(8,128)S(1)} %all-to-all-done.2.own_ref, f32[32,8,1024]{2,1,0:T(8,128)S(1)} %collective-permute-done.15.other_ref, f32[1024,512]{1,0:T(8,128)S(1)} %get-tuple-element.14.f0_ref, f32[512,512]{1,0:T(8,128)S(1)} %copy-done.3, ...), custom_call_target="tpu_custom_call" | custom-call | flops 1000000000 | bytes 8388608 | tf_op jit(solution)/shard_map/pallas_call | solution.py:240
  (50 shorter events, 5.8 us)
Async XLA Ops:
  1.7 15.6 %collective-permute-start = (f32[4,16,512]{2,1,0:T(8,128)S(1)}, f32[4,16,512]{2,1,0:T(8,128)S(1)}, u32[]{:S(2)}, u32[]{:S(2)}) collective-permute-start(f32[4,16,512]{2,1,0:T(8,128)S(1)} %slice.71), channel_id=1, source_target_pairs={{4,0},{5,1},{6,2},{7,3}} | collective-permute-start | bytes 393224 | tf_op jit(solution)/shard_map/ppermute | solution.py:328
  8.8 33.6 %all-to-all-start = ((f32[64,8,256]{2,1,0:T(8,128)}), f32[64,8,256]{2,1,0:T(8,128)S(1)}, u32[]{:S(2)}, u32[]{:S(2)}) async-start(f32[64,8,256]{2,1,0:T(8,128)} %dynamic-slice_bitcast_fusion), calls=%async_computation | async-start | bytes 1048576 | tf_op jit(solution)/shard_map/all_to_all | solution.py:322
  17.4 8.1 %collective-permute-start.2 = (f32[80,256]{1,0:T(8,128)S(1)}, f32[80,256]{1,0:T(8,128)S(1)}, u32[]{:S(2)}, u32[]{:S(2)}) collective-permute-start(f32[80,256]{1,0:T(8,128)S(1)} %get-tuple-element.24), channel_id=1, source_target_pairs={{0,128},{4,132},{1,129},{5,133},{2,130},{6,134},{3,131},{7,135}} | collective-permute-start | bytes 245768 | tf_op jit(solution)/shard_map/ppermute | solution.py:277
  22.3 3.4 %collective-permute-start.3 = (f32[80,256]{1,0:T(8,128)S(1)}, f32[80,256]{1,0:T(8,128)S(1)}, u32[]{:S(2)}, u32[]{:S(2)}) collective-permute-start(f32[80,256]{1,0:T(8,128)S(1)} %get-tuple-element.25), channel_id=1, source_target_pairs={{0,192},{4,196},{1,193},{5,197},{2,194},{6,198},{3,195},{7,199}} | collective-permute-start | bytes 245768 | tf_op jit(solution)/shard_map/ppermute | solution.py:277
  23.6 5.3 %collective-permute-start.1 = (f32[80,256]{1,0:T(8,128)S(1)}, f32[80,256]{1,0:T(8,128)S(1)}, u32[]{:S(2)}, u32[]{:S(2)}) collective-permute-start(f32[80,256]{1,0:T(8,128)S(1)} %get-tuple-element.26), channel_id=1, source_target_pairs={{0,64},{4,68},{1,65},{5,69},{2,66},{6,70},{3,67},{7,71}} | collective-permute-start | bytes 245768 | tf_op jit(solution)/shard_map/ppermute | solution.py:277
  28.9 3.9 %collective-permute-start.6 = (f32[80,256]{1,0:T(8,128)S(1)}, f32[80,256]{1,0:T(8,128)S(1)}, u32[]{:S(2)}, u32[]{:S(2)}) collective-permute-start(f32[80,256]{1,0:T(8,128)S(1)} %fusion.1), channel_id=1, source_target_pairs={{0,48},{4,52},{64,112},{68,116},{128,176},{132,180},{192,240},{196... | collective-permute-start | bytes 245768 | tf_op jit(solution)/shard_map/ppermute | solution.py:277
  30.2 2.8 %collective-permute-start.5 = (f32[80,256]{1,0:T(8,128)S(1)}, f32[80,256]{1,0:T(8,128)S(1)}, u32[]{:S(2)}, u32[]{:S(2)}) collective-permute-start(f32[80,256]{1,0:T(8,128)S(1)} %fusion.1), channel_id=1, source_target_pairs={{0,32},{4,36},{64,96},{68,100},{128,160},{132,164},{192,224},{196,... | collective-permute-start | bytes 245768 | tf_op jit(solution)/shard_map/ppermute | solution.py:277
  31.5 3.4 %collective-permute-start.4 = (f32[80,256]{1,0:T(8,128)S(1)}, f32[80,256]{1,0:T(8,128)S(1)}, u32[]{:S(2)}, u32[]{:S(2)}) collective-permute-start(f32[80,256]{1,0:T(8,128)S(1)} %fusion.1), channel_id=1, source_target_pairs={{0,16},{4,20},{64,80},{68,84},{128,144},{132,148},{192,208},{196,2... | collective-permute-start | bytes 245768 | tf_op jit(solution)/shard_map/ppermute | solution.py:277
  35.0 2.8 %collective-permute-start.7 = (f32[80,256]{1,0:T(8,128)S(1)}, f32[80,256]{1,0:T(8,128)S(1)}, u32[]{:S(2)}, u32[]{:S(2)}) collective-permute-start(f32[80,256]{1,0:T(8,128)S(1)} %add_add_fusion), channel_id=1, source_target_pairs={{0,8},{4,12},{16,24},{20,28},{32,40},{36,44},{48,56},{52,60},{64,7... | collective-permute-start | bytes 245768 | tf_op jit(solution)/shard_map/ppermute | solution.py:277
  37.8 12.8 %collective-permute-start.10 = (f32[80,256]{1,0:T(8,128)S(1)}, f32[80,256]{1,0:T(8,128)S(1)}, u32[]{:S(2)}, u32[]{:S(2)}) collective-permute-start(f32[80,256]{1,0:T(8,128)S(1)} %add.55), channel_id=1, source_target_pairs={{0,192},{4,196},{8,200},{12,204},{16,208},{20,212},{24,216},{28,22... | collective-permute-start | bytes 245768 | tf_op jit(solution)/shard_map/ppermute | solution.py:277
  38.6 12.0 %collective-permute-start.9 = (f32[80,256]{1,0:T(8,128)S(1)}, f32[80,256]{1,0:T(8,128)S(1)}, u32[]{:S(2)}, u32[]{:S(2)}) collective-permute-start(f32[80,256]{1,0:T(8,128)S(1)} %add.55), channel_id=1, source_target_pairs={{0,128},{4,132},{8,136},{12,140},{16,144},{20,148},{24,152},{28,15... | collective-permute-start | bytes 245768 | tf_op jit(solution)/shard_map/ppermute | solution.py:277
  42.3 8.3 %collective-permute-start.8 = (f32[80,256]{1,0:T(8,128)S(1)}, f32[80,256]{1,0:T(8,128)S(1)}, u32[]{:S(2)}, u32[]{:S(2)}) collective-permute-start(f32[80,256]{1,0:T(8,128)S(1)} %add.55), channel_id=1, source_target_pairs={{0,64},{4,68},{8,72},{12,76},{16,80},{20,84},{24,88},{28,92},{32,9... | collective-permute-start | bytes 245768 | tf_op jit(solution)/shard_map/ppermute | solution.py:277
  42.3 0.8 copy-start.10
  46.4 8.5 %all-to-all-start.1 = ((f32[4,8,256]{2,1,0:T(8,128)}), f32[4,8,256]{2,1,0:T(8,128)S(1)}, u32[]{:S(2)}, u32[]{:S(2)}) async-start(f32[4,8,256]{2,1,0:T(8,128)} %shard_map.59), calls=%async_computation.1 | async-start | bytes 65536 | tf_op jit(solution)/shard_map/all_to_all | solution.py:336
  54.9 11.9 %collective-permute-start.13 = (f32[4,80,256]{2,1,0:T(8,128)S(1)}, f32[4,80,256]{2,1,0:T(8,128)S(1)}, u32[]{:S(2)}, u32[]{:S(2)}) collective-permute-start(f32[4,80,256]{2,1,0:T(8,128)S(1)} %pad_maximum_fusion.1), channel_id=1, source_target_pairs={{0,3},{1,0},{2,1},{3,2},{4,7},{5,4},{6,5},{7,6},{8,11},{9,8},{10,9... | collective-permute-start | bytes 983048 | tf_op jit(solution)/shard_map/ppermute | solution.py:309
  55.9 11.0 %collective-permute-start.12 = (f32[4,80,256]{2,1,0:T(8,128)S(1)}, f32[4,80,256]{2,1,0:T(8,128)S(1)}, u32[]{:S(2)}, u32[]{:S(2)}) collective-permute-start(f32[4,80,256]{2,1,0:T(8,128)S(1)} %pad_maximum_fusion.1), channel_id=1, source_target_pairs={{0,2},{1,3},{2,0},{3,1},{4,6},{5,7},{6,4},{7,5},{8,10},{9,11},{10,... | collective-permute-start | bytes 983048 | tf_op jit(solution)/shard_map/ppermute | solution.py:309
  57.0 15.3 %collective-permute-start.11 = (f32[4,80,256]{2,1,0:T(8,128)S(1)}, f32[4,80,256]{2,1,0:T(8,128)S(1)}, u32[]{:S(2)}, u32[]{:S(2)}) collective-permute-start(f32[4,80,256]{2,1,0:T(8,128)S(1)} %pad_maximum_fusion.1), channel_id=1, source_target_pairs={{0,1},{1,2},{2,3},{3,0},{4,5},{5,6},{6,7},{7,4},{8,9},{9,10},{10,1... | collective-permute-start | bytes 983048 | tf_op jit(solution)/shard_map/ppermute | solution.py:309
  58.1 50.1 %all-to-all-start.2 = ((f32[32,8,1024]{2,1,0:T(8,128)}), f32[32,8,1024]{2,1,0:T(8,128)S(1)}, u32[]{:S(2)}, u32[]{:S(2)}) async-start(f32[32,8,1024]{2,1,0:T(8,128)} %broadcast_in_dim.8), calls=%async_computation.2 | async-start | bytes 2097152 | tf_op jit(solution)/shard_map/all_to_all | solution.py:340
  72.5 5.1 %collective-permute-start.14 = (f32[4,4,80,256]{3,2,1,0:T(8,128)S(1)}, f32[4,4,80,256]{3,2,1,0:T(8,128)S(1)}, u32[]{:S(2)}, u32[]{:S(2)}) collective-permute-start(f32[4,4,80,256]{3,2,1,0:T(8,128)S(1)} %pad_maximum_fusion.own_ref), channel_id=1, source_target_pairs={{0,4},{4,0},{8,12},{12,8},{16,20},{20,16},{24,28},{28,24},{32,36},... | collective-permute-start | bytes 3932168 | tf_op jit(solution)/shard_map/ppermute | solution.py:277
  92.5 16.1 %copy-start.8 = (s32[64]{0:T(128)S(1)}, s32[64]{0:T(128)}, u32[]{:S(2)}) copy-start(s32[64]{0:T(128)} %live_ref.3) | copy-start | bytes 772
  106.6 1.0 copy-start.1
  107.5 0.7 copy-start.6
  108.2 10.5 %collective-permute-start.15 = (f32[32,8,1024]{2,1,0:T(8,128)S(1)}, f32[32,8,1024]{2,1,0:T(8,128)S(1)}, u32[]{:S(2)}, u32[]{:S(2)}) collective-permute-start(f32[32,8,1024]{2,1,0:T(8,128)S(1)} %all-to-all-done.2.own_ref), channel_id=1, source_target_pairs={{0,4},{4,0},{8,12},{12,8},{16,20},{20,16},{24,28},{28,24},{32,36},... | collective-permute-start | bytes 3145736 | tf_op jit(solution)/shard_map/ppermute | solution.py:277
  108.6 1.6 %copy-start = (f32[512,1024]{1,0:T(8,128)S(1)}, f32[512,1024]{1,0:T(8,128)}, u32[]{:S(2)}) copy-start(f32[512,1024]{1,0:T(8,128)} %panel_ref.1) | copy-start | bytes 6291460
  110.2 1.2 copy-start.2
  111.4 0.9 copy-start.7
  112.4 6.4 %copy-start.3 = (f32[512,512]{1,0:T(8,128)S(1)}, f32[512,512]{1,0:T(8,128)}, u32[]{:S(2)}) copy-start(f32[512,512]{1,0:T(8,128)} %copy-done.1) | copy-start | bytes 3145732
  112.4 6.4 %copy-start.5 = (f32[512,512]{1,0:T(8,128)S(1)}, f32[512,512]{1,0:T(8,128)}, u32[]{:S(2)}) copy-start(f32[512,512]{1,0:T(8,128)} %window_ref.1) | copy-start | bytes 3145732
  112.4 6.4 %copy-start.9 = (s32[4]{0:T(128)S(1)}, s32[4]{0:T(128)}, u32[]{:S(2)}) copy-start(s32[4]{0:T(128)} %rows_ref.3) | copy-start | bytes 52
  118.7 1.6 %copy-start.4 = (f32[512,1024]{1,0:T(8,128)S(1)}, f32[512,1024]{1,0:T(8,128)}, u32[]{:S(2)}) copy-start(f32[512,1024]{1,0:T(8,128)} %get-tuple-element.10.factor_ref) | copy-start | bytes 6291460

commit v4 on v3

--- a/solution.py
+++ b/solution.py
@@ -228,8 +228,25 @@
     out_ref[...] = window_ref[...] - mul_t(factor_ref[...], s_ref[...])
 
 
-def kernel_pick(rows_ref, parts_ref, out_ref):
-    out_ref[...] = parts_ref[...]
+def kernel_pick(rows_ref, parts_ref, out_ref, sems):
+    y = lax.axis_index("cols")
+    copies = [
+        pltpu.make_async_copy(parts_ref.at[rows_ref[lax.rem(y + d, NY)]], out_ref.at[d], sems.at[d]) for d in range(NY)
+    ]
+    for c in copies:
+        c.start()
+    for c in copies:
+        c.wait()
+
+
+def kernel_fan(q0_ref, q1_ref, q2_ref, q3_ref, out_ref):
+    y = lax.axis_index("cols")
+    width = q0_ref.shape[1]
+    for d, q_ref in enumerate((q0_ref, q1_ref, q2_ref, q3_ref)):
+        at = pl.ds(pl.multiple_of(lax.rem(y - d + NY, NY) * width, width), width)
+        value = q_ref[...]
+        for j in range(out_ref.shape[0]):
+            out_ref[j, :, at] = value
 
 
 SMEM = pl.BlockSpec(memory_space=pltpu.SMEM)
@@ -249,16 +266,13 @@
 
 
 def pick(window_rows, parts):
-    block = (1,) + parts.shape[1:]
     return pl.pallas_call(
         kernel_pick,
         out_shape=jax.ShapeDtypeStruct((NY,) + parts.shape[1:], F32),
-        grid_spec=pltpu.PrefetchScalarGridSpec(
-            num_scalar_prefetch=1,
-            grid=(NY,),
-            in_specs=[pl.BlockSpec(block, lambda i, rows: (rows[i], 0, 0))],
-            out_specs=pl.BlockSpec(block, lambda i, rows: (i, 0, 0)),
-        ),
+        in_specs=[SMEM, pl.BlockSpec(memory_space=pl.ANY)],
+        out_specs=VM,
+        scratch_shapes=[pltpu.SemaphoreType.DMA((NY,))],
+        compiler_params=pltpu.CompilerParams(vmem_limit_bytes=56 << 20),
     )(window_rows, parts)
 
 
@@ -301,12 +315,17 @@
     piece = jnp.where(root, v[0], 0.0)
     piece = piece + sum(by_x(v[d], d, lambda x, z, c: x == 0 and z == 0) for d in range(1, NX))
     piece = piece + sum(by_z(piece, d, lambda x, z, c: z == 0) for d in (2, 4, 6))
+    even = piece
     piece = piece + by_z(piece, 1, lambda x, z, c: z % 2 == 0)
-    return piece, jnp.stack([piece] + [by_x(piece, d) for d in range(1, NX)])
+    return even, jnp.stack([piece] + [by_x(piece, d) for d in range(1, NX)])
+
+
+def by_y(v, d):
+    return lax.ppermute(v, "cols", [(i, (i + d) % NY) for i in range(NY)])
 
 
 def gather_y(v):
-    return jnp.stack([v] + [lax.ppermute(v, "cols", [(i, (i + d) % NY) for i in range(NY)]) for d in range(1, NY)])
+    return jnp.stack([v] + [by_y(v, d) for d in range(1, NY)])
 
 
 def after(value, *others):
@@ -331,22 +350,22 @@
     stack = jnp.concatenate([jnp.where(core == 0, f, s) for f, s in zip(first, second)], axis=1)
     piece, part = spread_static(stack, x, z)
 
-    parts = after(parts, piece)
-    chosen = pick(window_rows, parts)
-    quarters = lax.all_to_all(chosen, "cols", 0, 0)
-    shard = jnp.concatenate([quarters[q] for q in range(NY)], axis=1)
-    own = gather_y(after(part, shard))
+    chosen = pick(window_rows, after(parts, piece))
+    quarters = [chosen[0]] + [by_y(chosen[d], d) for d in range(1, NY)]
+    own = gather_y(after(part, *quarters[1:]))
     other = swap_core(own)
-    t_own = lax.all_to_all(jnp.broadcast_to(after(shard, part), (32,) + shard.shape), "rows", 0, 0, axis_index_groups=GROUPS)
+    quarters = after(quarters, part)
+    (fan,) = call(kernel_fan, 10**6, 8, [(NX * NZ, 8, 2 * B)], [], *quarters)
+    t_own = lax.all_to_all(fan, "rows", 0, 0, axis_index_groups=GROUPS)
 
     f0, d0 = call(kernel_a, 25 * 10**8, 24, [(2 * B, B), (4, NB, NB)], [(2, 5 * H, H), (2 * B, B), (NB, NB)], own, other)
     f1, d1 = call(kernel_b, 25 * 10**8, 20, [(B, B), (4, NB, NB)], [(2, 5 * H, H), (B, B), (NB, NB)], own, other, f0)
     t_other = swap_core(after(t_own, f1))
     factor, inv = call(
-        kernel_own, 10**8, 28, [(B, 2 * B), (4, H, H)], [], row_live, f0, f1, d0, d1, panel
+        kernel_own, 10**8, 58, [(B, 2 * B), (4, H, H)], [], row_live, f0, f1, d0, d1, panel
     )
     (updated,) = call(
-        kernel_window, 10**9, 32, [(B, B)], [(B, 2 * B)],
+        kernel_window, 10**8, 58, [(B, B)], [(B, 2 * B)],
         row_live, window_rows, t_own, t_other, f0, f1, inv, factor, window_block,
     )
     return factor, updated

time: 129 us -> 130 us (level)
  Pallas kernels: 46 us -> 51.5 us
  local copies, waits for them, and re-layouts: 11.9 us -> 7.89 us
  waiting for transfers between devices: 20 us -> 18.2 us
  starting transfers between devices: 48.7 us -> 50.5 us
    pallas_call x4 -> x5, Pallas kernels: 42.7 us -> 49.4 us  [call(): pl.pallas_call(kernel, out_shape=[jax.ShapeDtypeStruct(s, F32) for s in o...]
    all_to_all x2 -> x1, starting transfers between devices: 12.9 us -> 8.38 us  [shards(): t_own = lax.all_to_all(fan, 'rows', 0, 0, axis_index_groups=GROUPS)]
    all_to_all x2 -> x1, waiting for transfers between devices: 4.25 us -> 0.01 us  [shards(): t_own = lax.all_to_all(fan, 'rows', 0, 0, axis_index_groups=GROUPS)]
    ppermute x3 -> x6, starting transfers between devices: 2.14 us -> 6.31 us  [by_y(): return lax.ppermute(v, 'cols', [(i, (i + d) % NY) for i in range(NY)])]
    unnamed x23 -> x15, local copies, waits for them, and re-layouts: 7.83 us -> 4.17 us
    ppermute x3 -> x6, waiting for transfers between devices: 5.52 us -> 7.97 us  [by_y(): return lax.ppermute(v, 'cols', [(i, (i + d) % NY) for i in range(NY)])]
    ppermute x12, starting transfers between devices: 20 us -> 22.2 us  [move(): return lax.ppermute(v, 'rows', pairs)]
  transfers between devices with their start and end apart: 19 -> 21, of which waited for: 9 -> 10; matrix products, arithmetic and copies ran while one was open for 3% -> 2% of each run, Pallas kernels for 30% -> 32%
where the time goes in v4:
time: 130 us; the launch traced here: 129 us
  Pallas kernels  51.5 us (40%)
  starting transfers between devices  50.5 us (39%)
  waiting for transfers between devices  18.2 us (14%)
  local copies, waits for them, and re-layouts  7.89 us (6%)
    pallas_call x5, Pallas kernels, call(): pl.pallas_call(kernel, out_shape=[jax.ShapeDtypeStruct(s, F32) for s in o...  49.4 us
    ppermute x12, starting transfers between devices, move(): return lax.ppermute(v, 'rows', pairs)  22.2 us
    ppermute x12, waiting for transfers between devices, move(): return lax.ppermute(v, 'rows', pairs)  10.2 us
    all_to_all x1, starting transfers between devices, shards(): parts = lax.all_to_all(mine, 'rows', 0, 0)  8.5 us
    all_to_all x1, starting transfers between devices, shards(): t_own = lax.all_to_all(fan, 'rows', 0, 0, axis_index_groups=GROUPS)  8.38 us
    ppermute x6, waiting for transfers between devices, by_y(): return lax.ppermute(v, 'cols', [(i, (i + d) % NY) for i in range(NY)])  7.97 us
    ppermute x6, starting transfers between devices, by_y(): return lax.ppermute(v, 'cols', [(i, (i + d) % NY) for i in range(NY)])  6.31 us
    ppermute x1, starting transfers between devices, shards(): low = lax.ppermute(bot[:, :, B:], 'rows', [(1, 0)])  5.15 us
  transfers between devices with their start and end apart: 21, of which 10 were waited for; matrix products, arithmetic and copies ran while one was open for 2% of the time, Pallas kernels for 32%

profile of v4, /device:TPU:1, one launch (start us, length us, event | category | flops | bytes accessed | tf_op | source)
XLA Modules:
  0.0 129.3 jit_solution(16197270768644175432)
XLA Ops:
  0.6 1.1 constant_dynamic-slice_fusion
  1.7 5.2 %collective-permute-start = (f32[4,16,512]{2,1,0:T(8,128)S(1)}, f32[4,16,512]{2,1,0:T(8,128)S(1)}, u32[]{:S(2)}, u32[]{:S(2)}) collective-permute-start(f32[4,16,512]{2,1,0:T(8,128)S(1)} %slice.71), channel_id=1, source_target_pairs={{4,0},{5,1},{6,2},{7,3}} | collective-permute-start | bytes 393224 | tf_op jit(solution)/shard_map/ppermute | solution.py:347
  6.9 1.9 %dynamic-slice_bitcast_fusion = f32[64,8,256]{2,1,0:T(8,128)} fusion(f32[512,1024]{1,0:T(8,128)} %panel_ref.1, s32[]{:T(128)S(6)} %select_n.74), kind=kLoop, calls=%fused_computation.1 | loop fusion | bytes 1048580 | tf_op jit(solution)/shard_map/reshape | solution.py:340
  8.8 8.5 %all-to-all-start = ((f32[64,8,256]{2,1,0:T(8,128)}), f32[64,8,256]{2,1,0:T(8,128)S(1)}, u32[]{:S(2)}, u32[]{:S(2)}) async-start(f32[64,8,256]{2,1,0:T(8,128)} %dynamic-slice_bitcast_fusion), calls=%async_computation | async-start | bytes 1048576 | tf_op jit(solution)/shard_map/all_to_all | solution.py:341
  17.4 4.9 %collective-permute-start.2 = (f32[80,256]{1,0:T(8,128)S(1)}, f32[80,256]{1,0:T(8,128)S(1)}, u32[]{:S(2)}, u32[]{:S(2)}) collective-permute-start(f32[80,256]{1,0:T(8,128)S(1)} %get-tuple-element.30), channel_id=1, source_target_pairs={{0,128},{4,132},{1,129},{5,133},{2,130},{6,134},{3,131},{7,135}} | collective-permute-start | bytes 245768 | tf_op jit(solution)/shard_map/ppermute | solution.py:291
  22.3 1.3 %collective-permute-start.3 = (f32[80,256]{1,0:T(8,128)S(1)}, f32[80,256]{1,0:T(8,128)S(1)}, u32[]{:S(2)}, u32[]{:S(2)}) collective-permute-start(f32[80,256]{1,0:T(8,128)S(1)} %get-tuple-element.31), channel_id=1, source_target_pairs={{0,192},{4,196},{1,193},{5,197},{2,194},{6,198},{3,195},{7,199}} | collective-permute-start | bytes 245768 | tf_op jit(solution)/shard_map/ppermute | solution.py:291
  23.6 1.3 %collective-permute-start.1 = (f32[80,256]{1,0:T(8,128)S(1)}, f32[80,256]{1,0:T(8,128)S(1)}, u32[]{:S(2)}, u32[]{:S(2)}) collective-permute-start(f32[80,256]{1,0:T(8,128)S(1)} %get-tuple-element.32), channel_id=1, source_target_pairs={{0,64},{4,68},{1,65},{5,69},{2,66},{6,70},{3,67},{7,71}} | collective-permute-start | bytes 245768 | tf_op jit(solution)/shard_map/ppermute | solution.py:291
  25.7 3.2 %collective-permute-done.1 = f32[80,256]{1,0:T(8,128)S(1)} collective-permute-done((f32[80,256]{1,0:T(8,128)S(1)}, f32[80,256]{1,0:T(8,128)S(1)}, u32[]{:S(2)}, u32[]{:S(2)}) %collective-permute-start.1) | collective-permute-done | bytes 81952 | tf_op jit(solution)/shard_map/ppermute | solution.py:291
  28.9 1.3 %collective-permute-start.6 = (f32[80,256]{1,0:T(8,128)S(1)}, f32[80,256]{1,0:T(8,128)S(1)}, u32[]{:S(2)}, u32[]{:S(2)}) collective-permute-start(f32[80,256]{1,0:T(8,128)S(1)} %fusion.1), channel_id=1, source_target_pairs={{0,48},{4,52},{64,112},{68,116},{128,176},{132,180},{192,240},{196... | collective-permute-start | bytes 245768 | tf_op jit(solution)/shard_map/ppermute | solution.py:291
  30.2 1.3 %collective-permute-start.5 = (f32[80,256]{1,0:T(8,128)S(1)}, f32[80,256]{1,0:T(8,128)S(1)}, u32[]{:S(2)}, u32[]{:S(2)}) collective-permute-start(f32[80,256]{1,0:T(8,128)S(1)} %fusion.1), channel_id=1, source_target_pairs={{0,32},{4,36},{64,96},{68,100},{128,160},{132,164},{192,224},{196,... | collective-permute-start | bytes 245768 | tf_op jit(solution)/shard_map/ppermute | solution.py:291
  31.5 1.3 %collective-permute-start.4 = (f32[80,256]{1,0:T(8,128)S(1)}, f32[80,256]{1,0:T(8,128)S(1)}, u32[]{:S(2)}, u32[]{:S(2)}) collective-permute-start(f32[80,256]{1,0:T(8,128)S(1)} %fusion.1), channel_id=1, source_target_pairs={{0,16},{4,20},{64,80},{68,84},{128,144},{132,148},{192,208},{196,2... | collective-permute-start | bytes 245768 | tf_op jit(solution)/shard_map/ppermute | solution.py:291
  33.0 2.0 %collective-permute-done.4 = f32[80,256]{1,0:T(8,128)S(1)} collective-permute-done((f32[80,256]{1,0:T(8,128)S(1)}, f32[80,256]{1,0:T(8,128)S(1)}, u32[]{:S(2)}, u32[]{:S(2)}) %collective-permute-start.4) | collective-permute-done | bytes 81952 | tf_op jit(solution)/shard_map/ppermute | solution.py:291
  35.0 1.3 %collective-permute-start.7 = (f32[80,256]{1,0:T(8,128)S(1)}, f32[80,256]{1,0:T(8,128)S(1)}, u32[]{:S(2)}, u32[]{:S(2)}) collective-permute-start(f32[80,256]{1,0:T(8,128)S(1)} %add_add_fusion), channel_id=1, source_target_pairs={{0,8},{4,12},{16,24},{20,28},{32,40},{36,44},{48,56},{52,60},{64,7... | collective-permute-start | bytes 245768 | tf_op jit(solution)/shard_map/ppermute | solution.py:291
  36.3 1.5 %collective-permute-done.7 = f32[80,256]{1,0:T(8,128)S(1)} collective-permute-done((f32[80,256]{1,0:T(8,128)S(1)}, f32[80,256]{1,0:T(8,128)S(1)}, u32[]{:S(2)}, u32[]{:S(2)}) %collective-permute-start.7) | collective-permute-done | bytes 81952 | tf_op jit(solution)/shard_map/ppermute | solution.py:291
  37.8 0.9 collective-permute-start.10
  38.6 3.7 %collective-permute-start.9 = (f32[80,256]{1,0:T(8,128)S(1)}, f32[80,256]{1,0:T(8,128)S(1)}, u32[]{:S(2)}, u32[]{:S(2)}) collective-permute-start(f32[80,256]{1,0:T(8,128)S(1)} %add.55), channel_id=1, source_target_pairs={{0,128},{4,132},{8,136},{12,140},{16,144},{20,148},{24,152},{28,15... | collective-permute-start | bytes 245768 | tf_op jit(solution)/shard_map/ppermute | solution.py:291
  43.1 2.1 %shard_map.59 = f32[4,8,256]{2,1,0:T(8,128)} custom-call(s32[4]{0:T(128)} %rows_ref.3, f32[64,8,256]{2,1,0:T(8,128)} %copy-done.5), custom_call_target="tpu_custom_call" | custom-call | tf_op jit(solution)/shard_map/pallas_call | solution.py:269
  46.0 2.7 %collective-permute-start.13 = (f32[8,256]{1,0:T(8,128)S(1)}, f32[8,256]{1,0:T(8,128)S(1)}, u32[]{:S(2)}, u32[]{:S(2)}) collective-permute-start(f32[8,256]{1,0:T(8,128)S(1)} %get-tuple-element.34), channel_id=1, source_target_pairs={{0,3},{1,0},{2,1},{3,2},{4,7},{5,4},{6,5},{7,6},{8,11},{9,8},{10,9... | collective-permute-start | bytes 24584 | tf_op jit(solution)/shard_map/ppermute | solution.py:324
  49.8 2.9 %collective-permute-done.12.q2_ref = f32[8,256]{1,0:T(8,128)S(1)} collective-permute-done((f32[8,256]{1,0:T(8,128)S(1)}, f32[8,256]{1,0:T(8,128)S(1)}, u32[]{:S(2)}, u32[]{:S(2)}) %collective-permute-start.12) | collective-permute-done | bytes 8224 | tf_op jit(solution)/shard_map/ppermute | solution.py:324
  53.2 1.3 %collective-permute-start.15 = (f32[4,80,256]{2,1,0:T(8,128)S(1)}, f32[4,80,256]{2,1,0:T(8,128)S(1)}, u32[]{:S(2)}, u32[]{:S(2)}) collective-permute-start(f32[4,80,256]{2,1,0:T(8,128)S(1)} %pad_maximum_fusion.1), channel_id=1, source_target_pairs={{0,2},{1,3},{2,0},{3,1},{4,6},{5,7},{6,4},{7,5},{8,10},{9,11},{10,... | collective-permute-start | bytes 983048 | tf_op jit(solution)/shard_map/ppermute | solution.py:324
  54.5 0.9 collective-permute-start.14
  55.3 1.0 shard_map.63
  56.4 8.4 %all-to-all-start.1 = ((f32[32,8,1024]{2,1,0:T(8,128)}), f32[32,8,1024]{2,1,0:T(8,128)S(1)}, u32[]{:S(2)}, u32[]{:S(2)}) async-start(f32[32,8,1024]{2,1,0:T(8,128)} %shard_map.63), calls=%async_computation.1 | async-start | bytes 2097152 | tf_op jit(solution)/shard_map/all_to_all | solution.py:359
  64.8 5.0 %collective-permute-done.14 = f32[4,80,256]{2,1,0:T(8,128)S(1)} collective-permute-done((f32[4,80,256]{2,1,0:T(8,128)S(1)}, f32[4,80,256]{2,1,0:T(8,128)S(1)}, u32[]{:S(2)}, u32[]{:S(2)}) %collective-permute-start.14) | collective-permute-done | bytes 327712 | tf_op jit(solution)/shard_map/ppermute | solution.py:324
  69.9 4.6 %collective-permute-start.17 = (f32[4,4,80,256]{3,2,1,0:T(8,128)S(1)}, f32[4,4,80,256]{3,2,1,0:T(8,128)S(1)}, u32[]{:S(2)}, u32[]{:S(2)}) collective-permute-start(f32[4,4,80,256]{3,2,1,0:T(8,128)S(1)} %pad_maximum_fusion.own_ref), channel_id=1, source_target_pairs={{0,4},{4,0},{8,12},{12,8},{16,20},{20,16},{24,28},{28,24},{32,36},... | collective-permute-start | bytes 3932168 | tf_op jit(solution)/shard_map/ppermute | solution.py:291
  74.4 2.7 %collective-permute-done.17.other_ref = f32[4,4,80,256]{3,2,1,0:T(8,128)S(1)} collective-permute-done((f32[4,4,80,256]{3,2,1,0:T(8,128)S(1)}, f32[4,4,80,256]{3,2,1,0:T(8,128)S(1)}, u32[]{:S(2)}, u32[]{:S(2)}) %collective-permute-start.17) | collective-permute-done | bytes 1310752 | tf_op jit(solution)/shard_map/ppermute | solution.py:291
  77.1 14.9 %shard_map.60 = (f32[1024,512]{1,0:T(8,128)S(1)}, f32[4,128,128]{2,1,0:T(8,128)S(1)}) custom-call(f32[4,4,80,256]{3,2,1,0:T(8,128)S(1)} %pad_maximum_fusion.own_ref, f32[4,4,80,256]{3,2,1,0:T(8,128)S(1)} %collective-permute-done.17.other_ref), custom_call_target="tpu_custom_call" | custom-call | flops 2500000000 | bytes 8388608 | tf_op jit(solution)/shard_map/pallas_call | solution.py:257
  92.7 14.0 %shard_map.61 = (f32[512,512]{1,0:T(8,128)S(1)}, f32[4,128,128]{2,1,0:T(8,128)S(1)}) custom-call(f32[4,4,80,256]{3,2,1,0:T(8,128)S(1)} %pad_maximum_fusion.own_ref, f32[4,4,80,256]{3,2,1,0:T(8,128)S(1)} %collective-permute-done.17.other_ref, f32[1024,512]{1,0:T(8,128)S(1)} %get-tuple-element.17.f0_ref), custom_call_target="tpu_custom_call" | custom-call | flops 2500000000 | bytes 8388608 | tf_op jit(solution)/shard_map/pallas_call | solution.py:257
  106.8 1.0 copy-done.1
  108.9 8.9 %shard_map.62 = (f32[512,1024]{1,0:T(8,128)}, f32[4,256,256]{2,1,0:T(8,128)}) custom-call(s32[64]{0:T(128)} %live_ref.3, f32[1024,512]{1,0:T(8,128)} %copy-done, f32[512,512]{1,0:T(8,128)} %copy-done.1, f32[4,128,128]{2,1,0:T(8,128)} %copy-done.2, f32[4,128,128]{2,1,0:T(8,128)} %copy-done.3, f32[512,1024]{1,0:T(8,128)} %panel_ref.1), custom_call_target="tpu_custom_call" | custom-call | flops 100000000 | bytes 8388608 | tf_op jit(solution)/shard_map/pallas_call | solution.py:257
  117.8 1.0 copy-done.6
  118.8 10.5 %shard_map.64 = f32[512,512]{1,0:T(8,128)} custom-call(s32[64]{0:T(128)} %live_ref.3, s32[4]{0:T(128)} %rows_ref.3, f32[32,8,1024]{2,1,0:T(8,128)} %copy-done.4, f32[32,8,1024]{2,1,0:T(8,128)} %copy-done.6, f32[1024,512]{1,0:T(8,128)} %copy-done, f32[512,512]{1,0:T(8,128)} %copy-done.1, f32[4,256,256]{2,1,0:T(8,128)} %get-tuple-element.27.inv_ref, ...), custom_call_target="tpu_custom_call" | custom-call | flops 100000000 | bytes 8388608 | tf_op jit(solution)/shard_map/pallas_call | solution.py:257
  (45 shorter events, 6.0 us)
Async XLA Ops:
  1.7 15.6 %collective-permute-start = (f32[4,16,512]{2,1,0:T(8,128)S(1)}, f32[4,16,512]{2,1,0:T(8,128)S(1)}, u32[]{:S(2)}, u32[]{:S(2)}) collective-permute-start(f32[4,16,512]{2,1,0:T(8,128)S(1)} %slice.71), channel_id=1, source_target_pairs={{4,0},{5,1},{6,2},{7,3}} | collective-permute-start | bytes 393224 | tf_op jit(solution)/shard_map/ppermute | solution.py:347
  8.8 33.6 %all-to-all-start = ((f32[64,8,256]{2,1,0:T(8,128)}), f32[64,8,256]{2,1,0:T(8,128)S(1)}, u32[]{:S(2)}, u32[]{:S(2)}) async-start(f32[64,8,256]{2,1,0:T(8,128)} %dynamic-slice_bitcast_fusion), calls=%async_computation | async-start | bytes 1048576 | tf_op jit(solution)/shard_map/all_to_all | solution.py:341
  17.4 8.1 %collective-permute-start.2 = (f32[80,256]{1,0:T(8,128)S(1)}, f32[80,256]{1,0:T(8,128)S(1)}, u32[]{:S(2)}, u32[]{:S(2)}) collective-permute-start(f32[80,256]{1,0:T(8,128)S(1)} %get-tuple-element.30), channel_id=1, source_target_pairs={{0,128},{4,132},{1,129},{5,133},{2,130},{6,134},{3,131},{7,135}} | collective-permute-start | bytes 245768 | tf_op jit(solution)/shard_map/ppermute | solution.py:291
  22.3 3.4 %collective-permute-start.3 = (f32[80,256]{1,0:T(8,128)S(1)}, f32[80,256]{1,0:T(8,128)S(1)}, u32[]{:S(2)}, u32[]{:S(2)}) collective-permute-start(f32[80,256]{1,0:T(8,128)S(1)} %get-tuple-element.31), channel_id=1, source_target_pairs={{0,192},{4,196},{1,193},{5,197},{2,194},{6,198},{3,195},{7,199}} | collective-permute-start | bytes 245768 | tf_op jit(solution)/shard_map/ppermute | solution.py:291
  23.6 5.3 %collective-permute-start.1 = (f32[80,256]{1,0:T(8,128)S(1)}, f32[80,256]{1,0:T(8,128)S(1)}, u32[]{:S(2)}, u32[]{:S(2)}) collective-permute-start(f32[80,256]{1,0:T(8,128)S(1)} %get-tuple-element.32), channel_id=1, source_target_pairs={{0,64},{4,68},{1,65},{5,69},{2,66},{6,70},{3,67},{7,71}} | collective-permute-start | bytes 245768 | tf_op jit(solution)/shard_map/ppermute | solution.py:291
  28.9 3.9 %collective-permute-start.6 = (f32[80,256]{1,0:T(8,128)S(1)}, f32[80,256]{1,0:T(8,128)S(1)}, u32[]{:S(2)}, u32[]{:S(2)}) collective-permute-start(f32[80,256]{1,0:T(8,128)S(1)} %fusion.1), channel_id=1, source_target_pairs={{0,48},{4,52},{64,112},{68,116},{128,176},{132,180},{192,240},{196... | collective-permute-start | bytes 245768 | tf_op jit(solution)/shard_map/ppermute | solution.py:291
  30.2 2.8 %collective-permute-start.5 = (f32[80,256]{1,0:T(8,128)S(1)}, f32[80,256]{1,0:T(8,128)S(1)}, u32[]{:S(2)}, u32[]{:S(2)}) collective-permute-start(f32[80,256]{1,0:T(8,128)S(1)} %fusion.1), channel_id=1, source_target_pairs={{0,32},{4,36},{64,96},{68,100},{128,160},{132,164},{192,224},{196,... | collective-permute-start | bytes 245768 | tf_op jit(solution)/shard_map/ppermute | solution.py:291
  31.5 3.4 %collective-permute-start.4 = (f32[80,256]{1,0:T(8,128)S(1)}, f32[80,256]{1,0:T(8,128)S(1)}, u32[]{:S(2)}, u32[]{:S(2)}) collective-permute-start(f32[80,256]{1,0:T(8,128)S(1)} %fusion.1), channel_id=1, source_target_pairs={{0,16},{4,20},{64,80},{68,84},{128,144},{132,148},{192,208},{196,2... | collective-permute-start | bytes 245768 | tf_op jit(solution)/shard_map/ppermute | solution.py:291
  35.0 2.8 %collective-permute-start.7 = (f32[80,256]{1,0:T(8,128)S(1)}, f32[80,256]{1,0:T(8,128)S(1)}, u32[]{:S(2)}, u32[]{:S(2)}) collective-permute-start(f32[80,256]{1,0:T(8,128)S(1)} %add_add_fusion), channel_id=1, source_target_pairs={{0,8},{4,12},{16,24},{20,28},{32,40},{36,44},{48,56},{52,60},{64,7... | collective-permute-start | bytes 245768 | tf_op jit(solution)/shard_map/ppermute | solution.py:291
  37.8 11.3 %collective-permute-start.10 = (f32[80,256]{1,0:T(8,128)S(1)}, f32[80,256]{1,0:T(8,128)S(1)}, u32[]{:S(2)}, u32[]{:S(2)}) collective-permute-start(f32[80,256]{1,0:T(8,128)S(1)} %add.55), channel_id=1, source_target_pairs={{0,192},{4,196},{8,200},{12,204},{16,208},{20,212},{24,216},{28,22... | collective-permute-start | bytes 245768 | tf_op jit(solution)/shard_map/ppermute | solution.py:291
  38.6 11.1 %collective-permute-start.9 = (f32[80,256]{1,0:T(8,128)S(1)}, f32[80,256]{1,0:T(8,128)S(1)}, u32[]{:S(2)}, u32[]{:S(2)}) collective-permute-start(f32[80,256]{1,0:T(8,128)S(1)} %add.55), channel_id=1, source_target_pairs={{0,128},{4,132},{8,136},{12,140},{16,144},{20,148},{24,152},{28,15... | collective-permute-start | bytes 245768 | tf_op jit(solution)/shard_map/ppermute | solution.py:291
  42.3 7.4 %collective-permute-start.8 = (f32[80,256]{1,0:T(8,128)S(1)}, f32[80,256]{1,0:T(8,128)S(1)}, u32[]{:S(2)}, u32[]{:S(2)}) collective-permute-start(f32[80,256]{1,0:T(8,128)S(1)} %add.55), channel_id=1, source_target_pairs={{0,64},{4,68},{8,72},{12,76},{16,80},{20,84},{24,88},{28,92},{32,9... | collective-permute-start | bytes 245768 | tf_op jit(solution)/shard_map/ppermute | solution.py:291
  42.3 0.8 copy-start.5
  46.0 3.8 %collective-permute-start.13 = (f32[8,256]{1,0:T(8,128)S(1)}, f32[8,256]{1,0:T(8,128)S(1)}, u32[]{:S(2)}, u32[]{:S(2)}) collective-permute-start(f32[8,256]{1,0:T(8,128)S(1)} %get-tuple-element.34), channel_id=1, source_target_pairs={{0,3},{1,0},{2,1},{3,2},{4,7},{5,4},{6,5},{7,6},{8,11},{9,8},{10,9... | collective-permute-start | bytes 24584 | tf_op jit(solution)/shard_map/ppermute | solution.py:324
  48.7 4.0 %collective-permute-start.12 = (f32[8,256]{1,0:T(8,128)S(1)}, f32[8,256]{1,0:T(8,128)S(1)}, u32[]{:S(2)}, u32[]{:S(2)}) collective-permute-start(f32[8,256]{1,0:T(8,128)S(1)} %get-tuple-element.35), channel_id=1, source_target_pairs={{0,2},{1,3},{2,0},{3,1},{4,6},{5,7},{6,4},{7,5},{8,10},{9,11},{10,... | collective-permute-start | bytes 24584 | tf_op jit(solution)/shard_map/ppermute | solution.py:324
  49.1 3.7 %collective-permute-start.11 = (f32[8,256]{1,0:T(8,128)S(1)}, f32[8,256]{1,0:T(8,128)S(1)}, u32[]{:S(2)}, u32[]{:S(2)}) collective-permute-start(f32[8,256]{1,0:T(8,128)S(1)} %get-tuple-element.36), channel_id=1, source_target_pairs={{0,1},{1,2},{2,3},{3,0},{4,5},{5,6},{6,7},{7,4},{8,9},{9,10},{10,1... | collective-permute-start | bytes 24584 | tf_op jit(solution)/shard_map/ppermute | solution.py:324
  52.8 12.0 %collective-permute-start.16 = (f32[4,80,256]{2,1,0:T(8,128)S(1)}, f32[4,80,256]{2,1,0:T(8,128)S(1)}, u32[]{:S(2)}, u32[]{:S(2)}) collective-permute-start(f32[4,80,256]{2,1,0:T(8,128)S(1)} %pad_maximum_fusion.1), channel_id=1, source_target_pairs={{0,3},{1,0},{2,1},{3,2},{4,7},{5,4},{6,5},{7,6},{8,11},{9,8},{10,9... | collective-permute-start | bytes 983048 | tf_op jit(solution)/shard_map/ppermute | solution.py:324
  53.2 11.6 %collective-permute-start.15 = (f32[4,80,256]{2,1,0:T(8,128)S(1)}, f32[4,80,256]{2,1,0:T(8,128)S(1)}, u32[]{:S(2)}, u32[]{:S(2)}) collective-permute-start(f32[4,80,256]{2,1,0:T(8,128)S(1)} %pad_maximum_fusion.1), channel_id=1, source_target_pairs={{0,2},{1,3},{2,0},{3,1},{4,6},{5,7},{6,4},{7,5},{8,10},{9,11},{10,... | collective-permute-start | bytes 983048 | tf_op jit(solution)/shard_map/ppermute | solution.py:324
  54.5 15.3 %collective-permute-start.14 = (f32[4,80,256]{2,1,0:T(8,128)S(1)}, f32[4,80,256]{2,1,0:T(8,128)S(1)}, u32[]{:S(2)}, u32[]{:S(2)}) collective-permute-start(f32[4,80,256]{2,1,0:T(8,128)S(1)} %pad_maximum_fusion.1), channel_id=1, source_target_pairs={{0,1},{1,2},{2,3},{3,0},{4,5},{5,6},{6,7},{7,4},{8,9},{9,10},{10,1... | collective-permute-start | bytes 983048 | tf_op jit(solution)/shard_map/ppermute | solution.py:324
  56.4 52.1 %all-to-all-start.1 = ((f32[32,8,1024]{2,1,0:T(8,128)}), f32[32,8,1024]{2,1,0:T(8,128)S(1)}, u32[]{:S(2)}, u32[]{:S(2)}) async-start(f32[32,8,1024]{2,1,0:T(8,128)} %shard_map.63), calls=%async_computation.1 | async-start | bytes 2097152 | tf_op jit(solution)/shard_map/all_to_all | solution.py:359
  69.9 7.2 %collective-permute-start.17 = (f32[4,4,80,256]{3,2,1,0:T(8,128)S(1)}, f32[4,4,80,256]{3,2,1,0:T(8,128)S(1)}, u32[]{:S(2)}, u32[]{:S(2)}) collective-permute-start(f32[4,4,80,256]{3,2,1,0:T(8,128)S(1)} %pad_maximum_fusion.own_ref), channel_id=1, source_target_pairs={{0,4},{4,0},{8,12},{12,8},{16,20},{20,16},{24,28},{28,24},{32,36},... | collective-permute-start | bytes 3932168 | tf_op jit(solution)/shard_map/ppermute | solution.py:291
  92.0 0.7 copy-start.2
  92.7 14.1 %copy-start = (f32[1024,512]{1,0:T(8,128)}, f32[1024,512]{1,0:T(8,128)S(1)}, u32[]{:S(2)}) copy-start(f32[1024,512]{1,0:T(8,128)S(1)} %get-tuple-element.17.f0_ref) | copy-start | bytes 6291460
  106.8 1.0 copy-start.1
  107.8 0.7 copy-start.3
  108.5 9.3 %copy-start.4 = (f32[32,8,1024]{2,1,0:T(8,128)}, f32[32,8,1024]{2,1,0:T(8,128)S(1)}, u32[]{:S(2)}) copy-start(f32[32,8,1024]{2,1,0:T(8,128)S(1)} %all-to-all-done.1.own_ref) | copy-start | bytes 3145732
  108.5 9.3 %collective-permute-start.18 = (f32[32,8,1024]{2,1,0:T(8,128)S(1)}, f32[32,8,1024]{2,1,0:T(8,128)S(1)}, u32[]{:S(2)}, u32[]{:S(2)}) collective-permute-start(f32[32,8,1024]{2,1,0:T(8,128)S(1)} %all-to-all-done.1.own_ref), channel_id=1, source_target_pairs={{0,4},{4,0},{8,12},{12,8},{16,20},{20,16},{24,28},{28,24},{32,36},... | collective-permute-start | bytes 3145736 | tf_op jit(solution)/shard_map/ppermute | solution.py:291
  117.8 1.0 copy-start.6

commit v5 on v4

--- a/solution.py
+++ b/solution.py
@@ -11,6 +11,7 @@
 B = 512
 NB = 128
 H = B // 2
+COST = 25 * 10**8
 NX, NZ, NY = 4, 8, 4
 CONTRACT = (((1,), (1,)), ((), ()))
 
@@ -198,34 +199,33 @@
             s_ref[:, e:] = s_ref[:, e:] - mul_t(X, f_ref[p + H :, p : p + H])
 
 
-def kernel_own(live_ref, f0_ref, f1_ref, d0_ref, d1_ref, panel_ref, factor_ref, inv_ref):
+def kernel_c(live_ref, rows_ref, own_ref, other_ref, f0_ref, f1_ref, d0_ref, d1_ref, panel_ref, window_ref, factor_ref, out_ref, s_ref):
     row = lax.axis_index("rows")
+    _, y, mine = coords()
+    live_t = live_ref[rows_ref[y]].astype(F32)
     live = jnp.where(row < 2, 1, live_ref[row]).astype(F32)
-    factor_ref[...] = panel_ref[...] * live
+    s_ref[:B, :] = panel_ref[...] * live
+    for j in range(NX * NZ):
+        s_ref[pl.ds(pl.multiple_of(B + (2 * j + mine) * 8, 8), 8), :] = own_ref[j] * live_t
+        s_ref[pl.ds(pl.multiple_of(B + (2 * j + 1 - mine) * 8, 8), 8), :] = other_ref[j] * live_t
+    inv = []
     for k in range(4):
         f_ref, d_ref, p = (f0_ref, d0_ref, k * H) if k < 2 else (f1_ref, d1_ref, k * H - B)
-        inv_ref[k] = pair_inverse(d_ref, 2 * (k % 2), f_ref[p + NB : p + H, p : p + NB])
-    solve_rows(factor_ref, lambda k: inv_ref[k], f0_ref, f1_ref)
+        inv.append(pair_inverse(d_ref, 2 * (k % 2), f_ref[p + NB : p + H, p : p + NB]))
+    solve_rows(s_ref, lambda k: inv[k], f0_ref, f1_ref)
 
     @pl.when(row == 0)
     def _():
-        factor_ref[:, :B] = f0_ref[:B, :]
-        factor_ref[:, B:] = jnp.zeros((B, B), F32)
+        s_ref[:B, :B] = f0_ref[:B, :]
+        s_ref[:B, B:] = jnp.zeros((B, B), F32)
 
     @pl.when(row == 1)
     def _():
-        factor_ref[:, :B] = f0_ref[B:, :]
-        factor_ref[:, B:] = f1_ref[...]
-
-
-def kernel_window(live_ref, rows_ref, own_ref, other_ref, f0_ref, f1_ref, inv_ref, factor_ref, window_ref, out_ref, s_ref):
-    _, y, mine = coords()
-    live_t = live_ref[rows_ref[y]].astype(F32)
-    for j in range(NX * NZ):
-        s_ref[pl.ds(pl.multiple_of((2 * j + mine) * 8, 8), 8), :] = own_ref[j] * live_t
-        s_ref[pl.ds(pl.multiple_of((2 * j + 1 - mine) * 8, 8), 8), :] = other_ref[j] * live_t
-    solve_rows(s_ref, lambda k: inv_ref[k], f0_ref, f1_ref)
-    out_ref[...] = window_ref[...] - mul_t(factor_ref[...], s_ref[...])
+        s_ref[:B, :B] = f0_ref[B:, :]
+        s_ref[:B, B:] = f1_ref[...]
+
+    factor_ref[...] = s_ref[:B, :]
+    out_ref[...] = window_ref[...] - mul_t(s_ref[:B, :], s_ref[B:, :])
 
 
 def kernel_pick(rows_ref, parts_ref, out_ref, sems):
@@ -315,9 +315,8 @@
     piece = jnp.where(root, v[0], 0.0)
     piece = piece + sum(by_x(v[d], d, lambda x, z, c: x == 0 and z == 0) for d in range(1, NX))
     piece = piece + sum(by_z(piece, d, lambda x, z, c: z == 0) for d in (2, 4, 6))
-    even = piece
     piece = piece + by_z(piece, 1, lambda x, z, c: z % 2 == 0)
-    return even, jnp.stack([piece] + [by_x(piece, d) for d in range(1, NX)])
+    return piece, jnp.stack([piece] + [by_x(piece, d) for d in range(1, NX)])
 
 
 def by_y(v, d):
@@ -336,9 +335,6 @@
     row = lax.axis_index("rows")
     y = lax.axis_index("cols")
     x, z, core = row // (2 * NZ), (row // 2) % NZ, row % 2
-    width = 2 * B // NY
-    mine = lax.dynamic_slice_in_dim(panel, y * width, width, 1).reshape(64, 8, width)
-    parts = lax.all_to_all(mine, "rows", 0, 0)
 
     def rows_of(i):
         return lax.dynamic_slice_in_dim(panel, i * H + y * 64, 64, 0).reshape(NX, 16, 2 * B)
@@ -350,25 +346,25 @@
     stack = jnp.concatenate([jnp.where(core == 0, f, s) for f, s in zip(first, second)], axis=1)
     piece, part = spread_static(stack, x, z)
 
-    chosen = pick(window_rows, after(parts, piece))
+    width = 2 * B // NY
+    mine = lax.dynamic_slice_in_dim(panel, y * width, width, 1).reshape(64, 8, width)
+    parts = lax.all_to_all(after(mine, piece), "rows", 0, 0)
+
+    own = gather_y(part)
+    other = swap_core(own)
+    chosen = pick(window_rows, after(parts, part))
     quarters = [chosen[0]] + [by_y(chosen[d], d) for d in range(1, NY)]
-    own = gather_y(after(part, *quarters[1:]))
-    other = swap_core(own)
-    quarters = after(quarters, part)
+    quarters = after(quarters, own)
     (fan,) = call(kernel_fan, 10**6, 8, [(NX * NZ, 8, 2 * B)], [], *quarters)
     t_own = lax.all_to_all(fan, "rows", 0, 0, axis_index_groups=GROUPS)
 
-    f0, d0 = call(kernel_a, 25 * 10**8, 24, [(2 * B, B), (4, NB, NB)], [(2, 5 * H, H), (2 * B, B), (NB, NB)], own, other)
-    f1, d1 = call(kernel_b, 25 * 10**8, 20, [(B, B), (4, NB, NB)], [(2, 5 * H, H), (B, B), (NB, NB)], own, other, f0)
+    f0, d0 = call(kernel_a, COST, 60, [(2 * B, B), (4, NB, NB)], [(2, 5 * H, H), (2 * B, B), (NB, NB)], own, other)
+    f1, d1 = call(kernel_b, COST, 60, [(B, B), (4, NB, NB)], [(2, 5 * H, H), (B, B), (NB, NB)], own, other, f0)
     t_other = swap_core(after(t_own, f1))
-    factor, inv = call(
-        kernel_own, 10**8, 58, [(B, 2 * B), (4, H, H)], [], row_live, f0, f1, d0, d1, panel
+    return call(
+        kernel_c, 10**8, 60, [(B, 2 * B), (B, B)], [(2 * B, 2 * B)],
+        row_live, window_rows, t_own, t_other, f0, f1, d0, d1, panel, window_block,
     )
-    (updated,) = call(
-        kernel_window, 10**8, 58, [(B, B)], [(B, 2 * B)],
-        row_live, window_rows, t_own, t_other, f0, f1, inv, factor, window_block,
-    )
-    return factor, updated
 
 
 def solution(mesh):

time: 130 us -> 134 us (1.031)
  waiting for transfers between devices: 18.2 us -> 28.1 us
  starting transfers between devices: 50.5 us -> 44.4 us
  local copies, waits for them, and re-layouts: 7.89 us -> 5.55 us
  Pallas kernels: 51.5 us -> 53.8 us
    ppermute x12, waiting for transfers between devices: 10.2 us -> 19.4 us  [move(): return lax.ppermute(v, 'rows', pairs)]
    ppermute x12, starting transfers between devices: 22.2 us -> 14.8 us  [move(): return lax.ppermute(v, 'rows', pairs)]
    all_to_all x1, starting transfers between devices: 8.5 us -> 11.1 us  [shards(): parts = lax.all_to_all(after(mine, piece), 'rows', 0, 0)]
    unnamed x15 -> x9, local copies, waits for them, and re-layouts: 4.17 us -> 1.82 us
    pallas_call x5 -> x4, Pallas kernels: 49.4 us -> 51.7 us  [call(): pl.pallas_call(kernel, out_shape=[jax.ShapeDtypeStruct(s, F32) for s in o...]
    all_to_all x1, starting transfers between devices: 8.38 us -> 6.4 us  [shards(): t_own = lax.all_to_all(fan, 'rows', 0, 0, axis_index_groups=GROUPS)]
  transfers between devices with their start and end apart: 21 -> 21, of which waited for: 10 -> 12; matrix products, arithmetic and copies ran while one was open for 2% -> 2% of each run, Pallas kernels for 32% -> 28%
where the time goes in v5:
time: 134 us; the launch traced here: 133 us
  Pallas kernels  53.8 us (40%)
  starting transfers between devices  44.4 us (33%)
  waiting for transfers between devices  28.1 us (21%)
  local copies, waits for them, and re-layouts  5.55 us (4%)
    pallas_call x4, Pallas kernels, call(): pl.pallas_call(kernel, out_shape=[jax.ShapeDtypeStruct(s, F32) for s in o...  51.7 us
    ppermute x12, waiting for transfers between devices, move(): return lax.ppermute(v, 'rows', pairs)  19.4 us
    ppermute x12, starting transfers between devices, move(): return lax.ppermute(v, 'rows', pairs)  14.8 us
    all_to_all x1, starting transfers between devices, shards(): parts = lax.all_to_all(after(mine, piece), 'rows', 0, 0)  11.1 us
    ppermute x6, waiting for transfers between devices, by_y(): return lax.ppermute(v, 'cols', [(i, (i + d) % NY) for i in range(NY)])  7.77 us
    ppermute x6, starting transfers between devices, by_y(): return lax.ppermute(v, 'cols', [(i, (i + d) % NY) for i in range(NY)])  6.95 us
    all_to_all x1, starting transfers between devices, shards(): t_own = lax.all_to_all(fan, 'rows', 0, 0, axis_index_groups=GROUPS)  6.4 us
    ppermute x1, starting transfers between devices, shards(): low = lax.ppermute(bot[:, :, B:], 'rows', [(1, 0)])  5.15 us
  transfers between devices with their start and end apart: 21, of which 12 were waited for; matrix products, arithmetic and copies ran while one was open for 2% of the time, Pallas kernels for 28%

profile of v5, /device:TPU:1, one launch (start us, length us, event | category | flops | bytes accessed | tf_op | source)
XLA Modules:
  0.0 132.9 jit_solution(12834811101098094608)
XLA Ops:
  0.6 1.1 constant_dynamic-slice_fusion
  1.7 5.2 %collective-permute-start = (f32[4,16,512]{2,1,0:T(8,128)S(1)}, f32[4,16,512]{2,1,0:T(8,128)S(1)}, u32[]{:S(2)}, u32[]{:S(2)}) collective-permute-start(f32[4,16,512]{2,1,0:T(8,128)S(1)} %slice.71), channel_id=1, source_target_pairs={{4,0},{5,1},{6,2},{7,3}} | collective-permute-start | bytes 393224 | tf_op jit(solution)/shard_map/ppermute | solution.py:343
  7.0 0.9 collective-permute-done
  7.9 1.3 collective-permute-start.2
  9.2 1.3 collective-permute-start.3
  10.5 1.3 collective-permute-start.1
  12.3 1.3 collective-permute-done.1
  13.6 1.3 collective-permute-start.6
  14.9 1.3 collective-permute-start.5
  16.2 1.3 collective-permute-start.4
  17.7 2.1 %collective-permute-done.4 = f32[80,256]{1,0:T(8,128)S(1)} collective-permute-done((f32[80,256]{1,0:T(8,128)S(1)}, f32[80,256]{1,0:T(8,128)S(1)}, u32[]{:S(2)}, u32[]{:S(2)}) %collective-permute-start.4) | collective-permute-done | bytes 81952 | tf_op jit(solution)/shard_map/ppermute | solution.py:291
  19.8 1.3 collective-permute-start.7
  21.1 1.9 %dynamic-slice_bitcast_fusion = f32[64,8,256]{2,1,0:T(8,128)} fusion(f32[512,1024]{1,0:T(8,128)} %panel_ref.1, s32[]{:T(128)S(6)} %select_n.60), kind=kLoop, calls=%fused_computation.1 | loop fusion | bytes 1048580 | tf_op jit(solution)/shard_map/reshape | solution.py:350
  23.0 11.1 %all-to-all-start = ((f32[64,8,256]{2,1,0:T(8,128)}), f32[64,8,256]{2,1,0:T(8,128)S(1)}, u32[]{:S(2)}, u32[]{:S(2)}) async-start(f32[64,8,256]{2,1,0:T(8,128)} %dynamic-slice_bitcast_fusion), calls=%async_computation | async-start | bytes 1048576 | tf_op jit(solution)/shard_map/all_to_all | solution.py:351
  34.1 2.9 %collective-permute-start.10 = (f32[80,256]{1,0:T(8,128)S(1)}, f32[80,256]{1,0:T(8,128)S(1)}, u32[]{:S(2)}, u32[]{:S(2)}) collective-permute-start(f32[80,256]{1,0:T(8,128)S(1)} %add.56), channel_id=1, source_target_pairs={{0,192},{4,196},{8,200},{12,204},{16,208},{20,212},{24,216},{28,22... | collective-permute-start | bytes 245768 | tf_op jit(solution)/shard_map/ppermute | solution.py:291
  38.0 1.3 collective-permute-done.10
  39.3 4.0 %collective-permute-done.9 = f32[80,256]{1,0:T(8,128)S(1)} collective-permute-done((f32[80,256]{1,0:T(8,128)S(1)}, f32[80,256]{1,0:T(8,128)S(1)}, u32[]{:S(2)}, u32[]{:S(2)}) %collective-permute-start.9) | collective-permute-done | bytes 81952 | tf_op jit(solution)/shard_map/ppermute | solution.py:291
  43.3 5.1 %collective-permute-done.8 = f32[80,256]{1,0:T(8,128)S(1)} collective-permute-done((f32[80,256]{1,0:T(8,128)S(1)}, f32[80,256]{1,0:T(8,128)S(1)}, u32[]{:S(2)}, u32[]{:S(2)}) %collective-permute-start.8) | collective-permute-done | bytes 81952 | tf_op jit(solution)/shard_map/ppermute | solution.py:291
  48.4 2.5 %collective-permute-start.15 = (f32[4,80,256]{2,1,0:T(8,128)S(1)}, f32[4,80,256]{2,1,0:T(8,128)S(1)}, u32[]{:S(2)}, u32[]{:S(2)}) collective-permute-start(f32[4,80,256]{2,1,0:T(8,128)S(1)} %get-tuple-element.27), channel_id=1, source_target_pairs={{0,2},{1,3},{2,0},{3,1},{4,6},{5,7},{6,4},{7,5},{8,10},{9,11},{10,... | collective-permute-start | bytes 983048 | tf_op jit(solution)/shard_map/ppermute | solution.py:323
  51.3 2.3 %collective-permute-start.16 = (f32[4,80,256]{2,1,0:T(8,128)S(1)}, f32[4,80,256]{2,1,0:T(8,128)S(1)}, u32[]{:S(2)}, u32[]{:S(2)}) collective-permute-start(f32[4,80,256]{2,1,0:T(8,128)S(1)} %get-tuple-element.27), channel_id=1, source_target_pairs={{0,3},{1,0},{2,1},{3,2},{4,7},{5,4},{6,5},{7,6},{8,11},{9,8},{10,9... | collective-permute-start | bytes 983048 | tf_op jit(solution)/shard_map/ppermute | solution.py:323
  54.4 2.1 %shard_map.59 = f32[4,8,256]{2,1,0:T(8,128)} custom-call(s32[4]{0:T(128)} %rows_ref.3, f32[64,8,256]{2,1,0:T(8,128)} %copy-done.1), custom_call_target="tpu_custom_call" | custom-call | tf_op jit(solution)/shard_map/pallas_call | solution.py:269
  57.3 0.9 collective-permute-start.12
  59.6 7.2 %collective-permute-done.14 = f32[4,80,256]{2,1,0:T(8,128)S(1)} collective-permute-done((f32[4,80,256]{2,1,0:T(8,128)S(1)}, f32[4,80,256]{2,1,0:T(8,128)S(1)}, u32[]{:S(2)}, u32[]{:S(2)}) %collective-permute-start.14) | collective-permute-done | bytes 327712 | tf_op jit(solution)/shard_map/ppermute | solution.py:323
  67.0 1.2 shard_map.60
  68.1 6.4 %all-to-all-start.1 = ((f32[32,8,1024]{2,1,0:T(8,128)}), f32[32,8,1024]{2,1,0:T(8,128)S(1)}, u32[]{:S(2)}, u32[]{:S(2)}) async-start(f32[32,8,1024]{2,1,0:T(8,128)} %shard_map.60), calls=%async_computation.1 | async-start | bytes 2097152 | tf_op jit(solution)/shard_map/all_to_all | solution.py:359
  74.5 1.1 collective-permute-start.17
  75.7 2.8 %collective-permute-done.17.other_ref = f32[4,4,80,256]{3,2,1,0:T(8,128)} collective-permute-done((f32[4,4,80,256]{3,2,1,0:T(8,128)S(1)}, f32[4,4,80,256]{3,2,1,0:T(8,128)}, u32[]{:S(2)}, u32[]{:S(2)}) %collective-permute-start.17) | collective-permute-done | bytes 1310752 | tf_op jit(solution)/shard_map/ppermute | solution.py:291
  78.5 18.1 %shard_map.61 = (f32[1024,512]{1,0:T(8,128)}, f32[4,128,128]{2,1,0:T(8,128)}) custom-call(f32[4,4,80,256]{3,2,1,0:T(8,128)} %copy-done.2, f32[4,4,80,256]{3,2,1,0:T(8,128)} %collective-permute-done.17.other_ref), custom_call_target="tpu_custom_call" | custom-call | flops 2500000000 | bytes 8388608 | tf_op jit(solution)/shard_map/pallas_call | solution.py:257
  96.6 17.5 %shard_map.62 = (f32[512,512]{1,0:T(8,128)}, f32[4,128,128]{2,1,0:T(8,128)}) custom-call(f32[4,4,80,256]{3,2,1,0:T(8,128)} %copy-done.2, f32[4,4,80,256]{3,2,1,0:T(8,128)} %collective-permute-done.17.other_ref, f32[1024,512]{1,0:T(8,128)} %get-tuple-element.19.f0_ref), custom_call_target="tpu_custom_call" | custom-call | flops 2500000000 | bytes 8388608 | tf_op jit(solution)/shard_map/pallas_call | solution.py:257
  114.7 2.3 %collective-permute-done.18.other_ref = f32[32,8,1024]{2,1,0:T(8,128)S(1)} collective-permute-done((f32[32,8,1024]{2,1,0:T(8,128)S(1)}, f32[32,8,1024]{2,1,0:T(8,128)S(1)}, u32[]{:S(2)}, u32[]{:S(2)}) %collective-permute-start.18) | collective-permute-done | bytes 1048608 | tf_op jit(solution)/shard_map/ppermute | solution.py:291
  117.0 1.0 copy-done.3
  118.0 14.9 %shard_map.63 = (f32[512,1024]{1,0:T(8,128)}, f32[512,512]{1,0:T(8,128)}) custom-call(s32[64]{0:T(128)} %live_ref.1, s32[4]{0:T(128)} %rows_ref.3, f32[32,8,1024]{2,1,0:T(8,128)} %copy-done, f32[32,8,1024]{2,1,0:T(8,128)} %copy-done.3, f32[1024,512]{1,0:T(8,128)} %get-tuple-element.19.f0_ref, f32[512,512]{1,0:T(8,128)} %get-tuple-element.20.f1_ref, ...), custom_call_target="tpu_custom_call" | custom-call | flops 100000000 | bytes 8388608 | tf_op jit(solution)/shard_map/pallas_call | solution.py:257
  (38 shorter events, 5.9 us)
Async XLA Ops:
  1.7 6.1 %collective-permute-start = (f32[4,16,512]{2,1,0:T(8,128)S(1)}, f32[4,16,512]{2,1,0:T(8,128)S(1)}, u32[]{:S(2)}, u32[]{:S(2)}) collective-permute-start(f32[4,16,512]{2,1,0:T(8,128)S(1)} %slice.71), channel_id=1, source_target_pairs={{4,0},{5,1},{6,2},{7,3}} | collective-permute-start | bytes 393224 | tf_op jit(solution)/shard_map/ppermute | solution.py:343
  7.9 4.0 %collective-permute-start.2 = (f32[80,256]{1,0:T(8,128)S(1)}, f32[80,256]{1,0:T(8,128)S(1)}, u32[]{:S(2)}, u32[]{:S(2)}) collective-permute-start(f32[80,256]{1,0:T(8,128)S(1)} %get-tuple-element.28), channel_id=1, source_target_pairs={{0,128},{4,132},{1,129},{5,133},{2,130},{6,134},{3,131},{7,135}} | collective-permute-start | bytes 245768 | tf_op jit(solution)/shard_map/ppermute | solution.py:291
  9.2 3.1 %collective-permute-start.3 = (f32[80,256]{1,0:T(8,128)S(1)}, f32[80,256]{1,0:T(8,128)S(1)}, u32[]{:S(2)}, u32[]{:S(2)}) collective-permute-start(f32[80,256]{1,0:T(8,128)S(1)} %get-tuple-element.29), channel_id=1, source_target_pairs={{0,192},{4,196},{1,193},{5,197},{2,194},{6,198},{3,195},{7,199}} | collective-permute-start | bytes 245768 | tf_op jit(solution)/shard_map/ppermute | solution.py:291
  10.5 3.1 %collective-permute-start.1 = (f32[80,256]{1,0:T(8,128)S(1)}, f32[80,256]{1,0:T(8,128)S(1)}, u32[]{:S(2)}, u32[]{:S(2)}) collective-permute-start(f32[80,256]{1,0:T(8,128)S(1)} %get-tuple-element.30), channel_id=1, source_target_pairs={{0,64},{4,68},{1,65},{5,69},{2,66},{6,70},{3,67},{7,71}} | collective-permute-start | bytes 245768 | tf_op jit(solution)/shard_map/ppermute | solution.py:291
  13.6 3.9 %collective-permute-start.6 = (f32[80,256]{1,0:T(8,128)S(1)}, f32[80,256]{1,0:T(8,128)S(1)}, u32[]{:S(2)}, u32[]{:S(2)}) collective-permute-start(f32[80,256]{1,0:T(8,128)S(1)} %fusion.1), channel_id=1, source_target_pairs={{0,48},{4,52},{64,112},{68,116},{128,176},{132,180},{192,240},{196... | collective-permute-start | bytes 245768 | tf_op jit(solution)/shard_map/ppermute | solution.py:291
  14.9 2.8 %collective-permute-start.5 = (f32[80,256]{1,0:T(8,128)S(1)}, f32[80,256]{1,0:T(8,128)S(1)}, u32[]{:S(2)}, u32[]{:S(2)}) collective-permute-start(f32[80,256]{1,0:T(8,128)S(1)} %fusion.1), channel_id=1, source_target_pairs={{0,32},{4,36},{64,96},{68,100},{128,160},{132,164},{192,224},{196,... | collective-permute-start | bytes 245768 | tf_op jit(solution)/shard_map/ppermute | solution.py:291
  16.2 3.5 %collective-permute-start.4 = (f32[80,256]{1,0:T(8,128)S(1)}, f32[80,256]{1,0:T(8,128)S(1)}, u32[]{:S(2)}, u32[]{:S(2)}) collective-permute-start(f32[80,256]{1,0:T(8,128)S(1)} %fusion.1), channel_id=1, source_target_pairs={{0,16},{4,20},{64,80},{68,84},{128,144},{132,148},{192,208},{196,2... | collective-permute-start | bytes 245768 | tf_op jit(solution)/shard_map/ppermute | solution.py:291
  19.8 3.2 %collective-permute-start.7 = (f32[80,256]{1,0:T(8,128)S(1)}, f32[80,256]{1,0:T(8,128)S(1)}, u32[]{:S(2)}, u32[]{:S(2)}) collective-permute-start(f32[80,256]{1,0:T(8,128)S(1)} %add_add_fusion), channel_id=1, source_target_pairs={{0,8},{4,12},{16,24},{20,28},{32,40},{36,44},{48,56},{52,60},{64,7... | collective-permute-start | bytes 245768 | tf_op jit(solution)/shard_map/ppermute | solution.py:291
  23.0 30.7 %all-to-all-start = ((f32[64,8,256]{2,1,0:T(8,128)}), f32[64,8,256]{2,1,0:T(8,128)S(1)}, u32[]{:S(2)}, u32[]{:S(2)}) async-start(f32[64,8,256]{2,1,0:T(8,128)} %dynamic-slice_bitcast_fusion), calls=%async_computation | async-start | bytes 1048576 | tf_op jit(solution)/shard_map/all_to_all | solution.py:351
  34.1 5.2 %collective-permute-start.10 = (f32[80,256]{1,0:T(8,128)S(1)}, f32[80,256]{1,0:T(8,128)S(1)}, u32[]{:S(2)}, u32[]{:S(2)}) collective-permute-start(f32[80,256]{1,0:T(8,128)S(1)} %add.56), channel_id=1, source_target_pairs={{0,192},{4,196},{8,200},{12,204},{16,208},{20,212},{24,216},{28,22... | collective-permute-start | bytes 245768 | tf_op jit(solution)/shard_map/ppermute | solution.py:291
  37.0 6.3 %collective-permute-start.9 = (f32[80,256]{1,0:T(8,128)S(1)}, f32[80,256]{1,0:T(8,128)S(1)}, u32[]{:S(2)}, u32[]{:S(2)}) collective-permute-start(f32[80,256]{1,0:T(8,128)S(1)} %add.56), channel_id=1, source_target_pairs={{0,128},{4,132},{8,136},{12,140},{16,144},{20,148},{24,152},{28,15... | collective-permute-start | bytes 245768 | tf_op jit(solution)/shard_map/ppermute | solution.py:291
  37.4 11.0 %collective-permute-start.8 = (f32[80,256]{1,0:T(8,128)S(1)}, f32[80,256]{1,0:T(8,128)S(1)}, u32[]{:S(2)}, u32[]{:S(2)}) collective-permute-start(f32[80,256]{1,0:T(8,128)S(1)} %add.56), channel_id=1, source_target_pairs={{0,64},{4,68},{8,72},{12,76},{16,80},{20,84},{24,88},{28,92},{32,9... | collective-permute-start | bytes 245768 | tf_op jit(solution)/shard_map/ppermute | solution.py:291
  48.4 10.3 %collective-permute-start.15 = (f32[4,80,256]{2,1,0:T(8,128)S(1)}, f32[4,80,256]{2,1,0:T(8,128)S(1)}, u32[]{:S(2)}, u32[]{:S(2)}) collective-permute-start(f32[4,80,256]{2,1,0:T(8,128)S(1)} %get-tuple-element.27), channel_id=1, source_target_pairs={{0,2},{1,3},{2,0},{3,1},{4,6},{5,7},{6,4},{7,5},{8,10},{9,11},{10,... | collective-permute-start | bytes 983048 | tf_op jit(solution)/shard_map/ppermute | solution.py:323
  50.9 15.8 %collective-permute-start.14 = (f32[4,80,256]{2,1,0:T(8,128)S(1)}, f32[4,80,256]{2,1,0:T(8,128)S(1)}, u32[]{:S(2)}, u32[]{:S(2)}) collective-permute-start(f32[4,80,256]{2,1,0:T(8,128)S(1)} %get-tuple-element.27), channel_id=1, source_target_pairs={{0,1},{1,2},{2,3},{3,0},{4,5},{5,6},{6,7},{7,4},{8,9},{9,10},{10,1... | collective-permute-start | bytes 983048 | tf_op jit(solution)/shard_map/ppermute | solution.py:323
  51.3 15.4 %collective-permute-start.16 = (f32[4,80,256]{2,1,0:T(8,128)S(1)}, f32[4,80,256]{2,1,0:T(8,128)S(1)}, u32[]{:S(2)}, u32[]{:S(2)}) collective-permute-start(f32[4,80,256]{2,1,0:T(8,128)S(1)} %get-tuple-element.27), channel_id=1, source_target_pairs={{0,3},{1,0},{2,1},{3,2},{4,7},{5,4},{6,5},{7,6},{8,11},{9,8},{10,9... | collective-permute-start | bytes 983048 | tf_op jit(solution)/shard_map/ppermute | solution.py:323
  53.6 0.8 copy-start.1
  57.3 9.7 %collective-permute-start.13 = (f32[8,256]{1,0:T(8,128)S(1)}, f32[8,256]{1,0:T(8,128)S(1)}, u32[]{:S(2)}, u32[]{:S(2)}) collective-permute-start(f32[8,256]{1,0:T(8,128)S(1)} %get-tuple-element.31), channel_id=1, source_target_pairs={{0,3},{1,0},{2,1},{3,2},{4,7},{5,4},{6,5},{7,6},{8,11},{9,8},{10,9... | collective-permute-start | bytes 24584 | tf_op jit(solution)/shard_map/ppermute | solution.py:323
  57.3 9.6 %collective-permute-start.12 = (f32[8,256]{1,0:T(8,128)S(1)}, f32[8,256]{1,0:T(8,128)S(1)}, u32[]{:S(2)}, u32[]{:S(2)}) collective-permute-start(f32[8,256]{1,0:T(8,128)S(1)} %get-tuple-element.32), channel_id=1, source_target_pairs={{0,2},{1,3},{2,0},{3,1},{4,6},{5,7},{6,4},{7,5},{8,10},{9,11},{10,... | collective-permute-start | bytes 24584 | tf_op jit(solution)/shard_map/ppermute | solution.py:323
  58.8 8.2 %collective-permute-start.11 = (f32[8,256]{1,0:T(8,128)S(1)}, f32[8,256]{1,0:T(8,128)S(1)}, u32[]{:S(2)}, u32[]{:S(2)}) collective-permute-start(f32[8,256]{1,0:T(8,128)S(1)} %get-tuple-element.33), channel_id=1, source_target_pairs={{0,1},{1,2},{2,3},{3,0},{4,5},{5,6},{6,7},{7,4},{8,9},{9,10},{10,1... | collective-permute-start | bytes 24584 | tf_op jit(solution)/shard_map/ppermute | solution.py:323
  66.9 7.6 %copy-start.2 = (f32[4,4,80,256]{3,2,1,0:T(8,128)}, f32[4,4,80,256]{3,2,1,0:T(8,128)S(1)}, u32[]{:S(2)}) copy-start(f32[4,4,80,256]{3,2,1,0:T(8,128)S(1)} %pad_maximum_fusion.own_ref) | copy-start | bytes 3932164
  68.1 46.0 %all-to-all-start.1 = ((f32[32,8,1024]{2,1,0:T(8,128)}), f32[32,8,1024]{2,1,0:T(8,128)S(1)}, u32[]{:S(2)}, u32[]{:S(2)}) async-start(f32[32,8,1024]{2,1,0:T(8,128)} %shard_map.60), calls=%async_computation.1 | async-start | bytes 2097152 | tf_op jit(solution)/shard_map/all_to_all | solution.py:359
  74.5 3.9 %collective-permute-start.17 = (f32[4,4,80,256]{3,2,1,0:T(8,128)S(1)}, f32[4,4,80,256]{3,2,1,0:T(8,128)}, u32[]{:S(2)}, u32[]{:S(2)}) collective-permute-start(f32[4,4,80,256]{3,2,1,0:T(8,128)S(1)} %pad_maximum_fusion.own_ref), channel_id=1, source_target_pairs={{0,4},{4,0},{8,12},{12,8},{16,20},{20,16},{24,28},{28,24},{32,36},... | collective-permute-start | bytes 3932168 | tf_op jit(solution)/shard_map/ppermute | solution.py:291
  114.1 2.9 %copy-start = (f32[32,8,1024]{2,1,0:T(8,128)}, f32[32,8,1024]{2,1,0:T(8,128)S(1)}, u32[]{:S(2)}) copy-start(f32[32,8,1024]{2,1,0:T(8,128)S(1)} %all-to-all-done.1.own_ref) | copy-start | bytes 3145732
  114.1 2.9 %collective-permute-start.18 = (f32[32,8,1024]{2,1,0:T(8,128)S(1)}, f32[32,8,1024]{2,1,0:T(8,128)S(1)}, u32[]{:S(2)}, u32[]{:S(2)}) collective-permute-start(f32[32,8,1024]{2,1,0:T(8,128)S(1)} %all-to-all-done.1.own_ref), channel_id=1, source_target_pairs={{0,4},{4,0},{8,12},{12,8},{16,20},{20,16},{24,28},{28,24},{32,36},... | collective-permute-start | bytes 3145736 | tf_op jit(solution)/shard_map/ppermute | solution.py:291
  117.0 1.0 copy-start.3

commit v6 on v5

--- a/solution.py
+++ b/solution.py
@@ -11,7 +11,7 @@
 B = 512
 NB = 128
 H = B // 2
-COST = 25 * 10**8
+COST = 35 * 10**8
 NX, NZ, NY = 4, 8, 4
 CONTRACT = (((1,), (1,)), ((), ()))
 
@@ -228,10 +228,11 @@
     out_ref[...] = window_ref[...] - mul_t(s_ref[:B, :], s_ref[B:, :])
 
 
-def kernel_pick(rows_ref, parts_ref, out_ref, sems):
+def kernel_pick(rows_ref, parts_ref, *refs):
     y = lax.axis_index("cols")
+    outs, sems = refs[:NY], refs[NY]
     copies = [
-        pltpu.make_async_copy(parts_ref.at[rows_ref[lax.rem(y + d, NY)]], out_ref.at[d], sems.at[d]) for d in range(NY)
+        pltpu.make_async_copy(parts_ref.at[rows_ref[lax.rem(y + d, NY)]], outs[d], sems.at[d]) for d in range(NY)
     ]
     for c in copies:
         c.start()
@@ -268,11 +269,11 @@
 def pick(window_rows, parts):
     return pl.pallas_call(
         kernel_pick,
-        out_shape=jax.ShapeDtypeStruct((NY,) + parts.shape[1:], F32),
-        in_specs=[SMEM, pl.BlockSpec(memory_space=pl.ANY)],
-        out_specs=VM,
+        out_shape=[jax.ShapeDtypeStruct(parts.shape[1:], F32)] * NY,
+        in_specs=[SMEM, pl.BlockSpec(memory_space=pltpu.HBM)],
+        out_specs=[VM] * NY,
         scratch_shapes=[pltpu.SemaphoreType.DMA((NY,))],
-        compiler_params=pltpu.CompilerParams(vmem_limit_bytes=56 << 20),
+        compiler_params=pltpu.CompilerParams(vmem_limit_bytes=8 << 20),
     )(window_rows, parts)
 
 
@@ -316,7 +317,7 @@
     piece = piece + sum(by_x(v[d], d, lambda x, z, c: x == 0 and z == 0) for d in range(1, NX))
     piece = piece + sum(by_z(piece, d, lambda x, z, c: z == 0) for d in (2, 4, 6))
     piece = piece + by_z(piece, 1, lambda x, z, c: z % 2 == 0)
-    return piece, jnp.stack([piece] + [by_x(piece, d) for d in range(1, NX)])
+    return piece
 
 
 def by_y(v, d):
@@ -344,23 +345,24 @@
     first = [top[:, :, :H], bot[:, :, :H], bot[:, :, H:B], low[:, :, :H], low[:, :, H:]]
     second = [top[:, :, :H], top[:, :, H:B], bot[:, :, :H], bot[:, :, H:B], top[:, :, B : B + H]]
     stack = jnp.concatenate([jnp.where(core == 0, f, s) for f, s in zip(first, second)], axis=1)
-    piece, part = spread_static(stack, x, z)
+    piece = spread_static(stack, x, z)
 
     width = 2 * B // NY
     mine = lax.dynamic_slice_in_dim(panel, y * width, width, 1).reshape(64, 8, width)
-    parts = lax.all_to_all(after(mine, piece), "rows", 0, 0)
-
-    own = gather_y(part)
+    chosen = pick(window_rows, lax.all_to_all(mine, "rows", 0, 0))
+    piece = after(piece, *chosen)
+    quarters = [chosen[0]] + [by_y(chosen[d], d) for d in range(1, NY)]
+    part = jnp.stack([piece] + [by_x(piece, d) for d in range(1, NX)])
+
+    own = gather_y(after(part, *quarters[1:]))
     other = swap_core(own)
-    chosen = pick(window_rows, after(parts, part))
-    quarters = [chosen[0]] + [by_y(chosen[d], d) for d in range(1, NY)]
-    quarters = after(quarters, own)
+    quarters = after(quarters, part)
     (fan,) = call(kernel_fan, 10**6, 8, [(NX * NZ, 8, 2 * B)], [], *quarters)
     t_own = lax.all_to_all(fan, "rows", 0, 0, axis_index_groups=GROUPS)
 
-    f0, d0 = call(kernel_a, COST, 60, [(2 * B, B), (4, NB, NB)], [(2, 5 * H, H), (2 * B, B), (NB, NB)], own, other)
-    f1, d1 = call(kernel_b, COST, 60, [(B, B), (4, NB, NB)], [(2, 5 * H, H), (B, B), (NB, NB)], own, other, f0)
-    t_other = swap_core(after(t_own, f1))
+    f0, d0 = call(kernel_a, COST, 24, [(2 * B, B), (4, NB, NB)], [(2, 5 * H, H), (2 * B, B), (NB, NB)], own, other)
+    t_other = swap_core(after(t_own, f0))
+    f1, d1 = call(kernel_b, COST, 20, [(B, B), (4, NB, NB)], [(2, 5 * H, H), (B, B), (NB, NB)], own, other, f0)
     return call(
         kernel_c, 10**8, 60, [(B, 2 * B), (B, B)], [(2 * B, 2 * B)],
         row_live, window_rows, t_own, t_other, f0, f1, d0, d1, panel, window_block,

time: 134 us -> 125 us (0.933)
  waiting for transfers between devices: 28.1 us -> 18 us
  Pallas kernels: 53.8 us -> 45.6 us
  starting transfers between devices: 44.4 us -> 50.3 us
  local copies, waits for them, and re-layouts: 5.55 us -> 8.76 us
    ppermute x12, waiting for transfers between devices: 19.4 us -> 10.3 us  [move(): return lax.ppermute(v, 'rows', pairs)]
    pallas_call x4, Pallas kernels: 51.7 us -> 44.9 us  [call(): pl.pallas_call(kernel, out_shape=[jax.ShapeDtypeStruct(s, F32) for s in o...]
    ppermute x12, starting transfers between devices: 14.8 us -> 20.3 us  [move(): return lax.ppermute(v, 'rows', pairs)]
    unnamed x9 -> x17, local copies, waits for them, and re-layouts: 1.82 us -> 5.79 us
    all_to_all x1, starting transfers between devices: 11.1 us -> 8.5 us  [shards(): chosen = pick(window_rows, lax.all_to_all(mine, 'rows', 0, 0))]
    all_to_all x1, starting transfers between devices: 6.4 us -> 8.81 us  [shards(): t_own = lax.all_to_all(fan, 'rows', 0, 0, axis_index_groups=GROUPS)]
    pallas_call x1, Pallas kernels: 2.07 us -> 0.64 us  [pick(): pl.pallas_call(kernel_pick, out_shape=[jax.ShapeDtypeStruct(parts.shape[1...]
  transfers between devices with their start and end apart: 21 -> 21, of which waited for: 12 -> 11; matrix products, arithmetic and copies ran while one was open for 2% -> 2% of each run, Pallas kernels for 28% -> 24%
where the time goes in v6:
time: 125 us; the launch traced here: 124 us
  starting transfers between devices  50.3 us (40%)
  Pallas kernels  45.6 us (36%)
  waiting for transfers between devices  18 us (14%)
  local copies, waits for them, and re-layouts  8.76 us (7%)
    pallas_call x4, Pallas kernels, call(): pl.pallas_call(kernel, out_shape=[jax.ShapeDtypeStruct(s, F32) for s in o...  44.9 us
    ppermute x12, starting transfers between devices, move(): return lax.ppermute(v, 'rows', pairs)  20.3 us
    ppermute x12, waiting for transfers between devices, move(): return lax.ppermute(v, 'rows', pairs)  10.3 us
    all_to_all x1, starting transfers between devices, shards(): t_own = lax.all_to_all(fan, 'rows', 0, 0, axis_index_groups=GROUPS)  8.81 us
    all_to_all x1, starting transfers between devices, shards(): chosen = pick(window_rows, lax.all_to_all(mine, 'rows', 0, 0))  8.5 us
    ppermute x6, waiting for transfers between devices, by_y(): return lax.ppermute(v, 'cols', [(i, (i + d) % NY) for i in range(NY)])  7.69 us
    ppermute x6, starting transfers between devices, by_y(): return lax.ppermute(v, 'cols', [(i, (i + d) % NY) for i in range(NY)])  7.55 us
    unnamed x17, local copies, waits for them, and re-layouts  5.79 us
  transfers between devices with their start and end apart: 21, of which 11 were waited for; matrix products, arithmetic and copies ran while one was open for 2% of the time, Pallas kernels for 24%

profile of v6, /device:TPU:1, one launch (start us, length us, event | category | flops | bytes accessed | tf_op | source)
XLA Modules:
  0.0 123.8 jit_solution(7984476086023649596)
XLA Ops:
  0.6 1.1 constant_dynamic-slice_fusion
  1.7 5.2 %collective-permute-start.3 = (f32[4,16,512]{2,1,0:T(8,128)S(1)}, f32[4,16,512]{2,1,0:T(8,128)S(1)}, u32[]{:S(2)}, u32[]{:S(2)}) collective-permute-start(f32[4,16,512]{2,1,0:T(8,128)S(1)} %slice.55), channel_id=1, source_target_pairs={{4,0},{5,1},{6,2},{7,3}} | collective-permute-start | bytes 393224 | tf_op jit(solution)/shard_map/ppermute | solution.py:344
  6.9 1.9 %dynamic-slice_bitcast_fusion = f32[64,8,256]{2,1,0:T(8,128)} fusion(f32[512,1024]{1,0:T(8,128)} %panel_ref.1, s32[]{:T(128)S(6)} %select_n.60), kind=kLoop, calls=%fused_computation.1 | loop fusion | bytes 1048580 | tf_op jit(solution)/shard_map/reshape | solution.py:351
  8.8 8.5 %all-to-all-start = ((f32[64,8,256]{2,1,0:T(8,128)}), f32[64,8,256]{2,1,0:T(8,128)S(1)}, u32[]{:S(2)}, u32[]{:S(2)}) async-start(f32[64,8,256]{2,1,0:T(8,128)} %dynamic-slice_bitcast_fusion), calls=%async_computation | async-start | bytes 1048576 | tf_op jit(solution)/shard_map/all_to_all | solution.py:352
  17.4 4.9 %collective-permute-start.5 = (f32[80,256]{1,0:T(8,128)S(1)}, f32[80,256]{1,0:T(8,128)S(1)}, u32[]{:S(2)}, u32[]{:S(2)}) collective-permute-start(f32[80,256]{1,0:T(8,128)S(1)} %get-tuple-element.34), channel_id=1, source_target_pairs={{0,128},{4,132},{1,129},{5,133},{2,130},{6,134},{3,131},{7,135}} | collective-permute-start | bytes 245768 | tf_op jit(solution)/shard_map/ppermute | solution.py:292
  22.3 1.3 %collective-permute-start.6 = (f32[80,256]{1,0:T(8,128)S(1)}, f32[80,256]{1,0:T(8,128)S(1)}, u32[]{:S(2)}, u32[]{:S(2)}) collective-permute-start(f32[80,256]{1,0:T(8,128)S(1)} %get-tuple-element.35), channel_id=1, source_target_pairs={{0,192},{4,196},{1,193},{5,197},{2,194},{6,198},{3,195},{7,199}} | collective-permute-start | bytes 245768 | tf_op jit(solution)/shard_map/ppermute | solution.py:292
  23.6 1.3 %collective-permute-start.4 = (f32[80,256]{1,0:T(8,128)S(1)}, f32[80,256]{1,0:T(8,128)S(1)}, u32[]{:S(2)}, u32[]{:S(2)}) collective-permute-start(f32[80,256]{1,0:T(8,128)S(1)} %get-tuple-element.36), channel_id=1, source_target_pairs={{0,64},{4,68},{1,65},{5,69},{2,66},{6,70},{3,67},{7,71}} | collective-permute-start | bytes 245768 | tf_op jit(solution)/shard_map/ppermute | solution.py:292
  25.7 3.2 %collective-permute-done.4 = f32[80,256]{1,0:T(8,128)S(1)} collective-permute-done((f32[80,256]{1,0:T(8,128)S(1)}, f32[80,256]{1,0:T(8,128)S(1)}, u32[]{:S(2)}, u32[]{:S(2)}) %collective-permute-start.4) | collective-permute-done | bytes 81952 | tf_op jit(solution)/shard_map/ppermute | solution.py:292
  28.9 1.3 %collective-permute-start.9 = (f32[80,256]{1,0:T(8,128)S(1)}, f32[80,256]{1,0:T(8,128)S(1)}, u32[]{:S(2)}, u32[]{:S(2)}) collective-permute-start(f32[80,256]{1,0:T(8,128)S(1)} %fusion.1), channel_id=1, source_target_pairs={{0,48},{4,52},{64,112},{68,116},{128,176},{132,180},{192,240},{196... | collective-permute-start | bytes 245768 | tf_op jit(solution)/shard_map/ppermute | solution.py:292
  30.2 1.3 %collective-permute-start.8 = (f32[80,256]{1,0:T(8,128)S(1)}, f32[80,256]{1,0:T(8,128)S(1)}, u32[]{:S(2)}, u32[]{:S(2)}) collective-permute-start(f32[80,256]{1,0:T(8,128)S(1)} %fusion.1), channel_id=1, source_target_pairs={{0,32},{4,36},{64,96},{68,100},{128,160},{132,164},{192,224},{196,... | collective-permute-start | bytes 245768 | tf_op jit(solution)/shard_map/ppermute | solution.py:292
  31.5 1.3 %collective-permute-start.7 = (f32[80,256]{1,0:T(8,128)S(1)}, f32[80,256]{1,0:T(8,128)S(1)}, u32[]{:S(2)}, u32[]{:S(2)}) collective-permute-start(f32[80,256]{1,0:T(8,128)S(1)} %fusion.1), channel_id=1, source_target_pairs={{0,16},{4,20},{64,80},{68,84},{128,144},{132,148},{192,208},{196,2... | collective-permute-start | bytes 245768 | tf_op jit(solution)/shard_map/ppermute | solution.py:292
  33.0 2.0 %collective-permute-done.7 = f32[80,256]{1,0:T(8,128)S(1)} collective-permute-done((f32[80,256]{1,0:T(8,128)S(1)}, f32[80,256]{1,0:T(8,128)S(1)}, u32[]{:S(2)}, u32[]{:S(2)}) %collective-permute-start.7) | collective-permute-done | bytes 81952 | tf_op jit(solution)/shard_map/ppermute | solution.py:292
  35.0 1.3 %collective-permute-start.10 = (f32[80,256]{1,0:T(8,128)S(1)}, f32[80,256]{1,0:T(8,128)S(1)}, u32[]{:S(2)}, u32[]{:S(2)}) collective-permute-start(f32[80,256]{1,0:T(8,128)S(1)} %add_add_fusion), channel_id=1, source_target_pairs={{0,8},{4,12},{16,24},{20,28},{32,40},{36,44},{48,56},{52,60},{64,7... | collective-permute-start | bytes 245768 | tf_op jit(solution)/shard_map/ppermute | solution.py:292
  36.3 1.5 %collective-permute-done.10 = f32[80,256]{1,0:T(8,128)S(1)} collective-permute-done((f32[80,256]{1,0:T(8,128)S(1)}, f32[80,256]{1,0:T(8,128)S(1)}, u32[]{:S(2)}, u32[]{:S(2)}) %collective-permute-start.10) | collective-permute-done | bytes 81952 | tf_op jit(solution)/shard_map/ppermute | solution.py:292
  39.3 3.7 %collective-permute-start.12 = (f32[80,256]{1,0:T(8,128)S(1)}, f32[80,256]{1,0:T(8,128)S(1)}, u32[]{:S(2)}, u32[]{:S(2)}) collective-permute-start(f32[80,256]{1,0:T(8,128)S(1)} %add.56), channel_id=1, source_target_pairs={{0,128},{4,132},{8,136},{12,140},{16,144},{20,148},{24,152},{28,15... | collective-permute-start | bytes 245768 | tf_op jit(solution)/shard_map/ppermute | solution.py:292
  43.0 1.3 %collective-permute-start = (f32[8,256]{1,0:T(8,128)S(1)}, f32[8,256]{1,0:T(8,128)S(1)}, u32[]{:S(2)}, u32[]{:S(2)}) collective-permute-start(f32[8,256]{1,0:T(8,128)S(1)} %get-tuple-element.18), channel_id=1, source_target_pairs={{0,1},{1,2},{2,3},{3,0},{4,5},{5,6},{6,7},{7,4},{8,9},{9,10},{10,1... | collective-permute-start | bytes 24584 | tf_op jit(solution)/shard_map/ppermute | solution.py:324
  44.3 2.6 %collective-permute-start.1 = (f32[8,256]{1,0:T(8,128)S(1)}, f32[8,256]{1,0:T(8,128)S(1)}, u32[]{:S(2)}, u32[]{:S(2)}) collective-permute-start(f32[8,256]{1,0:T(8,128)S(1)} %get-tuple-element.19), channel_id=1, source_target_pairs={{0,2},{1,3},{2,0},{3,1},{4,6},{5,7},{6,4},{7,5},{8,10},{9,11},{10,... | collective-permute-start | bytes 24584 | tf_op jit(solution)/shard_map/ppermute | solution.py:324
  46.9 1.1 collective-permute-start.2
  48.3 1.4 %collective-permute-done.2.q3_ref = f32[8,256]{1,0:T(8,128)S(1)} collective-permute-done((f32[8,256]{1,0:T(8,128)S(1)}, f32[8,256]{1,0:T(8,128)S(1)}, u32[]{:S(2)}, u32[]{:S(2)}) %collective-permute-start.2) | collective-permute-done | bytes 8224 | tf_op jit(solution)/shard_map/ppermute | solution.py:324
  49.7 2.0 %collective-permute-start.16 = (f32[4,80,256]{2,1,0:T(8,128)S(1)}, f32[4,80,256]{2,1,0:T(8,128)S(1)}, u32[]{:S(2)}, u32[]{:S(2)}) collective-permute-start(f32[4,80,256]{2,1,0:T(8,128)S(1)} %pad_maximum_fusion.1), channel_id=1, source_target_pairs={{0,3},{1,0},{2,1},{3,2},{4,7},{5,4},{6,5},{7,6},{8,11},{9,8},{10,9... | collective-permute-start | bytes 983048 | tf_op jit(solution)/shard_map/ppermute | solution.py:324
  52.3 1.0 shard_map.60
  53.3 8.8 %all-to-all-start.1 = ((f32[32,8,1024]{2,1,0:T(8,128)}), f32[32,8,1024]{2,1,0:T(8,128)}, u32[]{:S(2)}, u32[]{:S(2)}) async-start(f32[32,8,1024]{2,1,0:T(8,128)} %shard_map.60), calls=%async_computation.1 | async-start | bytes 2097152 | tf_op jit(solution)/shard_map/all_to_all | solution.py:361
  62.2 6.1 %collective-permute-done.14 = f32[4,80,256]{2,1,0:T(8,128)S(1)} collective-permute-done((f32[4,80,256]{2,1,0:T(8,128)S(1)}, f32[4,80,256]{2,1,0:T(8,128)S(1)}, u32[]{:S(2)}, u32[]{:S(2)}) %collective-permute-start.14) | collective-permute-done | bytes 327712 | tf_op jit(solution)/shard_map/ppermute | solution.py:324
  68.4 2.0 %collective-permute-start.17 = (f32[4,4,80,256]{3,2,1,0:T(8,128)S(1)}, f32[4,4,80,256]{3,2,1,0:T(8,128)S(1)}, u32[]{:S(2)}, u32[]{:S(2)}) collective-permute-start(f32[4,4,80,256]{3,2,1,0:T(8,128)S(1)} %pad_maximum_fusion.own_ref), channel_id=1, source_target_pairs={{0,4},{4,0},{8,12},{12,8},{16,20},{20,16},{24,28},{28,24},{32,36},... | collective-permute-start | bytes 3932168 | tf_op jit(solution)/shard_map/ppermute | solution.py:292
  70.5 2.7 %collective-permute-done.17.other_ref = f32[4,4,80,256]{3,2,1,0:T(8,128)S(1)} collective-permute-done((f32[4,4,80,256]{3,2,1,0:T(8,128)S(1)}, f32[4,4,80,256]{3,2,1,0:T(8,128)S(1)}, u32[]{:S(2)}, u32[]{:S(2)}) %collective-permute-start.17) | collective-permute-done | bytes 1310752 | tf_op jit(solution)/shard_map/ppermute | solution.py:292
  73.1 14.9 %shard_map.61 = (f32[1024,512]{1,0:T(8,128)S(1)}, f32[4,128,128]{2,1,0:T(8,128)S(1)}) custom-call(f32[4,4,80,256]{3,2,1,0:T(8,128)S(1)} %pad_maximum_fusion.own_ref, f32[4,4,80,256]{3,2,1,0:T(8,128)S(1)} %collective-permute-done.17.other_ref), custom_call_target="tpu_custom_call" | custom-call | flops 3500000000 | bytes 8388608 | tf_op jit(solution)/shard_map/pallas_call | solution.py:258
  88.8 1.1 copy-done.5
  89.9 1.0 collective-permute-start.18
  90.9 1.3 %copy-done.6 = f32[4,4,80,256]{3,2,1,0:T(8,128)S(1)} copy-done((f32[4,4,80,256]{3,2,1,0:T(8,128)S(1)}, f32[4,4,80,256]{3,2,1,0:T(8,128)}, u32[]{:S(2)}) %copy-start.6) | copy-done | bytes 1310744
  92.2 14.1 %shard_map.62 = (f32[512,512]{1,0:T(8,128)S(1)}, f32[4,128,128]{2,1,0:T(8,128)S(1)}) custom-call(f32[4,4,80,256]{3,2,1,0:T(8,128)S(1)} %pad_maximum_fusion.own_ref, f32[4,4,80,256]{3,2,1,0:T(8,128)S(1)} %copy-done.6, f32[1024,512]{1,0:T(8,128)S(1)} %get-tuple-element.27.f0_ref), custom_call_target="tpu_custom_call" | custom-call | flops 3500000000 | bytes 8388608 | tf_op jit(solution)/shard_map/pallas_call | solution.py:258
  106.2 1.0 copy-done.1
  109.0 14.9 %shard_map.63 = (f32[512,1024]{1,0:T(8,128)}, f32[512,512]{1,0:T(8,128)}) custom-call(s32[64]{0:T(128)} %live_ref.1, s32[4]{0:T(128)} %rows_ref.3, f32[32,8,1024]{2,1,0:T(8,128)} %all-to-all-done.1.own_ref, f32[32,8,1024]{2,1,0:T(8,128)} %copy-done.7, f32[1024,512]{1,0:T(8,128)} %copy-done, f32[512,512]{1,0:T(8,128)} %copy-done.1, f32[4,128,128]{2,1,0:T(8,128)} %copy-done.2, ...), custom_call_target="tpu_custom_call" | custom-call | flops 100000000 | bytes 8388608 | tf_op jit(solution)/shard_map/pallas_call | solution.py:258
  (45 shorter events, 5.9 us)
Async XLA Ops:
  1.7 15.6 %collective-permute-start.3 = (f32[4,16,512]{2,1,0:T(8,128)S(1)}, f32[4,16,512]{2,1,0:T(8,128)S(1)}, u32[]{:S(2)}, u32[]{:S(2)}) collective-permute-start(f32[4,16,512]{2,1,0:T(8,128)S(1)} %slice.55), channel_id=1, source_target_pairs={{4,0},{5,1},{6,2},{7,3}} | collective-permute-start | bytes 393224 | tf_op jit(solution)/shard_map/ppermute | solution.py:344
  8.8 29.0 %all-to-all-start = ((f32[64,8,256]{2,1,0:T(8,128)}), f32[64,8,256]{2,1,0:T(8,128)S(1)}, u32[]{:S(2)}, u32[]{:S(2)}) async-start(f32[64,8,256]{2,1,0:T(8,128)} %dynamic-slice_bitcast_fusion), calls=%async_computation | async-start | bytes 1048576 | tf_op jit(solution)/shard_map/all_to_all | solution.py:352
  17.3 20.5 %copy-start.4 = (s32[4]{0:T(128)S(1)}, s32[4]{0:T(128)}, u32[]{:S(2)}) copy-start(s32[4]{0:T(128)} %rows_ref.3) | copy-start | bytes 52
  17.4 8.1 %collective-permute-start.5 = (f32[80,256]{1,0:T(8,128)S(1)}, f32[80,256]{1,0:T(8,128)S(1)}, u32[]{:S(2)}, u32[]{:S(2)}) collective-permute-start(f32[80,256]{1,0:T(8,128)S(1)} %get-tuple-element.34), channel_id=1, source_target_pairs={{0,128},{4,132},{1,129},{5,133},{2,130},{6,134},{3,131},{7,135}} | collective-permute-start | bytes 245768 | tf_op jit(solution)/shard_map/ppermute | solution.py:292
  22.3 3.4 %collective-permute-start.6 = (f32[80,256]{1,0:T(8,128)S(1)}, f32[80,256]{1,0:T(8,128)S(1)}, u32[]{:S(2)}, u32[]{:S(2)}) collective-permute-start(f32[80,256]{1,0:T(8,128)S(1)} %get-tuple-element.35), channel_id=1, source_target_pairs={{0,192},{4,196},{1,193},{5,197},{2,194},{6,198},{3,195},{7,199}} | collective-permute-start | bytes 245768 | tf_op jit(solution)/shard_map/ppermute | solution.py:292
  23.6 5.3 %collective-permute-start.4 = (f32[80,256]{1,0:T(8,128)S(1)}, f32[80,256]{1,0:T(8,128)S(1)}, u32[]{:S(2)}, u32[]{:S(2)}) collective-permute-start(f32[80,256]{1,0:T(8,128)S(1)} %get-tuple-element.36), channel_id=1, source_target_pairs={{0,64},{4,68},{1,65},{5,69},{2,66},{6,70},{3,67},{7,71}} | collective-permute-start | bytes 245768 | tf_op jit(solution)/shard_map/ppermute | solution.py:292
  28.9 3.9 %collective-permute-start.9 = (f32[80,256]{1,0:T(8,128)S(1)}, f32[80,256]{1,0:T(8,128)S(1)}, u32[]{:S(2)}, u32[]{:S(2)}) collective-permute-start(f32[80,256]{1,0:T(8,128)S(1)} %fusion.1), channel_id=1, source_target_pairs={{0,48},{4,52},{64,112},{68,116},{128,176},{132,180},{192,240},{196... | collective-permute-start | bytes 245768 | tf_op jit(solution)/shard_map/ppermute | solution.py:292
  30.2 2.8 %collective-permute-start.8 = (f32[80,256]{1,0:T(8,128)S(1)}, f32[80,256]{1,0:T(8,128)S(1)}, u32[]{:S(2)}, u32[]{:S(2)}) collective-permute-start(f32[80,256]{1,0:T(8,128)S(1)} %fusion.1), channel_id=1, source_target_pairs={{0,32},{4,36},{64,96},{68,100},{128,160},{132,164},{192,224},{196,... | collective-permute-start | bytes 245768 | tf_op jit(solution)/shard_map/ppermute | solution.py:292
  31.5 3.4 %collective-permute-start.7 = (f32[80,256]{1,0:T(8,128)S(1)}, f32[80,256]{1,0:T(8,128)S(1)}, u32[]{:S(2)}, u32[]{:S(2)}) collective-permute-start(f32[80,256]{1,0:T(8,128)S(1)} %fusion.1), channel_id=1, source_target_pairs={{0,16},{4,20},{64,80},{68,84},{128,144},{132,148},{192,208},{196,2... | collective-permute-start | bytes 245768 | tf_op jit(solution)/shard_map/ppermute | solution.py:292
  35.0 2.8 %collective-permute-start.10 = (f32[80,256]{1,0:T(8,128)S(1)}, f32[80,256]{1,0:T(8,128)S(1)}, u32[]{:S(2)}, u32[]{:S(2)}) collective-permute-start(f32[80,256]{1,0:T(8,128)S(1)} %add_add_fusion), channel_id=1, source_target_pairs={{0,8},{4,12},{16,24},{20,28},{32,40},{36,44},{48,56},{52,60},{64,7... | collective-permute-start | bytes 245768 | tf_op jit(solution)/shard_map/ppermute | solution.py:292
  38.4 8.5 %collective-permute-start.13 = (f32[80,256]{1,0:T(8,128)S(1)}, f32[80,256]{1,0:T(8,128)S(1)}, u32[]{:S(2)}, u32[]{:S(2)}) collective-permute-start(f32[80,256]{1,0:T(8,128)S(1)} %add.56), channel_id=1, source_target_pairs={{0,192},{4,196},{8,200},{12,204},{16,208},{20,212},{24,216},{28,22... | collective-permute-start | bytes 245768 | tf_op jit(solution)/shard_map/ppermute | solution.py:292
  39.3 8.7 %collective-permute-start.12 = (f32[80,256]{1,0:T(8,128)S(1)}, f32[80,256]{1,0:T(8,128)S(1)}, u32[]{:S(2)}, u32[]{:S(2)}) collective-permute-start(f32[80,256]{1,0:T(8,128)S(1)} %add.56), channel_id=1, source_target_pairs={{0,128},{4,132},{8,136},{12,140},{16,144},{20,148},{24,152},{28,15... | collective-permute-start | bytes 245768 | tf_op jit(solution)/shard_map/ppermute | solution.py:292
  43.0 5.1 %collective-permute-start.11 = (f32[80,256]{1,0:T(8,128)S(1)}, f32[80,256]{1,0:T(8,128)S(1)}, u32[]{:S(2)}, u32[]{:S(2)}) collective-permute-start(f32[80,256]{1,0:T(8,128)S(1)} %add.56), channel_id=1, source_target_pairs={{0,64},{4,68},{8,72},{12,76},{16,80},{20,84},{24,88},{28,92},{32,9... | collective-permute-start | bytes 245768 | tf_op jit(solution)/shard_map/ppermute | solution.py:292
  43.0 5.2 %collective-permute-start = (f32[8,256]{1,0:T(8,128)S(1)}, f32[8,256]{1,0:T(8,128)S(1)}, u32[]{:S(2)}, u32[]{:S(2)}) collective-permute-start(f32[8,256]{1,0:T(8,128)S(1)} %get-tuple-element.18), channel_id=1, source_target_pairs={{0,1},{1,2},{2,3},{3,0},{4,5},{5,6},{6,7},{7,4},{8,9},{9,10},{10,1... | collective-permute-start | bytes 24584 | tf_op jit(solution)/shard_map/ppermute | solution.py:324
  44.3 4.0 %collective-permute-start.1 = (f32[8,256]{1,0:T(8,128)S(1)}, f32[8,256]{1,0:T(8,128)S(1)}, u32[]{:S(2)}, u32[]{:S(2)}) collective-permute-start(f32[8,256]{1,0:T(8,128)S(1)} %get-tuple-element.19), channel_id=1, source_target_pairs={{0,2},{1,3},{2,0},{3,1},{4,6},{5,7},{6,4},{7,5},{8,10},{9,11},{10,... | collective-permute-start | bytes 24584 | tf_op jit(solution)/shard_map/ppermute | solution.py:324
  46.9 2.8 %collective-permute-start.2 = (f32[8,256]{1,0:T(8,128)S(1)}, f32[8,256]{1,0:T(8,128)S(1)}, u32[]{:S(2)}, u32[]{:S(2)}) collective-permute-start(f32[8,256]{1,0:T(8,128)S(1)} %get-tuple-element.20), channel_id=1, source_target_pairs={{0,3},{1,0},{2,1},{3,2},{4,7},{5,4},{6,5},{7,6},{8,11},{9,8},{10,9... | collective-permute-start | bytes 24584 | tf_op jit(solution)/shard_map/ppermute | solution.py:324
  49.7 12.4 %collective-permute-start.16 = (f32[4,80,256]{2,1,0:T(8,128)S(1)}, f32[4,80,256]{2,1,0:T(8,128)S(1)}, u32[]{:S(2)}, u32[]{:S(2)}) collective-permute-start(f32[4,80,256]{2,1,0:T(8,128)S(1)} %pad_maximum_fusion.1), channel_id=1, source_target_pairs={{0,3},{1,0},{2,1},{3,2},{4,7},{5,4},{6,5},{7,6},{8,11},{9,8},{10,9... | collective-permute-start | bytes 983048 | tf_op jit(solution)/shard_map/ppermute | solution.py:324
  51.7 10.4 %collective-permute-start.15 = (f32[4,80,256]{2,1,0:T(8,128)S(1)}, f32[4,80,256]{2,1,0:T(8,128)S(1)}, u32[]{:S(2)}, u32[]{:S(2)}) collective-permute-start(f32[4,80,256]{2,1,0:T(8,128)S(1)} %pad_maximum_fusion.1), channel_id=1, source_target_pairs={{0,2},{1,3},{2,0},{3,1},{4,6},{5,7},{6,4},{7,5},{8,10},{9,11},{10,... | collective-permute-start | bytes 983048 | tf_op jit(solution)/shard_map/ppermute | solution.py:324
  51.7 16.6 %collective-permute-start.14 = (f32[4,80,256]{2,1,0:T(8,128)S(1)}, f32[4,80,256]{2,1,0:T(8,128)S(1)}, u32[]{:S(2)}, u32[]{:S(2)}) collective-permute-start(f32[4,80,256]{2,1,0:T(8,128)S(1)} %pad_maximum_fusion.1), channel_id=1, source_target_pairs={{0,1},{1,2},{2,3},{3,0},{4,5},{5,6},{6,7},{7,4},{8,9},{9,10},{10,1... | collective-permute-start | bytes 983048 | tf_op jit(solution)/shard_map/ppermute | solution.py:324
  53.3 36.5 %all-to-all-start.1 = ((f32[32,8,1024]{2,1,0:T(8,128)}), f32[32,8,1024]{2,1,0:T(8,128)}, u32[]{:S(2)}, u32[]{:S(2)}) async-start(f32[32,8,1024]{2,1,0:T(8,128)} %shard_map.60), calls=%async_computation.1 | async-start | bytes 2097152 | tf_op jit(solution)/shard_map/all_to_all | solution.py:361
  68.4 4.7 %collective-permute-start.17 = (f32[4,4,80,256]{3,2,1,0:T(8,128)S(1)}, f32[4,4,80,256]{3,2,1,0:T(8,128)S(1)}, u32[]{:S(2)}, u32[]{:S(2)}) collective-permute-start(f32[4,4,80,256]{3,2,1,0:T(8,128)S(1)} %pad_maximum_fusion.own_ref), channel_id=1, source_target_pairs={{0,4},{4,0},{8,12},{12,8},{16,20},{20,16},{24,28},{28,24},{32,36},... | collective-permute-start | bytes 3932168 | tf_op jit(solution)/shard_map/ppermute | solution.py:292
  88.1 0.7 copy-start.2
  88.8 1.1 copy-start.5
  89.8 16.4 %copy-start = (f32[1024,512]{1,0:T(8,128)}, f32[1024,512]{1,0:T(8,128)S(1)}, u32[]{:S(2)}) copy-start(f32[1024,512]{1,0:T(8,128)S(1)} %get-tuple-element.27.f0_ref) | copy-start | bytes 6291460
  89.9 18.1 %collective-permute-start.18 = (f32[32,8,1024]{2,1,0:T(8,128)}, f32[32,8,1024]{2,1,0:T(8,128)S(1)}, u32[]{:S(2)}, u32[]{:S(2)}) collective-permute-start(f32[32,8,1024]{2,1,0:T(8,128)} %all-to-all-done.1.own_ref), channel_id=1, source_target_pairs={{0,4},{4,0},{8,12},{12,8},{16,20},{20,16},{24,28},{28,24},{32,36},... | collective-permute-start | bytes 3145736 | tf_op jit(solution)/shard_map/ppermute | solution.py:292
  90.8 1.3 %copy-start.6 = (f32[4,4,80,256]{3,2,1,0:T(8,128)S(1)}, f32[4,4,80,256]{3,2,1,0:T(8,128)}, u32[]{:S(2)}) copy-start(f32[4,4,80,256]{3,2,1,0:T(8,128)} %copy-done.5) | copy-start | bytes 3932164
  106.2 1.0 copy-start.1
  107.3 0.7 copy-start.3
  108.0 1.0 copy-start.7

commit v7 on v6

--- a/solution.py
+++ b/solution.py
@@ -12,6 +12,7 @@
 NB = 128
 H = B // 2
 COST = 35 * 10**8
+LAST = 44
 NX, NZ, NY = 4, 8, 4
 CONTRACT = (((1,), (1,)), ((), ()))
 
@@ -147,38 +148,42 @@
     return row // (2 * NZ), lax.axis_index("cols"), lax.rem(row, 2)
 
 
-def place(own_ref, other_ref, m_ref):
+def place(own_ref, other_ref, where):
     x, y, mine = coords()
     for dy in range(NY):
         for dx in range(NX):
             row = lax.rem(y - dy + NY, NY) * 64 + lax.rem(x - dx + NX, NX) * 16
-            for b in range(5):
-                at = pl.ds(pl.multiple_of(row + b * H, 16), 16)
-                m_ref[mine, at, :] = own_ref[dy, dx, b * 16 : (b + 1) * 16]
-                m_ref[1 - mine, at, :] = other_ref[dy, dx, b * 16 : (b + 1) * 16]
-
-
-def kernel_a(own_ref, other_ref, f_ref, dinv_ref, m_ref, a_ref, d_ref):
-    place(own_ref, other_ref, m_ref)
-    a_ref[:H, :H] = m_ref[0, :H, :]
+
+            def put(src_ref, core):
+                for b, spot in enumerate(where[core]):
+                    if spot is not None:
+                        ref, r, c = spot
+                        at = pl.ds(pl.multiple_of(row + r, 16), 16)
+                        ref[at, c : c + H] = src_ref[dy, dx, b * 16 : (b + 1) * 16]
+
+            @pl.when(mine == 0)
+            def _():
+                put(own_ref, 0)
+                put(other_ref, 1)
+
+            @pl.when(mine == 1)
+            def _():
+                put(own_ref, 1)
+                put(other_ref, 0)
+
+
+def kernel_a(own_ref, other_ref, f_ref, dinv_ref, e_ref, a_ref, d_ref):
     a_ref[:H, H:] = jnp.zeros((H, H), F32)
-    a_ref[H:B, :H] = m_ref[0, H : 2 * H, :]
-    a_ref[H:B, H:] = m_ref[0, 2 * H : 3 * H, :]
-    for i in range(2):
-        for j in range(2):
-            o = (2 * i + j) * H
-            a_ref[B + i * H : B + (i + 1) * H, j * H : (j + 1) * H] = m_ref[1, o : o + H, :]
+    e_ref[:H, H:] = jnp.zeros((H, H), F32)
+    first = [(a_ref, 0, 0), (a_ref, H, 0), (a_ref, H, H), (e_ref, H, 0), (e_ref, H, H)]
+    second = [(a_ref, B, 0), (a_ref, B, H), (a_ref, B + H, 0), (a_ref, B + H, H), (e_ref, 0, 0)]
+    place(own_ref, other_ref, [first, second])
     tall_factor(a_ref, f_ref, dinv_ref, d_ref)
 
 
-def kernel_b(own_ref, other_ref, f0_ref, f1_ref, dinv_ref, m_ref, a_ref, d_ref):
-    place(own_ref, other_ref, m_ref)
-    a_ref[:H, :H] = m_ref[1, 4 * H :, :]
-    a_ref[:H, H:] = jnp.zeros((H, H), F32)
-    a_ref[H:, :H] = m_ref[0, 3 * H : 4 * H, :]
-    a_ref[H:, H:] = m_ref[0, 4 * H :, :]
+def kernel_b(e_ref, f0_ref, f1_ref, dinv_ref, a_ref, d_ref):
     low = f0_ref[B:, :]
-    a_ref[...] = a_ref[...] - mul_t(low, low)
+    a_ref[...] = e_ref[...] - mul_t(low, low)
     tall_factor(a_ref, f1_ref, dinv_ref, d_ref)
 
 
@@ -199,19 +204,31 @@
             s_ref[:, e:] = s_ref[:, e:] - mul_t(X, f_ref[p + H :, p : p + H])
 
 
-def kernel_c(live_ref, rows_ref, own_ref, other_ref, f0_ref, f1_ref, d0_ref, d1_ref, panel_ref, window_ref, factor_ref, out_ref, s_ref):
+def kernel_c(
+    live_ref, rows_ref, f0_ref, f1_ref, d0_ref, d1_ref, own_hbm, other_hbm, panel_hbm, window_hbm,
+    out_ref, factor_hbm, s_ref, t_ref, window_ref, sems,
+):
     row = lax.axis_index("rows")
     _, y, mine = coords()
-    live_t = live_ref[rows_ref[y]].astype(F32)
-    live = jnp.where(row < 2, 1, live_ref[row]).astype(F32)
-    s_ref[:B, :] = panel_ref[...] * live
-    for j in range(NX * NZ):
-        s_ref[pl.ds(pl.multiple_of(B + (2 * j + mine) * 8, 8), 8), :] = own_ref[j] * live_t
-        s_ref[pl.ds(pl.multiple_of(B + (2 * j + 1 - mine) * 8, 8), 8), :] = other_ref[j] * live_t
+    panel_in = pltpu.make_async_copy(panel_hbm, s_ref.at[pl.ds(0, B)], sems.at[0])
+    own_in = pltpu.make_async_copy(own_hbm, t_ref.at[0], sems.at[1])
+    other_in = pltpu.make_async_copy(other_hbm, t_ref.at[1], sems.at[2])
+    window_in = pltpu.make_async_copy(window_hbm, window_ref, sems.at[3])
+    for c in (panel_in, own_in, other_in, window_in):
+        c.start()
     inv = []
     for k in range(4):
         f_ref, d_ref, p = (f0_ref, d0_ref, k * H) if k < 2 else (f1_ref, d1_ref, k * H - B)
         inv.append(pair_inverse(d_ref, 2 * (k % 2), f_ref[p + NB : p + H, p : p + NB]))
+    live_t = live_ref[rows_ref[y]].astype(F32)
+    live = jnp.where(row < 2, 1, live_ref[row]).astype(F32)
+    panel_in.wait()
+    s_ref[:B, :] = s_ref[:B, :] * live
+    own_in.wait()
+    other_in.wait()
+    for j in range(NX * NZ):
+        s_ref[pl.ds(pl.multiple_of(B + (2 * j + mine) * 8, 8), 8), :] = t_ref[0, j] * live_t
+        s_ref[pl.ds(pl.multiple_of(B + (2 * j + 1 - mine) * 8, 8), 8), :] = t_ref[1, j] * live_t
     solve_rows(s_ref, lambda k: inv[k], f0_ref, f1_ref)
 
     @pl.when(row == 0)
@@ -224,8 +241,11 @@
         s_ref[:B, :B] = f0_ref[B:, :]
         s_ref[:B, B:] = f1_ref[...]
 
-    factor_ref[...] = s_ref[:B, :]
+    factor_out = pltpu.make_async_copy(s_ref.at[pl.ds(0, B)], factor_hbm, sems.at[4])
+    factor_out.start()
+    window_in.wait()
     out_ref[...] = window_ref[...] - mul_t(s_ref[:B, :], s_ref[B:, :])
+    factor_out.wait()
 
 
 def kernel_pick(rows_ref, parts_ref, *refs):
@@ -266,6 +286,24 @@
     )(*args)
 
 
+def last(row_live, window_rows, f0, f1, d0, d1, t_own, t_other, panel, window_block):
+    hbm = pl.BlockSpec(memory_space=pltpu.HBM)
+    updated, factor = pl.pallas_call(
+        kernel_c,
+        out_shape=[jax.ShapeDtypeStruct((B, B), F32), jax.ShapeDtypeStruct((B, 2 * B), F32)],
+        in_specs=[SMEM] * 2 + [VM] * 4 + [hbm] * 4,
+        out_specs=[VM, hbm],
+        scratch_shapes=[
+            pltpu.VMEM((2 * B, 2 * B), F32),
+            pltpu.VMEM((2,) + t_own.shape, F32),
+            pltpu.VMEM((B, B), F32),
+            pltpu.SemaphoreType.DMA((5,)),
+        ],
+        compiler_params=pltpu.CompilerParams(vmem_limit_bytes=LAST << 20),
+    )(row_live, window_rows, f0, f1, d0, d1, t_own, t_other, panel, window_block)
+    return factor, updated
+
+
 def pick(window_rows, parts):
     return pl.pallas_call(
         kernel_pick,
@@ -354,19 +392,16 @@
     quarters = [chosen[0]] + [by_y(chosen[d], d) for d in range(1, NY)]
     part = jnp.stack([piece] + [by_x(piece, d) for d in range(1, NX)])
 
-    own = gather_y(after(part, *quarters[1:]))
+    own = gather_y(part)
     other = swap_core(own)
     quarters = after(quarters, part)
     (fan,) = call(kernel_fan, 10**6, 8, [(NX * NZ, 8, 2 * B)], [], *quarters)
     t_own = lax.all_to_all(fan, "rows", 0, 0, axis_index_groups=GROUPS)
 
-    f0, d0 = call(kernel_a, COST, 24, [(2 * B, B), (4, NB, NB)], [(2, 5 * H, H), (2 * B, B), (NB, NB)], own, other)
+    f0, d0, e = call(kernel_a, COST, 24, [(2 * B, B), (4, NB, NB), (B, B)], [(2 * B, B), (NB, NB)], own, other)
     t_other = swap_core(after(t_own, f0))
-    f1, d1 = call(kernel_b, COST, 20, [(B, B), (4, NB, NB)], [(2, 5 * H, H), (B, B), (NB, NB)], own, other, f0)
-    return call(
-        kernel_c, 10**8, 60, [(B, 2 * B), (B, B)], [(2 * B, 2 * B)],
-        row_live, window_rows, t_own, t_other, f0, f1, d0, d1, panel, window_block,
-    )
+    f1, d1 = call(kernel_b, COST, 20, [(B, B), (4, NB, NB)], [(B, B), (NB, NB)], e, f0)
+    return last(row_live, window_rows, f0, f1, d0, d1, t_own, t_other, panel, window_block)
 
 
 def solution(mesh):

time: 125 us -> 137 us (1.096)
  waiting for transfers between devices: 18 us -> 34.6 us
  local copies, waits for them, and re-layouts: 8.76 us -> 5.19 us
  Pallas kernels: 45.6 us -> 42.8 us
  starting transfers between devices: 50.3 us -> 52 us
    pallas_call x4 -> x3, Pallas kernels: 44.9 us -> 30.2 us  [call(): pl.pallas_call(kernel, out_shape=[jax.ShapeDtypeStruct(s, F32) for s in o...]
    pallas_call x0 -> x1, Pallas kernels: none -> 11.9 us  [last(): pl.pallas_call(kernel_c, out_shape=[jax.ShapeDtypeStruct((B, B), F32), ja...]
    ppermute x6, waiting for transfers between devices: 7.69 us -> 16.5 us  [by_y(): return lax.ppermute(v, 'cols', [(i, (i + d) % NY) for i in range(NY)])]
    ppermute x12, waiting for transfers between devices: 10.3 us -> 15.3 us  [move(): return lax.ppermute(v, 'rows', pairs)]
    ppermute x12, starting transfers between devices: 20.3 us -> 25.1 us  [move(): return lax.ppermute(v, 'rows', pairs)]
    unnamed x17 -> x13, local copies, waits for them, and re-layouts: 5.79 us -> 2.21 us
    all_to_all x1, waiting for transfers between devices: 0.01 us -> 2.83 us  [shards(): t_own = lax.all_to_all(fan, 'rows', 0, 0, axis_index_groups=GROUPS)]
    all_to_all x1, starting transfers between devices: 8.81 us -> 6.26 us  [shards(): t_own = lax.all_to_all(fan, 'rows', 0, 0, axis_index_groups=GROUPS)]
  transfers between devices with their start and end apart: 21 -> 21, of which waited for: 11 -> 12; matrix products, arithmetic and copies ran while one was open for 2% -> 2% of each run, Pallas kernels for 24% -> 22%
where the time goes in v7:
time: 137 us; the launch traced here: 136 us
  starting transfers between devices  52 us (38%)
  Pallas kernels  42.8 us (31%)
  waiting for transfers between devices  34.6 us (25%)
  local copies, waits for them, and re-layouts  5.19 us (4%)
    pallas_call x3, Pallas kernels, call(): pl.pallas_call(kernel, out_shape=[jax.ShapeDtypeStruct(s, F32) for s in o...  30.2 us
    ppermute x12, starting transfers between devices, move(): return lax.ppermute(v, 'rows', pairs)  25.1 us
    ppermute x6, waiting for transfers between devices, by_y(): return lax.ppermute(v, 'cols', [(i, (i + d) % NY) for i in range(NY)])  16.5 us
    ppermute x12, waiting for transfers between devices, move(): return lax.ppermute(v, 'rows', pairs)  15.3 us
    pallas_call x1, Pallas kernels, last(): pl.pallas_call(kernel_c, out_shape=[jax.ShapeDtypeStruct((B, B), F32), ja...  11.9 us
    all_to_all x1, starting transfers between devices, shards(): chosen = pick(window_rows, lax.all_to_all(mine, 'rows', 0, 0))  8.5 us
    ppermute x6, starting transfers between devices, by_y(): return lax.ppermute(v, 'cols', [(i, (i + d) % NY) for i in range(NY)])  7.02 us
    all_to_all x1, starting transfers between devices, shards(): t_own = lax.all_to_all(fan, 'rows', 0, 0, axis_index_groups=GROUPS)  6.26 us
  transfers between devices with their start and end apart: 21, of which 12 were waited for; matrix products, arithmetic and copies ran while one was open for 2% of the time, Pallas kernels for 22%

profile of v7, /device:TPU:1, one launch (start us, length us, event | category | flops | bytes accessed | tf_op | source)
XLA Modules:
  0.0 136.0 jit_solution(13109263587075873004)
XLA Ops:
  0.6 1.1 constant_dynamic-slice_fusion
  1.7 5.2 %collective-permute-start = (f32[4,16,512]{2,1,0:T(8,128)S(1)}, f32[4,16,512]{2,1,0:T(8,128)S(1)}, u32[]{:S(2)}, u32[]{:S(2)}) collective-permute-start(f32[4,16,512]{2,1,0:T(8,128)S(1)} %slice.55), channel_id=1, source_target_pairs={{4,0},{5,1},{6,2},{7,3}} | collective-permute-start | bytes 393224 | tf_op jit(solution)/shard_map/ppermute | solution.py:382
  6.9 1.9 %dynamic-slice_bitcast_fusion = f32[64,8,256]{2,1,0:T(8,128)} fusion(f32[512,1024]{1,0:T(8,128)} %panel_hbm.1, s32[]{:T(128)S(6)} %select_n.74), kind=kLoop, calls=%fused_computation.1 | loop fusion | bytes 1048580 | tf_op jit(solution)/shard_map/reshape | solution.py:389
  8.8 8.5 %all-to-all-start = ((f32[64,8,256]{2,1,0:T(8,128)}), f32[64,8,256]{2,1,0:T(8,128)S(1)}, u32[]{:S(2)}, u32[]{:S(2)}) async-start(f32[64,8,256]{2,1,0:T(8,128)} %dynamic-slice_bitcast_fusion), calls=%async_computation | async-start | bytes 1048576 | tf_op jit(solution)/shard_map/all_to_all | solution.py:390
  17.4 4.9 %collective-permute-start.2 = (f32[80,256]{1,0:T(8,128)S(1)}, f32[80,256]{1,0:T(8,128)S(1)}, u32[]{:S(2)}, u32[]{:S(2)}) collective-permute-start(f32[80,256]{1,0:T(8,128)S(1)} %get-tuple-element.40), channel_id=1, source_target_pairs={{0,128},{4,132},{1,129},{5,133},{2,130},{6,134},{3,131},{7,135}} | collective-permute-start | bytes 245768 | tf_op jit(solution)/shard_map/ppermute | solution.py:330
  22.3 1.3 collective-permute-start.3
  23.6 1.3 collective-permute-start.1
  25.7 3.2 %collective-permute-done.1 = f32[80,256]{1,0:T(8,128)S(1)} collective-permute-done((f32[80,256]{1,0:T(8,128)S(1)}, f32[80,256]{1,0:T(8,128)S(1)}, u32[]{:S(2)}, u32[]{:S(2)}) %collective-permute-start.1) | collective-permute-done | bytes 81952 | tf_op jit(solution)/shard_map/ppermute | solution.py:330
  28.9 1.3 collective-permute-start.6
  30.2 1.3 collective-permute-start.5
  31.5 1.3 collective-permute-start.4
  33.0 2.0 %collective-permute-done.4 = f32[80,256]{1,0:T(8,128)S(1)} collective-permute-done((f32[80,256]{1,0:T(8,128)S(1)}, f32[80,256]{1,0:T(8,128)S(1)}, u32[]{:S(2)}, u32[]{:S(2)}) %collective-permute-start.4) | collective-permute-done | bytes 81952 | tf_op jit(solution)/shard_map/ppermute | solution.py:330
  35.0 1.3 collective-permute-start.7
  36.3 1.5 %collective-permute-done.7 = f32[80,256]{1,0:T(8,128)S(1)} collective-permute-done((f32[80,256]{1,0:T(8,128)S(1)}, f32[80,256]{1,0:T(8,128)S(1)}, u32[]{:S(2)}, u32[]{:S(2)}) %collective-permute-start.7) | collective-permute-done | bytes 81952 | tf_op jit(solution)/shard_map/ppermute | solution.py:330
  39.3 3.7 %collective-permute-start.9 = (f32[80,256]{1,0:T(8,128)S(1)}, f32[80,256]{1,0:T(8,128)S(1)}, u32[]{:S(2)}, u32[]{:S(2)}) collective-permute-start(f32[80,256]{1,0:T(8,128)S(1)} %add.55), channel_id=1, source_target_pairs={{0,128},{4,132},{8,136},{12,140},{16,144},{20,148},{24,152},{28,15... | collective-permute-start | bytes 245768 | tf_op jit(solution)/shard_map/ppermute | solution.py:330
  43.0 1.8 %collective-permute-done.9 = f32[80,256]{1,0:T(8,128)S(1)} collective-permute-done((f32[80,256]{1,0:T(8,128)S(1)}, f32[80,256]{1,0:T(8,128)S(1)}, u32[]{:S(2)}, u32[]{:S(2)}) %collective-permute-start.9) | collective-permute-done | bytes 81952 | tf_op jit(solution)/shard_map/ppermute | solution.py:330
  44.8 3.3 %collective-permute-done.8 = f32[80,256]{1,0:T(8,128)S(1)} collective-permute-done((f32[80,256]{1,0:T(8,128)S(1)}, f32[80,256]{1,0:T(8,128)S(1)}, u32[]{:S(2)}, u32[]{:S(2)}) %collective-permute-start.8) | collective-permute-done | bytes 81952 | tf_op jit(solution)/shard_map/ppermute | solution.py:330
  48.2 2.8 %collective-permute-start.13 = (f32[4,80,256]{2,1,0:T(8,128)S(1)}, f32[4,80,256]{2,1,0:T(8,128)S(1)}, u32[]{:S(2)}, u32[]{:S(2)}) collective-permute-start(f32[4,80,256]{2,1,0:T(8,128)S(1)} %get-tuple-element.39), channel_id=1, source_target_pairs={{0,3},{1,0},{2,1},{3,2},{4,7},{5,4},{6,5},{7,6},{8,11},{9,8},{10,9... | collective-permute-start | bytes 983048 | tf_op jit(solution)/shard_map/ppermute | solution.py:362
  52.1 1.6 %collective-permute-start.15 = (f32[8,256]{1,0:T(8,128)S(1)}, f32[8,256]{1,0:T(8,128)S(1)}, u32[]{:S(2)}, u32[]{:S(2)}) collective-permute-start(f32[8,256]{1,0:T(8,128)S(1)} %get-tuple-element.20), channel_id=1, source_target_pairs={{0,1},{1,2},{2,3},{3,0},{4,5},{5,6},{6,7},{7,4},{8,9},{9,10},{10,1... | collective-permute-start | bytes 24584 | tf_op jit(solution)/shard_map/ppermute | solution.py:362
  53.7 1.6 %collective-permute-start.16 = (f32[8,256]{1,0:T(8,128)S(1)}, f32[8,256]{1,0:T(8,128)S(1)}, u32[]{:S(2)}, u32[]{:S(2)}) collective-permute-start(f32[8,256]{1,0:T(8,128)S(1)} %get-tuple-element.21), channel_id=1, source_target_pairs={{0,2},{1,3},{2,0},{3,1},{4,6},{5,7},{6,4},{7,5},{8,10},{9,11},{10,... | collective-permute-start | bytes 24584 | tf_op jit(solution)/shard_map/ppermute | solution.py:362
  55.2 14.0 %collective-permute-done.15.q1_ref = f32[8,256]{1,0:T(8,128)S(1)} collective-permute-done((f32[8,256]{1,0:T(8,128)S(1)}, f32[8,256]{1,0:T(8,128)S(1)}, u32[]{:S(2)}, u32[]{:S(2)}) %collective-permute-start.15) | collective-permute-done | bytes 8224 | tf_op jit(solution)/shard_map/ppermute | solution.py:362
  69.2 2.5 %collective-permute-done.17.q3_ref = f32[8,256]{1,0:T(8,128)S(1)} collective-permute-done((f32[8,256]{1,0:T(8,128)S(1)}, f32[8,256]{1,0:T(8,128)S(1)}, u32[]{:S(2)}, u32[]{:S(2)}) %collective-permute-start.17) | collective-permute-done | bytes 8224 | tf_op jit(solution)/shard_map/ppermute | solution.py:362
  71.7 1.0 shard_map.62
  72.8 6.3 %all-to-all-start.1 = ((f32[32,8,1024]{2,1,0:T(8,128)}), f32[32,8,1024]{2,1,0:T(8,128)S(1)}, u32[]{:S(2)}, u32[]{:S(2)}) async-start(f32[32,8,1024]{2,1,0:T(8,128)} %shard_map.62), calls=%async_computation.1 | async-start | bytes 2097152 | tf_op jit(solution)/shard_map/all_to_all | solution.py:399
  79.2 2.4 %collective-permute-start.14 = (f32[4,4,80,256]{3,2,1,0:T(8,128)S(1)}, f32[4,4,80,256]{3,2,1,0:T(8,128)S(1)}, u32[]{:S(2)}, u32[]{:S(2)}) collective-permute-start(f32[4,4,80,256]{3,2,1,0:T(8,128)S(1)} %pad_maximum_fusion.own_ref), channel_id=1, source_target_pairs={{0,4},{4,0},{8,12},{12,8},{16,20},{20,16},{24,28},{28,24},{32,36},... | collective-permute-start | bytes 3932168 | tf_op jit(solution)/shard_map/ppermute | solution.py:330
  81.6 2.7 %collective-permute-done.14.other_ref = f32[4,4,80,256]{3,2,1,0:T(8,128)S(1)} collective-permute-done((f32[4,4,80,256]{3,2,1,0:T(8,128)S(1)}, f32[4,4,80,256]{3,2,1,0:T(8,128)S(1)}, u32[]{:S(2)}, u32[]{:S(2)}) %collective-permute-start.14) | collective-permute-done | bytes 1310752 | tf_op jit(solution)/shard_map/ppermute | solution.py:330
  84.2 15.1 %shard_map.60 = (f32[1024,512]{1,0:T(8,128)S(1)}, f32[4,128,128]{2,1,0:T(8,128)S(1)}, f32[512,512]{1,0:T(8,128)S(1)}) custom-call(f32[4,4,80,256]{3,2,1,0:T(8,128)S(1)} %pad_maximum_fusion.own_ref, f32[4,4,80,256]{3,2,1,0:T(8,128)S(1)} %collective-permute-done.14.other_ref), custom_call_target="tpu_custom_call" | custom-call | flops 3500000000 | bytes 8388608 | tf_op jit(solution)/shard_map/pallas_call | solution.py:278
  100.4 2.8 %all-to-all-done.1.own_hbm = f32[32,8,1024]{2,1,0:T(8,128)S(1)} async-done(((f32[32,8,1024]{2,1,0:T(8,128)}), f32[32,8,1024]{2,1,0:T(8,128)S(1)}, u32[]{:S(2)}, u32[]{:S(2)}) %all-to-all-start.1) | async-done | bytes 1048608 | tf_op jit(solution)/shard_map/all_to_all | solution.py:399
  103.2 5.4 %collective-permute-start.18 = (f32[32,8,1024]{2,1,0:T(8,128)S(1)}, f32[32,8,1024]{2,1,0:T(8,128)S(1)}, u32[]{:S(2)}, u32[]{:S(2)}) collective-permute-start(f32[32,8,1024]{2,1,0:T(8,128)S(1)} %all-to-all-done.1.own_hbm), channel_id=1, source_target_pairs={{0,4},{4,0},{8,12},{12,8},{16,20},{20,16},{24,28},{28,24},{32,36},... | collective-permute-start | bytes 3145736 | tf_op jit(solution)/shard_map/ppermute | solution.py:330
  108.6 1.2 copy-done.5
  109.8 14.0 %shard_map.61 = (f32[512,512]{1,0:T(8,128)S(1)}, f32[4,128,128]{2,1,0:T(8,128)S(1)}) custom-call(f32[512,512]{1,0:T(8,128)S(1)} %copy-done.5, f32[1024,512]{1,0:T(8,128)S(1)} %get-tuple-element.24.f0_ref), custom_call_target="tpu_custom_call" | custom-call | flops 3500000000 | bytes 8388608 | tf_op jit(solution)/shard_map/pallas_call | solution.py:278
  123.9 11.9 %shard_map.63 = (f32[512,512]{1,0:T(8,128)}, f32[512,1024]{1,0:T(8,128)}) custom-call(s32[64]{0:T(128)S(1)} %copy-done.3, s32[4]{0:T(128)S(1)} %copy-done.2, f32[1024,512]{1,0:T(8,128)S(1)} %get-tuple-element.24.f0_ref, f32[512,512]{1,0:T(8,128)S(1)} %get-tuple-element.26.f1_ref, f32[4,128,128]{2,1,0:T(8,128)S(1)} %get-tuple-element.27.d0_ref, ...), custom_call_target="tpu_custom_call" | custom-call | tf_op jit(solution)/shard_map/pallas_call | solution.py:291
  (41 shorter events, 4.7 us)
Async XLA Ops:
  1.7 15.6 %collective-permute-start = (f32[4,16,512]{2,1,0:T(8,128)S(1)}, f32[4,16,512]{2,1,0:T(8,128)S(1)}, u32[]{:S(2)}, u32[]{:S(2)}) collective-permute-start(f32[4,16,512]{2,1,0:T(8,128)S(1)} %slice.55), channel_id=1, source_target_pairs={{4,0},{5,1},{6,2},{7,3}} | collective-permute-start | bytes 393224 | tf_op jit(solution)/shard_map/ppermute | solution.py:382
  8.8 29.0 %all-to-all-start = ((f32[64,8,256]{2,1,0:T(8,128)}), f32[64,8,256]{2,1,0:T(8,128)S(1)}, u32[]{:S(2)}, u32[]{:S(2)}) async-start(f32[64,8,256]{2,1,0:T(8,128)} %dynamic-slice_bitcast_fusion), calls=%async_computation | async-start | bytes 1048576 | tf_op jit(solution)/shard_map/all_to_all | solution.py:390
  17.3 20.5 %copy-start.2 = (s32[4]{0:T(128)S(1)}, s32[4]{0:T(128)}, u32[]{:S(2)}) copy-start(s32[4]{0:T(128)} %rows_ref.3) | copy-start | bytes 52
  17.4 8.1 %collective-permute-start.2 = (f32[80,256]{1,0:T(8,128)S(1)}, f32[80,256]{1,0:T(8,128)S(1)}, u32[]{:S(2)}, u32[]{:S(2)}) collective-permute-start(f32[80,256]{1,0:T(8,128)S(1)} %get-tuple-element.40), channel_id=1, source_target_pairs={{0,128},{4,132},{1,129},{5,133},{2,130},{6,134},{3,131},{7,135}} | collective-permute-start | bytes 245768 | tf_op jit(solution)/shard_map/ppermute | solution.py:330
  22.3 3.4 %collective-permute-start.3 = (f32[80,256]{1,0:T(8,128)S(1)}, f32[80,256]{1,0:T(8,128)S(1)}, u32[]{:S(2)}, u32[]{:S(2)}) collective-permute-start(f32[80,256]{1,0:T(8,128)S(1)} %get-tuple-element.41), channel_id=1, source_target_pairs={{0,192},{4,196},{1,193},{5,197},{2,194},{6,198},{3,195},{7,199}} | collective-permute-start | bytes 245768 | tf_op jit(solution)/shard_map/ppermute | solution.py:330
  23.6 5.3 %collective-permute-start.1 = (f32[80,256]{1,0:T(8,128)S(1)}, f32[80,256]{1,0:T(8,128)S(1)}, u32[]{:S(2)}, u32[]{:S(2)}) collective-permute-start(f32[80,256]{1,0:T(8,128)S(1)} %get-tuple-element.42), channel_id=1, source_target_pairs={{0,64},{4,68},{1,65},{5,69},{2,66},{6,70},{3,67},{7,71}} | collective-permute-start | bytes 245768 | tf_op jit(solution)/shard_map/ppermute | solution.py:330
  28.9 3.9 %collective-permute-start.6 = (f32[80,256]{1,0:T(8,128)S(1)}, f32[80,256]{1,0:T(8,128)S(1)}, u32[]{:S(2)}, u32[]{:S(2)}) collective-permute-start(f32[80,256]{1,0:T(8,128)S(1)} %fusion.1), channel_id=1, source_target_pairs={{0,48},{4,52},{64,112},{68,116},{128,176},{132,180},{192,240},{196... | collective-permute-start | bytes 245768 | tf_op jit(solution)/shard_map/ppermute | solution.py:330
  30.2 2.8 %collective-permute-start.5 = (f32[80,256]{1,0:T(8,128)S(1)}, f32[80,256]{1,0:T(8,128)S(1)}, u32[]{:S(2)}, u32[]{:S(2)}) collective-permute-start(f32[80,256]{1,0:T(8,128)S(1)} %fusion.1), channel_id=1, source_target_pairs={{0,32},{4,36},{64,96},{68,100},{128,160},{132,164},{192,224},{196,... | collective-permute-start | bytes 245768 | tf_op jit(solution)/shard_map/ppermute | solution.py:330
  31.5 3.4 %collective-permute-start.4 = (f32[80,256]{1,0:T(8,128)S(1)}, f32[80,256]{1,0:T(8,128)S(1)}, u32[]{:S(2)}, u32[]{:S(2)}) collective-permute-start(f32[80,256]{1,0:T(8,128)S(1)} %fusion.1), channel_id=1, source_target_pairs={{0,16},{4,20},{64,80},{68,84},{128,144},{132,148},{192,208},{196,2... | collective-permute-start | bytes 245768 | tf_op jit(solution)/shard_map/ppermute | solution.py:330
  35.0 2.8 %collective-permute-start.7 = (f32[80,256]{1,0:T(8,128)S(1)}, f32[80,256]{1,0:T(8,128)S(1)}, u32[]{:S(2)}, u32[]{:S(2)}) collective-permute-start(f32[80,256]{1,0:T(8,128)S(1)} %add_add_fusion), channel_id=1, source_target_pairs={{0,8},{4,12},{16,24},{20,28},{32,40},{36,44},{48,56},{52,60},{64,7... | collective-permute-start | bytes 245768 | tf_op jit(solution)/shard_map/ppermute | solution.py:330
  38.4 4.6 %collective-permute-start.10 = (f32[80,256]{1,0:T(8,128)S(1)}, f32[80,256]{1,0:T(8,128)S(1)}, u32[]{:S(2)}, u32[]{:S(2)}) collective-permute-start(f32[80,256]{1,0:T(8,128)S(1)} %add.55), channel_id=1, source_target_pairs={{0,192},{4,196},{8,200},{12,204},{16,208},{20,212},{24,216},{28,22... | collective-permute-start | bytes 245768 | tf_op jit(solution)/shard_map/ppermute | solution.py:330
  39.3 5.6 %collective-permute-start.9 = (f32[80,256]{1,0:T(8,128)S(1)}, f32[80,256]{1,0:T(8,128)S(1)}, u32[]{:S(2)}, u32[]{:S(2)}) collective-permute-start(f32[80,256]{1,0:T(8,128)S(1)} %add.55), channel_id=1, source_target_pairs={{0,128},{4,132},{8,136},{12,140},{16,144},{20,148},{24,152},{28,15... | collective-permute-start | bytes 245768 | tf_op jit(solution)/shard_map/ppermute | solution.py:330
  43.0 5.1 %collective-permute-start.8 = (f32[80,256]{1,0:T(8,128)S(1)}, f32[80,256]{1,0:T(8,128)S(1)}, u32[]{:S(2)}, u32[]{:S(2)}) collective-permute-start(f32[80,256]{1,0:T(8,128)S(1)} %add.55), channel_id=1, source_target_pairs={{0,64},{4,68},{8,72},{12,76},{16,80},{20,84},{24,88},{28,92},{32,9... | collective-permute-start | bytes 245768 | tf_op jit(solution)/shard_map/ppermute | solution.py:330
  48.2 30.8 %collective-permute-start.13 = (f32[4,80,256]{2,1,0:T(8,128)S(1)}, f32[4,80,256]{2,1,0:T(8,128)S(1)}, u32[]{:S(2)}, u32[]{:S(2)}) collective-permute-start(f32[4,80,256]{2,1,0:T(8,128)S(1)} %get-tuple-element.39), channel_id=1, source_target_pairs={{0,3},{1,0},{2,1},{3,2},{4,7},{5,4},{6,5},{7,6},{8,11},{9,8},{10,9... | collective-permute-start | bytes 983048 | tf_op jit(solution)/shard_map/ppermute | solution.py:362
  51.0 28.0 %collective-permute-start.12 = (f32[4,80,256]{2,1,0:T(8,128)S(1)}, f32[4,80,256]{2,1,0:T(8,128)S(1)}, u32[]{:S(2)}, u32[]{:S(2)}) collective-permute-start(f32[4,80,256]{2,1,0:T(8,128)S(1)} %get-tuple-element.39), channel_id=1, source_target_pairs={{0,2},{1,3},{2,0},{3,1},{4,6},{5,7},{6,4},{7,5},{8,10},{9,11},{10,... | collective-permute-start | bytes 983048 | tf_op jit(solution)/shard_map/ppermute | solution.py:362
  51.4 27.7 %collective-permute-start.11 = (f32[4,80,256]{2,1,0:T(8,128)S(1)}, f32[4,80,256]{2,1,0:T(8,128)S(1)}, u32[]{:S(2)}, u32[]{:S(2)}) collective-permute-start(f32[4,80,256]{2,1,0:T(8,128)S(1)} %get-tuple-element.39), channel_id=1, source_target_pairs={{0,1},{1,2},{2,3},{3,0},{4,5},{5,6},{6,7},{7,4},{8,9},{9,10},{10,1... | collective-permute-start | bytes 983048 | tf_op jit(solution)/shard_map/ppermute | solution.py:362
  52.1 17.2 %collective-permute-start.15 = (f32[8,256]{1,0:T(8,128)S(1)}, f32[8,256]{1,0:T(8,128)S(1)}, u32[]{:S(2)}, u32[]{:S(2)}) collective-permute-start(f32[8,256]{1,0:T(8,128)S(1)} %get-tuple-element.20), channel_id=1, source_target_pairs={{0,1},{1,2},{2,3},{3,0},{4,5},{5,6},{6,7},{7,4},{8,9},{9,10},{10,1... | collective-permute-start | bytes 24584 | tf_op jit(solution)/shard_map/ppermute | solution.py:362
  53.7 15.6 %collective-permute-start.16 = (f32[8,256]{1,0:T(8,128)S(1)}, f32[8,256]{1,0:T(8,128)S(1)}, u32[]{:S(2)}, u32[]{:S(2)}) collective-permute-start(f32[8,256]{1,0:T(8,128)S(1)} %get-tuple-element.21), channel_id=1, source_target_pairs={{0,2},{1,3},{2,0},{3,1},{4,6},{5,7},{6,4},{7,5},{8,10},{9,11},{10,... | collective-permute-start | bytes 24584 | tf_op jit(solution)/shard_map/ppermute | solution.py:362
  69.2 2.5 %collective-permute-start.17 = (f32[8,256]{1,0:T(8,128)S(1)}, f32[8,256]{1,0:T(8,128)S(1)}, u32[]{:S(2)}, u32[]{:S(2)}) collective-permute-start(f32[8,256]{1,0:T(8,128)S(1)} %get-tuple-element.22), channel_id=1, source_target_pairs={{0,3},{1,0},{2,1},{3,2},{4,7},{5,4},{6,5},{7,6},{8,11},{9,8},{10,9... | collective-permute-start | bytes 24584 | tf_op jit(solution)/shard_map/ppermute | solution.py:362
  72.8 30.4 %all-to-all-start.1 = ((f32[32,8,1024]{2,1,0:T(8,128)}), f32[32,8,1024]{2,1,0:T(8,128)S(1)}, u32[]{:S(2)}, u32[]{:S(2)}) async-start(f32[32,8,1024]{2,1,0:T(8,128)} %shard_map.62), calls=%async_computation.1 | async-start | bytes 2097152 | tf_op jit(solution)/shard_map/all_to_all | solution.py:399
  79.2 5.1 %collective-permute-start.14 = (f32[4,4,80,256]{3,2,1,0:T(8,128)S(1)}, f32[4,4,80,256]{3,2,1,0:T(8,128)S(1)}, u32[]{:S(2)}, u32[]{:S(2)}) collective-permute-start(f32[4,4,80,256]{3,2,1,0:T(8,128)S(1)} %pad_maximum_fusion.own_ref), channel_id=1, source_target_pairs={{0,4},{4,0},{8,12},{12,8},{16,20},{20,16},{24,28},{28,24},{32,36},... | collective-permute-start | bytes 3932168 | tf_op jit(solution)/shard_map/ppermute | solution.py:330
  99.4 1.0 copy-start.4
  103.2 20.7 %collective-permute-start.18 = (f32[32,8,1024]{2,1,0:T(8,128)S(1)}, f32[32,8,1024]{2,1,0:T(8,128)S(1)}, u32[]{:S(2)}, u32[]{:S(2)}) collective-permute-start(f32[32,8,1024]{2,1,0:T(8,128)S(1)} %all-to-all-done.1.own_hbm), channel_id=1, source_target_pairs={{0,4},{4,0},{8,12},{12,8},{16,20},{20,16},{24,28},{28,24},{32,36},... | collective-permute-start | bytes 3145736 | tf_op jit(solution)/shard_map/ppermute | solution.py:330
  108.6 1.2 copy-start.5
  109.8 14.1 %copy-start = (f32[512,1024]{1,0:T(8,128)S(1)}, f32[512,1024]{1,0:T(8,128)}, u32[]{:S(2)}) copy-start(f32[512,1024]{1,0:T(8,128)} %panel_hbm.1) | copy-start | bytes 6291460
  109.8 14.1 %copy-start.1 = (f32[512,512]{1,0:T(8,128)S(1)}, f32[512,512]{1,0:T(8,128)}, u32[]{:S(2)}) copy-start(f32[512,512]{1,0:T(8,128)} %window_hbm.1) | copy-start | bytes 3145732
  109.8 14.1 %copy-start.3 = (s32[64]{0:T(128)S(1)}, s32[64]{0:T(128)}, u32[]{:S(2)}) copy-start(s32[64]{0:T(128)} %live_ref.1) | copy-start | bytes 772

commit v8 on v7

--- a/solution.py
+++ b/solution.py
@@ -392,7 +392,7 @@
     quarters = [chosen[0]] + [by_y(chosen[d], d) for d in range(1, NY)]
     part = jnp.stack([piece] + [by_x(piece, d) for d in range(1, NX)])
 
-    own = gather_y(part)
+    own = gather_y(after(part, *quarters[1:]))
     other = swap_core(own)
     quarters = after(quarters, part)
     (fan,) = call(kernel_fan, 10**6, 8, [(NX * NZ, 8, 2 * B)], [], *quarters)

time: 137 us -> 119 us (0.87)
  waiting for transfers between devices: 34.6 us -> 18.1 us
    ppermute x6, waiting for transfers between devices: 16.5 us -> 7.82 us  [by_y(): return lax.ppermute(v, 'cols', [(i, (i + d) % NY) for i in range(NY)])]
    ppermute x12, waiting for transfers between devices: 15.3 us -> 10.3 us  [move(): return lax.ppermute(v, 'rows', pairs)]
    ppermute x12, starting transfers between devices: 25.1 us -> 20.8 us  [move(): return lax.ppermute(v, 'rows', pairs)]
    all_to_all x1, waiting for transfers between devices: 2.83 us -> 0.01 us  [shards(): t_own = lax.all_to_all(fan, 'rows', 0, 0, axis_index_groups=GROUPS)]
    all_to_all x1, starting transfers between devices: 6.26 us -> 8.68 us  [shards(): t_own = lax.all_to_all(fan, 'rows', 0, 0, axis_index_groups=GROUPS)]
  transfers between devices with their start and end apart: 21 -> 21, of which waited for: 12 -> 11; matrix products, arithmetic and copies ran while one was open for 2% -> 2% of each run, Pallas kernels for 22% -> 26%
where the time goes in v8:
time: 119 us; the launch traced here: 118 us
  starting transfers between devices  50.7 us (43%)
  Pallas kernels  42.8 us (36%)
  waiting for transfers between devices  18.1 us (15%)
  local copies, waits for them, and re-layouts  5.19 us (4%)
    pallas_call x3, Pallas kernels, call(): pl.pallas_call(kernel, out_shape=[jax.ShapeDtypeStruct(s, F32) for s in o...  30.2 us
    ppermute x12, starting transfers between devices, move(): return lax.ppermute(v, 'rows', pairs)  20.8 us
    pallas_call x1, Pallas kernels, last(): pl.pallas_call(kernel_c, out_shape=[jax.ShapeDtypeStruct((B, B), F32), ja...  11.9 us
    ppermute x12, waiting for transfers between devices, move(): return lax.ppermute(v, 'rows', pairs)  10.3 us
    all_to_all x1, starting transfers between devices, shards(): t_own = lax.all_to_all(fan, 'rows', 0, 0, axis_index_groups=GROUPS)  8.68 us
    all_to_all x1, starting transfers between devices, shards(): chosen = pick(window_rows, lax.all_to_all(mine, 'rows', 0, 0))  8.5 us
    ppermute x6, waiting for transfers between devices, by_y(): return lax.ppermute(v, 'cols', [(i, (i + d) % NY) for i in range(NY)])  7.82 us
    ppermute x6, starting transfers between devices, by_y(): return lax.ppermute(v, 'cols', [(i, (i + d) % NY) for i in range(NY)])  7.55 us
  transfers between devices with their start and end apart: 21, of which 11 were waited for; matrix products, arithmetic and copies ran while one was open for 2% of the time, Pallas kernels for 26%

profile of v8, /device:TPU:1, one launch (start us, length us, event | category | flops | bytes accessed | tf_op | source)
XLA Modules:
  0.0 118.2 jit_solution(1589590851524439482)
XLA Ops:
  0.6 1.1 constant_dynamic-slice_fusion
  1.7 5.2 %collective-permute-start = (f32[4,16,512]{2,1,0:T(8,128)S(1)}, f32[4,16,512]{2,1,0:T(8,128)S(1)}, u32[]{:S(2)}, u32[]{:S(2)}) collective-permute-start(f32[4,16,512]{2,1,0:T(8,128)S(1)} %slice.55), channel_id=1, source_target_pairs={{4,0},{5,1},{6,2},{7,3}} | collective-permute-start | bytes 393224 | tf_op jit(solution)/shard_map/ppermute | solution.py:382
  6.9 1.9 %dynamic-slice_bitcast_fusion = f32[64,8,256]{2,1,0:T(8,128)} fusion(f32[512,1024]{1,0:T(8,128)} %panel_hbm.1, s32[]{:T(128)S(6)} %select_n.74), kind=kLoop, calls=%fused_computation.1 | loop fusion | bytes 1048580 | tf_op jit(solution)/shard_map/reshape | solution.py:389
  8.8 8.5 %all-to-all-start = ((f32[64,8,256]{2,1,0:T(8,128)}), f32[64,8,256]{2,1,0:T(8,128)S(1)}, u32[]{:S(2)}, u32[]{:S(2)}) async-start(f32[64,8,256]{2,1,0:T(8,128)} %dynamic-slice_bitcast_fusion), calls=%async_computation | async-start | bytes 1048576 | tf_op jit(solution)/shard_map/all_to_all | solution.py:390
  17.4 4.9 %collective-permute-start.2 = (f32[80,256]{1,0:T(8,128)S(1)}, f32[80,256]{1,0:T(8,128)S(1)}, u32[]{:S(2)}, u32[]{:S(2)}) collective-permute-start(f32[80,256]{1,0:T(8,128)S(1)} %get-tuple-element.40), channel_id=1, source_target_pairs={{0,128},{4,132},{1,129},{5,133},{2,130},{6,134},{3,131},{7,135}} | collective-permute-start | bytes 245768 | tf_op jit(solution)/shard_map/ppermute | solution.py:330
  22.3 1.3 %collective-permute-start.3 = (f32[80,256]{1,0:T(8,128)S(1)}, f32[80,256]{1,0:T(8,128)S(1)}, u32[]{:S(2)}, u32[]{:S(2)}) collective-permute-start(f32[80,256]{1,0:T(8,128)S(1)} %get-tuple-element.41), channel_id=1, source_target_pairs={{0,192},{4,196},{1,193},{5,197},{2,194},{6,198},{3,195},{7,199}} | collective-permute-start | bytes 245768 | tf_op jit(solution)/shard_map/ppermute | solution.py:330
  23.6 1.3 %collective-permute-start.1 = (f32[80,256]{1,0:T(8,128)S(1)}, f32[80,256]{1,0:T(8,128)S(1)}, u32[]{:S(2)}, u32[]{:S(2)}) collective-permute-start(f32[80,256]{1,0:T(8,128)S(1)} %get-tuple-element.42), channel_id=1, source_target_pairs={{0,64},{4,68},{1,65},{5,69},{2,66},{6,70},{3,67},{7,71}} | collective-permute-start | bytes 245768 | tf_op jit(solution)/shard_map/ppermute | solution.py:330
  25.7 3.2 %collective-permute-done.1 = f32[80,256]{1,0:T(8,128)S(1)} collective-permute-done((f32[80,256]{1,0:T(8,128)S(1)}, f32[80,256]{1,0:T(8,128)S(1)}, u32[]{:S(2)}, u32[]{:S(2)}) %collective-permute-start.1) | collective-permute-done | bytes 81952 | tf_op jit(solution)/shard_map/ppermute | solution.py:330
  28.9 1.3 %collective-permute-start.6 = (f32[80,256]{1,0:T(8,128)S(1)}, f32[80,256]{1,0:T(8,128)S(1)}, u32[]{:S(2)}, u32[]{:S(2)}) collective-permute-start(f32[80,256]{1,0:T(8,128)S(1)} %fusion.1), channel_id=1, source_target_pairs={{0,48},{4,52},{64,112},{68,116},{128,176},{132,180},{192,240},{196... | collective-permute-start | bytes 245768 | tf_op jit(solution)/shard_map/ppermute | solution.py:330
  30.2 1.3 %collective-permute-start.5 = (f32[80,256]{1,0:T(8,128)S(1)}, f32[80,256]{1,0:T(8,128)S(1)}, u32[]{:S(2)}, u32[]{:S(2)}) collective-permute-start(f32[80,256]{1,0:T(8,128)S(1)} %fusion.1), channel_id=1, source_target_pairs={{0,32},{4,36},{64,96},{68,100},{128,160},{132,164},{192,224},{196,... | collective-permute-start | bytes 245768 | tf_op jit(solution)/shard_map/ppermute | solution.py:330
  31.5 1.3 %collective-permute-start.4 = (f32[80,256]{1,0:T(8,128)S(1)}, f32[80,256]{1,0:T(8,128)S(1)}, u32[]{:S(2)}, u32[]{:S(2)}) collective-permute-start(f32[80,256]{1,0:T(8,128)S(1)} %fusion.1), channel_id=1, source_target_pairs={{0,16},{4,20},{64,80},{68,84},{128,144},{132,148},{192,208},{196,2... | collective-permute-start | bytes 245768 | tf_op jit(solution)/shard_map/ppermute | solution.py:330
  33.0 2.0 %collective-permute-done.4 = f32[80,256]{1,0:T(8,128)S(1)} collective-permute-done((f32[80,256]{1,0:T(8,128)S(1)}, f32[80,256]{1,0:T(8,128)S(1)}, u32[]{:S(2)}, u32[]{:S(2)}) %collective-permute-start.4) | collective-permute-done | bytes 81952 | tf_op jit(solution)/shard_map/ppermute | solution.py:330
  35.0 1.3 %collective-permute-start.7 = (f32[80,256]{1,0:T(8,128)S(1)}, f32[80,256]{1,0:T(8,128)S(1)}, u32[]{:S(2)}, u32[]{:S(2)}) collective-permute-start(f32[80,256]{1,0:T(8,128)S(1)} %add_add_fusion), channel_id=1, source_target_pairs={{0,8},{4,12},{16,24},{20,28},{32,40},{36,44},{48,56},{52,60},{64,7... | collective-permute-start | bytes 245768 | tf_op jit(solution)/shard_map/ppermute | solution.py:330
  36.3 1.5 %collective-permute-done.7 = f32[80,256]{1,0:T(8,128)S(1)} collective-permute-done((f32[80,256]{1,0:T(8,128)S(1)}, f32[80,256]{1,0:T(8,128)S(1)}, u32[]{:S(2)}, u32[]{:S(2)}) %collective-permute-start.7) | collective-permute-done | bytes 81952 | tf_op jit(solution)/shard_map/ppermute | solution.py:330
  38.4 0.8 collective-permute-start.10
  39.3 3.7 %collective-permute-start.9 = (f32[80,256]{1,0:T(8,128)S(1)}, f32[80,256]{1,0:T(8,128)S(1)}, u32[]{:S(2)}, u32[]{:S(2)}) collective-permute-start(f32[80,256]{1,0:T(8,128)S(1)} %add.55), channel_id=1, source_target_pairs={{0,128},{4,132},{8,136},{12,140},{16,144},{20,148},{24,152},{28,15... | collective-permute-start | bytes 245768 | tf_op jit(solution)/shard_map/ppermute | solution.py:330
  43.0 1.3 %collective-permute-start.11 = (f32[8,256]{1,0:T(8,128)S(1)}, f32[8,256]{1,0:T(8,128)S(1)}, u32[]{:S(2)}, u32[]{:S(2)}) collective-permute-start(f32[8,256]{1,0:T(8,128)S(1)} %get-tuple-element.21), channel_id=1, source_target_pairs={{0,1},{1,2},{2,3},{3,0},{4,5},{5,6},{6,7},{7,4},{8,9},{9,10},{10,1... | collective-permute-start | bytes 24584 | tf_op jit(solution)/shard_map/ppermute | solution.py:362
  44.3 2.6 %collective-permute-start.12 = (f32[8,256]{1,0:T(8,128)S(1)}, f32[8,256]{1,0:T(8,128)S(1)}, u32[]{:S(2)}, u32[]{:S(2)}) collective-permute-start(f32[8,256]{1,0:T(8,128)S(1)} %get-tuple-element.22), channel_id=1, source_target_pairs={{0,2},{1,3},{2,0},{3,1},{4,6},{5,7},{6,4},{7,5},{8,10},{9,11},{10,... | collective-permute-start | bytes 24584 | tf_op jit(solution)/shard_map/ppermute | solution.py:362
  46.9 1.1 collective-permute-start.13
  48.3 1.4 %collective-permute-done.13.q3_ref = f32[8,256]{1,0:T(8,128)S(1)} collective-permute-done((f32[8,256]{1,0:T(8,128)S(1)}, f32[8,256]{1,0:T(8,128)S(1)}, u32[]{:S(2)}, u32[]{:S(2)}) %collective-permute-start.13) | collective-permute-done | bytes 8224 | tf_op jit(solution)/shard_map/ppermute | solution.py:362
  49.7 2.0 %collective-permute-start.16 = (f32[4,80,256]{2,1,0:T(8,128)S(1)}, f32[4,80,256]{2,1,0:T(8,128)S(1)}, u32[]{:S(2)}, u32[]{:S(2)}) collective-permute-start(f32[4,80,256]{2,1,0:T(8,128)S(1)} %pad_maximum_fusion.1), channel_id=1, source_target_pairs={{0,3},{1,0},{2,1},{3,2},{4,7},{5,4},{6,5},{7,6},{8,11},{9,8},{10,9... | collective-permute-start | bytes 983048 | tf_op jit(solution)/shard_map/ppermute | solution.py:362
  52.3 1.0 shard_map.62
  53.3 8.7 %all-to-all-start.1 = ((f32[32,8,1024]{2,1,0:T(8,128)}), f32[32,8,1024]{2,1,0:T(8,128)S(1)}, u32[]{:S(2)}, u32[]{:S(2)}) async-start(f32[32,8,1024]{2,1,0:T(8,128)} %shard_map.62), calls=%async_computation.1 | async-start | bytes 2097152 | tf_op jit(solution)/shard_map/all_to_all | solution.py:399
  62.0 6.3 %collective-permute-done.14 = f32[4,80,256]{2,1,0:T(8,128)S(1)} collective-permute-done((f32[4,80,256]{2,1,0:T(8,128)S(1)}, f32[4,80,256]{2,1,0:T(8,128)S(1)}, u32[]{:S(2)}, u32[]{:S(2)}) %collective-permute-start.14) | collective-permute-done | bytes 327712 | tf_op jit(solution)/shard_map/ppermute | solution.py:362
  68.4 1.9 %collective-permute-start.17 = (f32[4,4,80,256]{3,2,1,0:T(8,128)S(1)}, f32[4,4,80,256]{3,2,1,0:T(8,128)S(1)}, u32[]{:S(2)}, u32[]{:S(2)}) collective-permute-start(f32[4,4,80,256]{3,2,1,0:T(8,128)S(1)} %pad_maximum_fusion.own_ref), channel_id=1, source_target_pairs={{0,4},{4,0},{8,12},{12,8},{16,20},{20,16},{24,28},{28,24},{32,36},... | collective-permute-start | bytes 3932168 | tf_op jit(solution)/shard_map/ppermute | solution.py:330
  70.3 2.7 %collective-permute-done.17.other_ref = f32[4,4,80,256]{3,2,1,0:T(8,128)S(1)} collective-permute-done((f32[4,4,80,256]{3,2,1,0:T(8,128)S(1)}, f32[4,4,80,256]{3,2,1,0:T(8,128)S(1)}, u32[]{:S(2)}, u32[]{:S(2)}) %collective-permute-start.17) | collective-permute-done | bytes 1310752 | tf_op jit(solution)/shard_map/ppermute | solution.py:330
  72.9 15.1 %shard_map.60 = (f32[1024,512]{1,0:T(8,128)S(1)}, f32[4,128,128]{2,1,0:T(8,128)S(1)}, f32[512,512]{1,0:T(8,128)S(1)}) custom-call(f32[4,4,80,256]{3,2,1,0:T(8,128)S(1)} %pad_maximum_fusion.own_ref, f32[4,4,80,256]{3,2,1,0:T(8,128)S(1)} %collective-permute-done.17.other_ref), custom_call_target="tpu_custom_call" | custom-call | flops 3500000000 | bytes 8388608 | tf_op jit(solution)/shard_map/pallas_call | solution.py:278
  88.1 1.0 copy-done.4
  89.1 1.7 %collective-permute-start.18 = (f32[32,8,1024]{2,1,0:T(8,128)S(1)}, f32[32,8,1024]{2,1,0:T(8,128)S(1)}, u32[]{:S(2)}, u32[]{:S(2)}) collective-permute-start(f32[32,8,1024]{2,1,0:T(8,128)S(1)} %all-to-all-done.1.own_hbm), channel_id=1, source_target_pairs={{0,4},{4,0},{8,12},{12,8},{16,20},{20,16},{24,28},{28,24},{32,36},... | collective-permute-start | bytes 3145736 | tf_op jit(solution)/shard_map/ppermute | solution.py:330
  90.7 1.2 %copy-done.5 = f32[512,512]{1,0:T(8,128)S(1)} copy-done((f32[512,512]{1,0:T(8,128)S(1)}, f32[512,512]{1,0:T(8,128)}, u32[]{:S(2)}) %copy-start.5) | copy-done | bytes 1048600
  92.0 14.0 %shard_map.61 = (f32[512,512]{1,0:T(8,128)S(1)}, f32[4,128,128]{2,1,0:T(8,128)S(1)}) custom-call(f32[512,512]{1,0:T(8,128)S(1)} %copy-done.5, f32[1024,512]{1,0:T(8,128)S(1)} %get-tuple-element.26.f0_ref), custom_call_target="tpu_custom_call" | custom-call | flops 3500000000 | bytes 8388608 | tf_op jit(solution)/shard_map/pallas_call | solution.py:278
  106.1 11.9 %shard_map.63 = (f32[512,512]{1,0:T(8,128)}, f32[512,1024]{1,0:T(8,128)}) custom-call(s32[64]{0:T(128)S(1)} %copy-done.3, s32[4]{0:T(128)S(1)} %copy-done.2, f32[1024,512]{1,0:T(8,128)S(1)} %get-tuple-element.26.f0_ref, f32[512,512]{1,0:T(8,128)S(1)} %get-tuple-element.28.f1_ref, f32[4,128,128]{2,1,0:T(8,128)S(1)} %get-tuple-element.29.d0_ref, ...), custom_call_target="tpu_custom_call" | custom-call | tf_op jit(solution)/shard_map/pallas_call | solution.py:291
  (41 shorter events, 2.7 us)
Async XLA Ops:
  1.7 15.6 %collective-permute-start = (f32[4,16,512]{2,1,0:T(8,128)S(1)}, f32[4,16,512]{2,1,0:T(8,128)S(1)}, u32[]{:S(2)}, u32[]{:S(2)}) collective-permute-start(f32[4,16,512]{2,1,0:T(8,128)S(1)} %slice.55), channel_id=1, source_target_pairs={{4,0},{5,1},{6,2},{7,3}} | collective-permute-start | bytes 393224 | tf_op jit(solution)/shard_map/ppermute | solution.py:382
  8.8 29.0 %all-to-all-start = ((f32[64,8,256]{2,1,0:T(8,128)}), f32[64,8,256]{2,1,0:T(8,128)S(1)}, u32[]{:S(2)}, u32[]{:S(2)}) async-start(f32[64,8,256]{2,1,0:T(8,128)} %dynamic-slice_bitcast_fusion), calls=%async_computation | async-start | bytes 1048576 | tf_op jit(solution)/shard_map/all_to_all | solution.py:390
  17.3 20.5 %copy-start.2 = (s32[4]{0:T(128)S(1)}, s32[4]{0:T(128)}, u32[]{:S(2)}) copy-start(s32[4]{0:T(128)} %rows_ref.3) | copy-start | bytes 52
  17.4 8.1 %collective-permute-start.2 = (f32[80,256]{1,0:T(8,128)S(1)}, f32[80,256]{1,0:T(8,128)S(1)}, u32[]{:S(2)}, u32[]{:S(2)}) collective-permute-start(f32[80,256]{1,0:T(8,128)S(1)} %get-tuple-element.40), channel_id=1, source_target_pairs={{0,128},{4,132},{1,129},{5,133},{2,130},{6,134},{3,131},{7,135}} | collective-permute-start | bytes 245768 | tf_op jit(solution)/shard_map/ppermute | solution.py:330
  22.3 3.4 %collective-permute-start.3 = (f32[80,256]{1,0:T(8,128)S(1)}, f32[80,256]{1,0:T(8,128)S(1)}, u32[]{:S(2)}, u32[]{:S(2)}) collective-permute-start(f32[80,256]{1,0:T(8,128)S(1)} %get-tuple-element.41), channel_id=1, source_target_pairs={{0,192},{4,196},{1,193},{5,197},{2,194},{6,198},{3,195},{7,199}} | collective-permute-start | bytes 245768 | tf_op jit(solution)/shard_map/ppermute | solution.py:330
  23.6 5.3 %collective-permute-start.1 = (f32[80,256]{1,0:T(8,128)S(1)}, f32[80,256]{1,0:T(8,128)S(1)}, u32[]{:S(2)}, u32[]{:S(2)}) collective-permute-start(f32[80,256]{1,0:T(8,128)S(1)} %get-tuple-element.42), channel_id=1, source_target_pairs={{0,64},{4,68},{1,65},{5,69},{2,66},{6,70},{3,67},{7,71}} | collective-permute-start | bytes 245768 | tf_op jit(solution)/shard_map/ppermute | solution.py:330
  28.9 3.9 %collective-permute-start.6 = (f32[80,256]{1,0:T(8,128)S(1)}, f32[80,256]{1,0:T(8,128)S(1)}, u32[]{:S(2)}, u32[]{:S(2)}) collective-permute-start(f32[80,256]{1,0:T(8,128)S(1)} %fusion.1), channel_id=1, source_target_pairs={{0,48},{4,52},{64,112},{68,116},{128,176},{132,180},{192,240},{196... | collective-permute-start | bytes 245768 | tf_op jit(solution)/shard_map/ppermute | solution.py:330
  30.2 2.8 %collective-permute-start.5 = (f32[80,256]{1,0:T(8,128)S(1)}, f32[80,256]{1,0:T(8,128)S(1)}, u32[]{:S(2)}, u32[]{:S(2)}) collective-permute-start(f32[80,256]{1,0:T(8,128)S(1)} %fusion.1), channel_id=1, source_target_pairs={{0,32},{4,36},{64,96},{68,100},{128,160},{132,164},{192,224},{196,... | collective-permute-start | bytes 245768 | tf_op jit(solution)/shard_map/ppermute | solution.py:330
  31.5 3.4 %collective-permute-start.4 = (f32[80,256]{1,0:T(8,128)S(1)}, f32[80,256]{1,0:T(8,128)S(1)}, u32[]{:S(2)}, u32[]{:S(2)}) collective-permute-start(f32[80,256]{1,0:T(8,128)S(1)} %fusion.1), channel_id=1, source_target_pairs={{0,16},{4,20},{64,80},{68,84},{128,144},{132,148},{192,208},{196,2... | collective-permute-start | bytes 245768 | tf_op jit(solution)/shard_map/ppermute | solution.py:330
  35.0 2.8 %collective-permute-start.7 = (f32[80,256]{1,0:T(8,128)S(1)}, f32[80,256]{1,0:T(8,128)S(1)}, u32[]{:S(2)}, u32[]{:S(2)}) collective-permute-start(f32[80,256]{1,0:T(8,128)S(1)} %add_add_fusion), channel_id=1, source_target_pairs={{0,8},{4,12},{16,24},{20,28},{32,40},{36,44},{48,56},{52,60},{64,7... | collective-permute-start | bytes 245768 | tf_op jit(solution)/shard_map/ppermute | solution.py:330
  38.4 8.5 %collective-permute-start.10 = (f32[80,256]{1,0:T(8,128)S(1)}, f32[80,256]{1,0:T(8,128)S(1)}, u32[]{:S(2)}, u32[]{:S(2)}) collective-permute-start(f32[80,256]{1,0:T(8,128)S(1)} %add.55), channel_id=1, source_target_pairs={{0,192},{4,196},{8,200},{12,204},{16,208},{20,212},{24,216},{28,22... | collective-permute-start | bytes 245768 | tf_op jit(solution)/shard_map/ppermute | solution.py:330
  39.3 8.7 %collective-permute-start.9 = (f32[80,256]{1,0:T(8,128)S(1)}, f32[80,256]{1,0:T(8,128)S(1)}, u32[]{:S(2)}, u32[]{:S(2)}) collective-permute-start(f32[80,256]{1,0:T(8,128)S(1)} %add.55), channel_id=1, source_target_pairs={{0,128},{4,132},{8,136},{12,140},{16,144},{20,148},{24,152},{28,15... | collective-permute-start | bytes 245768 | tf_op jit(solution)/shard_map/ppermute | solution.py:330
  43.0 5.1 %collective-permute-start.8 = (f32[80,256]{1,0:T(8,128)S(1)}, f32[80,256]{1,0:T(8,128)S(1)}, u32[]{:S(2)}, u32[]{:S(2)}) collective-permute-start(f32[80,256]{1,0:T(8,128)S(1)} %add.55), channel_id=1, source_target_pairs={{0,64},{4,68},{8,72},{12,76},{16,80},{20,84},{24,88},{28,92},{32,9... | collective-permute-start | bytes 245768 | tf_op jit(solution)/shard_map/ppermute | solution.py:330
  43.0 5.2 %collective-permute-start.11 = (f32[8,256]{1,0:T(8,128)S(1)}, f32[8,256]{1,0:T(8,128)S(1)}, u32[]{:S(2)}, u32[]{:S(2)}) collective-permute-start(f32[8,256]{1,0:T(8,128)S(1)} %get-tuple-element.21), channel_id=1, source_target_pairs={{0,1},{1,2},{2,3},{3,0},{4,5},{5,6},{6,7},{7,4},{8,9},{9,10},{10,1... | collective-permute-start | bytes 24584 | tf_op jit(solution)/shard_map/ppermute | solution.py:362
  44.3 4.0 %collective-permute-start.12 = (f32[8,256]{1,0:T(8,128)S(1)}, f32[8,256]{1,0:T(8,128)S(1)}, u32[]{:S(2)}, u32[]{:S(2)}) collective-permute-start(f32[8,256]{1,0:T(8,128)S(1)} %get-tuple-element.22), channel_id=1, source_target_pairs={{0,2},{1,3},{2,0},{3,1},{4,6},{5,7},{6,4},{7,5},{8,10},{9,11},{10,... | collective-permute-start | bytes 24584 | tf_op jit(solution)/shard_map/ppermute | solution.py:362
  46.9 2.8 %collective-permute-start.13 = (f32[8,256]{1,0:T(8,128)S(1)}, f32[8,256]{1,0:T(8,128)S(1)}, u32[]{:S(2)}, u32[]{:S(2)}) collective-permute-start(f32[8,256]{1,0:T(8,128)S(1)} %get-tuple-element.23), channel_id=1, source_target_pairs={{0,3},{1,0},{2,1},{3,2},{4,7},{5,4},{6,5},{7,6},{8,11},{9,8},{10,9... | collective-permute-start | bytes 24584 | tf_op jit(solution)/shard_map/ppermute | solution.py:362
  49.7 12.3 %collective-permute-start.16 = (f32[4,80,256]{2,1,0:T(8,128)S(1)}, f32[4,80,256]{2,1,0:T(8,128)S(1)}, u32[]{:S(2)}, u32[]{:S(2)}) collective-permute-start(f32[4,80,256]{2,1,0:T(8,128)S(1)} %pad_maximum_fusion.1), channel_id=1, source_target_pairs={{0,3},{1,0},{2,1},{3,2},{4,7},{5,4},{6,5},{7,6},{8,11},{9,8},{10,9... | collective-permute-start | bytes 983048 | tf_op jit(solution)/shard_map/ppermute | solution.py:362
  51.7 10.3 %collective-permute-start.15 = (f32[4,80,256]{2,1,0:T(8,128)S(1)}, f32[4,80,256]{2,1,0:T(8,128)S(1)}, u32[]{:S(2)}, u32[]{:S(2)}) collective-permute-start(f32[4,80,256]{2,1,0:T(8,128)S(1)} %pad_maximum_fusion.1), channel_id=1, source_target_pairs={{0,2},{1,3},{2,0},{3,1},{4,6},{5,7},{6,4},{7,5},{8,10},{9,11},{10,... | collective-permute-start | bytes 983048 | tf_op jit(solution)/shard_map/ppermute | solution.py:362
  51.7 16.6 %collective-permute-start.14 = (f32[4,80,256]{2,1,0:T(8,128)S(1)}, f32[4,80,256]{2,1,0:T(8,128)S(1)}, u32[]{:S(2)}, u32[]{:S(2)}) collective-permute-start(f32[4,80,256]{2,1,0:T(8,128)S(1)} %pad_maximum_fusion.1), channel_id=1, source_target_pairs={{0,1},{1,2},{2,3},{3,0},{4,5},{5,6},{6,7},{7,4},{8,9},{9,10},{10,1... | collective-permute-start | bytes 983048 | tf_op jit(solution)/shard_map/ppermute | solution.py:362
  53.3 35.7 %all-to-all-start.1 = ((f32[32,8,1024]{2,1,0:T(8,128)}), f32[32,8,1024]{2,1,0:T(8,128)S(1)}, u32[]{:S(2)}, u32[]{:S(2)}) async-start(f32[32,8,1024]{2,1,0:T(8,128)} %shard_map.62), calls=%async_computation.1 | async-start | bytes 2097152 | tf_op jit(solution)/shard_map/all_to_all | solution.py:399
  68.4 4.5 %collective-permute-start.17 = (f32[4,4,80,256]{3,2,1,0:T(8,128)S(1)}, f32[4,4,80,256]{3,2,1,0:T(8,128)S(1)}, u32[]{:S(2)}, u32[]{:S(2)}) collective-permute-start(f32[4,4,80,256]{3,2,1,0:T(8,128)S(1)} %pad_maximum_fusion.own_ref), channel_id=1, source_target_pairs={{0,4},{4,0},{8,12},{12,8},{16,20},{20,16},{24,28},{28,24},{32,36},... | collective-permute-start | bytes 3932168 | tf_op jit(solution)/shard_map/ppermute | solution.py:330
  88.1 1.0 copy-start.4
  89.1 17.0 %collective-permute-start.18 = (f32[32,8,1024]{2,1,0:T(8,128)S(1)}, f32[32,8,1024]{2,1,0:T(8,128)S(1)}, u32[]{:S(2)}, u32[]{:S(2)}) collective-permute-start(f32[32,8,1024]{2,1,0:T(8,128)S(1)} %all-to-all-done.1.own_hbm), channel_id=1, source_target_pairs={{0,4},{4,0},{8,12},{12,8},{16,20},{20,16},{24,28},{28,24},{32,36},... | collective-permute-start | bytes 3145736 | tf_op jit(solution)/shard_map/ppermute | solution.py:330
  90.7 1.2 %copy-start.5 = (f32[512,512]{1,0:T(8,128)S(1)}, f32[512,512]{1,0:T(8,128)}, u32[]{:S(2)}) copy-start(f32[512,512]{1,0:T(8,128)} %copy-done.4) | copy-start | bytes 3145732
  92.0 14.1 %copy-start = (f32[512,1024]{1,0:T(8,128)S(1)}, f32[512,1024]{1,0:T(8,128)}, u32[]{:S(2)}) copy-start(f32[512,1024]{1,0:T(8,128)} %panel_hbm.1) | copy-start | bytes 6291460
  92.0 14.1 %copy-start.1 = (f32[512,512]{1,0:T(8,128)S(1)}, f32[512,512]{1,0:T(8,128)}, u32[]{:S(2)}) copy-start(f32[512,512]{1,0:T(8,128)} %window_hbm.1) | copy-start | bytes 3145732
  92.0 14.1 %copy-start.3 = (s32[64]{0:T(128)S(1)}, s32[64]{0:T(128)}, u32[]{:S(2)}) copy-start(s32[64]{0:T(128)} %live_ref.1) | copy-start | bytes 772
